TPU v7x, 256 devices: a whole 4x4x8 slice. The times are simulated.
256 devices in a mesh: req: 32 (over z, y), head: 8 (over x, core).
Axes of the slice: x: 4, y: 4, z: 8, core: 2. Of those that a mesh axis runs over, the one named last changes fastest.
Arguments:
- hidden: bfloat16 [512, 2048], P('req'), may hold values from -6 to 6
- deal_order: int32 [512], replicated, may hold values from 0 to 511, each once
- lengths: int32 [512], replicated, may hold values from 1 to 8192, as said below
- page_table: int32 [512, 64], replicated, may hold values from 0 to 2047, as said below
- key_cache: bfloat16 [2048, 128, 8, 128], P('req', None, 'head'), as said below
- value_cache: bfloat16 [2048, 128, 8, 128], P('req', None, 'head'), may hold values from -12 to 12
- attn_gain: float32 [2048], replicated, may hold values from 0.1 to 1.9
- w_query: bfloat16 [2048, 2048], P(None, 'head'), may hold values from -0.125 to 0.125
- w_key: bfloat16 [2048, 1024], P(None, 'head'), may hold values from -0.125 to 0.125
- w_value: bfloat16 [2048, 1024], P(None, 'head'), may hold values from -0.125 to 0.125
- w_gate: bfloat16 [2048, 2048], P(None, 'head'), may hold values from -0.125 to 0.125
- w_out: bfloat16 [2048, 2048], P('head'), may hold values from -1.5 to 1.5
- query_gain: float32 [128], replicated, may hold values from 0.5 to 2
- key_gain: float32 [128], replicated, may hold values from 0.5 to 2
- mlp_gain: float32 [2048], replicated, may hold values from 0.1 to 1.9
- mlp_gate: bfloat16 [2048, 3072], P(None, 'head'), may hold values from -0.125 to 0.125
- mlp_up: bfloat16 [2048, 3072], P(None, 'head'), may hold values from -0.125 to 0.125
- mlp_down: bfloat16 [3072, 2048], P('head'), may hold values from -0.109375 to 0.109375
Outputs:
- output: bfloat16 [512, 2048], P('req')
Inputs may be any that keep to these rules, and one draw needn't show every extreme that they name: `lengths`: one request holds exactly 8192 cached tokens, and all requests together fill at most 2048 pages of 128 tokens. `page_table`: for request r the first ceil(lengths[r] / 128) entries of row r name, in order, the pages that hold its cached tokens; no page is named by two such entries; the other entries are arbitrary page numbers. `key_cache`: cached keys; entries lie within -402 and 402.
All inputs are finite; a program needn't handle non-finite values.
Results may differ from a plain program's by a relative error of at most 0.022.
Values may be sent and summed in bfloat16 or wider, within the bound.
A program may use at most 64 MiB of HBM per device.

v0:
```python
import math

import jax
import jax.numpy as jnp
from jax import lax
from jax.sharding import PartitionSpec as P

EPSILON = 1e-06
ROPE_BASE = 1000000.0
LOW_SCORE = -1e30
LOG_TWO = math.log(2.0)


def rms_inv(values):
    return lax.rsqrt(jnp.mean(values * values, axis=-1, keepdims=True) + EPSILON)


def rotate(values, position):
    half_dim = values.shape[-1] // 2
    exponent = jnp.arange(half_dim, dtype=jnp.float32) * (2.0 / values.shape[-1])
    frequency = ROPE_BASE ** (-exponent)
    angles = position[:, None] * frequency[None, :]
    ones_tail = (1,) * (values.ndim - 2)
    angles = angles.reshape((angles.shape[0],) + ones_tail + (half_dim,))
    cosine = jnp.cos(angles)
    sine_vals = jnp.sin(angles)
    front_half = values[..., :half_dim]
    back_half = values[..., half_dim:]
    return jnp.concatenate(
        [front_half * cosine - back_half * sine_vals, back_half * cosine + front_half * sine_vals],
        axis=-1,
    )


def norm_rotate(values, gain_vec, position):
    return rotate(values * rms_inv(values) * gain_vec, position)


def pick_rows(wanted, shard_rows):
    targets = jnp.arange(shard_rows.shape[0], dtype=jnp.int32)
    selector = (wanted[:, None] == targets[None, :]).astype(jnp.bfloat16)
    return jnp.dot(selector, shard_rows, preferred_element_type=jnp.float32)


def body(
    hidden,
    deal_order,
    lengths,
    page_table,
    key_cache,
    value_cache,
    attn_gain,
    w_query,
    w_key,
    w_value,
    w_gate,
    w_out,
    query_gain,
    key_gain,
    mlp_gain,
    mlp_gate,
    mlp_up,
    mlp_down,
):
    local_rows, model_width = hidden.shape
    req_devices = lax.axis_size("req")
    req_index = lax.axis_index("req")
    all_rows = local_rows * req_devices
    head_width = query_gain.shape[0]
    pool_pages = key_cache.shape[0]
    page_size = key_cache.shape[1]
    local_kv = key_cache.shape[2]
    group_size = w_query.shape[1] // (local_kv * head_width)
    scale_factor = 1.0 / math.sqrt(head_width)
    first_own = req_index * local_rows
    hidden_f = hidden.astype(jnp.float32)
    normed = (hidden_f * rms_inv(hidden_f) * attn_gain).astype(jnp.bfloat16)
    own_requests = lax.dynamic_slice_in_dim(deal_order, first_own, local_rows)
    position = lengths[own_requests].astype(jnp.float32)
    queries = jnp.dot(normed, w_query, preferred_element_type=jnp.float32).reshape(
        local_rows, local_kv, group_size, head_width
    )
    queries = norm_rotate(queries, query_gain, position).astype(jnp.bfloat16)
    new_keys = jnp.dot(normed, w_key, preferred_element_type=jnp.float32).reshape(
        local_rows, local_kv, head_width
    )
    new_keys = norm_rotate(new_keys, key_gain, position).astype(jnp.bfloat16)
    new_values = (
        jnp.dot(normed, w_value, preferred_element_type=jnp.float32)
        .astype(jnp.bfloat16)
        .reshape(local_rows, local_kv, head_width)
    )
    gate_logits = jnp.dot(normed, w_gate, preferred_element_type=jnp.float32)
    all_queries = lax.all_gather(queries, "req", axis=0, tiled=True)
    dealt_lengths = lengths[deal_order]
    dealt_tables = page_table[deal_order]
    page_counts = (dealt_lengths + page_size - 1) // page_size
    slot_ids = jnp.arange(dealt_tables.shape[1], dtype=jnp.int32)
    local_ids = dealt_tables - req_index * pool_pages
    usable = (
        (slot_ids[None, :] < page_counts[:, None]) & (local_ids >= 0) & (local_ids < pool_pages)
    )
    targets = jnp.where(usable, local_ids, pool_pages).reshape(-1)
    request_ids = jnp.broadcast_to(
        jnp.arange(all_rows, dtype=jnp.int32)[:, None], dealt_tables.shape
    ).reshape(-1)
    slot_flat = jnp.broadcast_to(slot_ids[None, :], dealt_tables.shape).reshape(-1)
    owners = jnp.full((pool_pages,), all_rows, jnp.int32).at[targets].set(request_ids, mode="drop")
    owner_slots = jnp.zeros((pool_pages,), jnp.int32).at[targets].set(slot_flat, mode="drop")
    safe_owners = jnp.minimum(owners, all_rows - 1)
    filled = jnp.where(
        owners < all_rows,
        jnp.clip(dealt_lengths[safe_owners] - owner_slots * page_size, 0, page_size),
        0,
    )
    page_queries = all_queries[safe_owners]
    scores = (
        jnp.einsum("pkgd,ptkd->pkgt", page_queries, key_cache, preferred_element_type=jnp.float32)
        * scale_factor
    )
    live_mask = (
        jnp.arange(page_size, dtype=jnp.int32)[None, None, None, :] < filled[:, None, None, None]
    )
    scores = jnp.where(live_mask, scores, LOW_SCORE)
    page_peaks = jnp.max(scores, axis=-1)
    local_peaks = (
        jnp.full((all_rows, local_kv, group_size), LOW_SCORE, jnp.float32)
        .at[owners]
        .max(page_peaks, mode="drop")
    )
    self_scores = (
        jnp.einsum("rkgd,rkd->rkg", queries, new_keys, preferred_element_type=jnp.float32)
        * scale_factor
    )
    own_peaks = jnp.maximum(
        lax.dynamic_slice_in_dim(local_peaks, first_own, local_rows), self_scores
    )
    with_self = lax.dynamic_update_slice_in_dim(local_peaks, own_peaks, first_own, 0)
    global_peaks = lax.pmax(with_self, "req")
    global_shift = LOG_TWO * jnp.ceil(global_peaks / LOG_TWO)
    weights = jnp.where(live_mask, jnp.exp(scores - global_shift[safe_owners][..., None]), 0.0)
    totals = (
        jnp.zeros((all_rows, local_kv, group_size), jnp.float32)
        .at[owners]
        .add(jnp.sum(weights, axis=-1), mode="drop")
    )
    page_numerators = jnp.einsum(
        "pkgt,ptkd->pkgd",
        weights.astype(jnp.bfloat16),
        value_cache,
        preferred_element_type=jnp.float32,
    )
    numerators = (
        jnp.zeros((all_rows, local_kv, group_size, head_width), jnp.float32)
        .at[owners]
        .add(page_numerators, mode="drop")
    )
    totals, numerators = (totals, numerators)
    own_totals, own_numerators = (
        lax.psum_scatter(totals, "req", scatter_dimension=0, tiled=True),
        lax.psum_scatter(numerators, "req", scatter_dimension=0, tiled=True),
    )
    own_shift = lax.dynamic_slice_in_dim(global_shift, first_own, local_rows)
    self_weight = jnp.exp(self_scores - own_shift)
    own_totals = own_totals + self_weight
    self_rounded = lax.optimization_barrier(self_weight.astype(jnp.bfloat16)).astype(jnp.float32)
    own_numerators = (
        own_numerators + self_rounded[..., None] * new_values.astype(jnp.float32)[:, :, None, :]
    )
    heads_out = (own_numerators / own_totals[..., None]).reshape(
        local_rows, local_kv * group_size * head_width
    )
    attended = (heads_out * jax.nn.sigmoid(gate_logits)).astype(jnp.bfloat16)
    projected = jnp.dot(attended, w_out, preferred_element_type=jnp.float32)
    attn_total = lax.psum(projected.astype(jnp.bfloat16), "head").astype(jnp.float32)
    mixed_rows = (hidden_f + attn_total).astype(jnp.bfloat16)
    mixed_f = mixed_rows.astype(jnp.float32)
    normed_two = (mixed_f * rms_inv(mixed_f) * mlp_gain).astype(jnp.bfloat16)
    gate_part = jnp.dot(normed_two, mlp_gate, preferred_element_type=jnp.float32)
    up_part = jnp.dot(normed_two, mlp_up, preferred_element_type=jnp.float32)
    inner_act = (jax.nn.silu(gate_part) * up_part).astype(jnp.bfloat16)
    down_part = jnp.dot(inner_act, mlp_down, preferred_element_type=jnp.float32)
    inverse_order = (
        jnp.zeros((all_rows,), jnp.int32).at[deal_order].set(jnp.arange(all_rows, dtype=jnp.int32))
    )
    wanted = lax.dynamic_slice_in_dim(inverse_order, first_own, local_rows)
    mlp_total = lax.psum(down_part.astype(jnp.bfloat16), "head").astype(jnp.float32)
    result = (mixed_f + mlp_total).astype(jnp.bfloat16)
    gathered = pick_rows(wanted, lax.all_gather(result, "req", axis=0, tiled=True))
    output = gathered.astype(jnp.bfloat16)
    return output


def solution(mesh):
    return jax.shard_map(
        body,
        mesh=mesh,
        in_specs=(
            P("req", None),
            P(),
            P(),
            P(),
            P("req", None, "head", None),
            P("req", None, "head", None),
            P(),
            P(None, "head"),
            P(None, "head"),
            P(None, "head"),
            P(None, "head"),
            P("head", None),
            P(),
            P(),
            P(),
            P(None, "head"),
            P(None, "head"),
            P("head", None),
        ),
        out_specs=P("req", None),
        check_vma=False,
    )
```

profile of v0, /device:TPU:1, one launch (start us, length us, event | category | flops | bytes accessed | tf_op | source)
XLA Modules:
  0.0 1035.3 jit_solution(14262938876819041306)
XLA Ops:
  8.3 1.0 fusion.17
  9.3 3.6 gather_fusion
  14.7 41.1 %all_gather.6 = bf16[512,1,2,128]{3,2,1,0:T(2,128)(2,1)S(1)} all-gather(bf16[16,1,2,128]{3,2,1,0:T(2,128)(2,1)S(1)} %pad_maximum_fusion), channel_id=1, replica_groups=mesh['req'=32,'head'=8] {'req'}, dimensions={0}, use_global_device_ids=true | all-gather | bytes 270336 | tf_op jit(solution)/shard_map/all_gather | solution.py:94
  56.0 1.0 gather_fusion.1
  57.9 120.0 %scatter_custom_fusion.2 = s32[64]{0:T(128)S(1)} fusion(s32[32768]{0:T(1024)S(1)} %bitcast.102, s32[32768]{0:T(1024)S(1)} %reshape.511, s32[]{:T(128)} %constant.24.clone.1), kind=kCustom, calls=%fused_computation.126 | custom fusion | bytes 260 | tf_op jit(solution)/shard_map/scatter | solution.py:109
  177.9 120.0 %scatter_custom_fusion.1 = s32[64]{0:T(128)S(1)} fusion(s32[32768]{0:T(1024)S(1)} %bitcast.103, s32[32768]{0:T(1024)S(1)} %reshape.503, s32[]{:T(128)} %constant.25.clone.1), kind=kCustom, calls=%fused_computation.128 | custom fusion | bytes 260 | tf_op jit(solution)/shard_map/scatter | solution.py:108
  299.6 1.3 fusion.80
  300.8 0.9 scatter_custom_fusion.3
  303.0 58.4 %pmax.7 = f32[512,1,2]{0,2,1:T(2,128)S(1)} all-reduce(f32[512,1,2]{0,2,1:T(2,128)S(1)} %dynamic_update_slice.3), channel_id=1, replica_groups=mesh['req'=32,'head'=8] {'req'}, use_global_device_ids=true, to_apply=%region_8.9 | all-reduce | flops 1024 | bytes 8192 | tf_op jit(solution)/shard_map/pmax | solution.py:139
  362.4 1.5 scatter_custom_fusion.5
  364.0 2.3 fusion
  366.5 2.8 scatter_fusion
  370.5 223.8 %reduce-scatter.10.cloned.1.call-done = f32[16,2]{1,0:T(8,128)} async-done(((f32[512,2]{1,0:T(8,128)}), f32[16,2]{1,0:T(8,128)}) %reduce-scatter.10.cloned.1.call-update) | async-done | bytes 144
  595.3 214.8 %reduce-scatter.8.cloned.1.call-done = f32[16,256]{1,0:T(8,128)} async-done(((f32[512,256]{1,0:T(8,128)}), f32[16,256]{1,0:T(8,128)}) %reduce-scatter.8.cloned.1.call-update) | async-done | bytes 16400
  810.9 3.0 convolution_convert_fusion.2
  814.0 65.5 %all-reduce.3.cloned.1.call-done = bf16[16,2048]{1,0:T(8,128)(2,1)} async-done(((bf16[16,2048]{1,0:T(8,128)(2,1)}), bf16[16,2048]{1,0:T(8,128)(2,1)}) %all-reduce.3.cloned.1.call-update) | async-done | bytes 65552 | tf_op jit(solution)/shard_map/psum | solution.py:175
  879.5 1.0 fusion.21
  880.5 1.8 fusion.41
  882.2 3.3 convolution_convert_fusion.1
  885.6 62.9 %all-reduce.5.cloned.1.call-done = bf16[16,2048]{1,0:T(8,128)(2,1)} async-done(((bf16[16,2048]{1,0:T(8,128)(2,1)}), bf16[16,2048]{1,0:T(8,128)(2,1)}) %all-reduce.5.cloned.1.call-update) | async-done | bytes 65552 | tf_op jit(solution)/shard_map/psum | solution.py:187
  948.5 1.5 fusion.24
  950.1 2.4 scatter_custom_fusion
  952.6 73.5 %all-gather.2.cloned.1.call-done = bf16[512,2048]{1,0:T(8,128)(2,1)} async-done(((bf16[16,2048]{1,0:T(8,128)(2,1)}), bf16[512,2048]{1,0:T(8,128)(2,1)}) %all-gather.2.cloned.1.call-update) | async-done | bytes 2097168 | tf_op jit(solution)/shard_map/all_gather | solution.py:189
  1026.1 2.6 convolution_convert_fusion
  (94 shorter events, 11.6 us)
Async XLA Ops:
  6.5 293.0 %copy-start = (bf16[64,128,1,128]{3,1,2,0:T(8,128)(2,1)S(1)}, bf16[64,128,1,128]{3,1,2,0:T(8,128)(2,1)}, u32[]{:S(2)}) copy-start(bf16[64,128,1,128]{3,1,2,0:T(8,128)(2,1)} %param.22) | copy-start | bytes 6291460
  6.5 7.1 copy-start.2
  6.5 6.4 copy-start.1
  6.5 7.1 copy-start.6
  6.5 7.1 copy-start.3
  6.5 587.7 %reduce-scatter.10.cloned.1.call-start = ((), (), s32[]{:S(2)}) async-start(), calls=%async_computation.6 | async-start | bytes 270336
  9.2 5.2 copy-start.10
  12.9 43.0 %copy-start.7 = (s32[512,64]{0,1:T(8,128)S(1)}, s32[512,64]{0,1:T(8,128)}, u32[]{:S(2)}) copy-start(s32[512,64]{0,1:T(8,128)} %param.21) | copy-start | bytes 393220
  298.0 3.9 copy-start.4
  299.5 2.7 copy-start.9
  364.0 446.1 %reduce-scatter.8.cloned.1.call-start = ((), (), s32[]{:S(2)}) async-start(), calls=%async_computation.5 | async-start | bytes 540672
  366.3 3.9 copy-start.5
  370.2 510.3 %copy-start.8 = (f32[2048]{0:T(1024)S(1)}, f32[2048]{0:T(1024)}, u32[]{:S(2)}) copy-start(f32[2048]{0:T(1024)} %param.32) | copy-start | bytes 24580
  370.2 509.3 %all-reduce.3.cloned.1.call-start = ((), (), s32[]{:S(2)}) async-start(), calls=%async_computation.2 | async-start | bytes 131072 | tf_op jit(solution)/shard_map/psum | solution.py:175
  813.9 134.6 %all-reduce.5.cloned.1.call-start = ((), (), s32[]{:S(2)}) async-start(), calls=%async_computation.3 | async-start | bytes 131072 | tf_op jit(solution)/shard_map/psum | solution.py:187
  885.5 140.6 %all-gather.2.cloned.1.call-start = ((), (), s32[]{:S(2)}) async-start(), calls=%async_computation.4 | async-start | bytes 2162688 | tf_op jit(solution)/shard_map/all_gather | solution.py:189
Sparse Core Ops, SparseCore 0:
  364.1 230.1 reduce-scatter.9
  598.6 211.4 reduce-scatter.7
  814.0 65.3 all-reduce.2
  885.7 62.8 all-reduce.4
  951.0 75.0 all-gather.1
where the time goes:
time: 1040 us
  waiting for transfers between devices  641 us (62%)
  local copies, waits for them, and re-layouts  254 us (24%)
  blocking collectives  99.5 us (10%)
  matrix products  15.3 us (1%)
  between operations  13.5 us (1%)
  other arithmetic  12.2 us (1%)
    unnamed x7, waiting for transfers between devices  439 us
    scatter x1, local copies, waits for them, and re-layouts, body(): jnp.full((pool_pages,), all_rows, jnp.int32).at[targets]  120 us
    scatter x1, local copies, waits for them, and re-layouts, body(): jnp.zeros((pool_pages,), jnp.int32).at[targets].set(slot_flat, mode='drop')  120 us
    all_gather x1, waiting for transfers between devices, body(): lax.all_gather(result, 'req', axis=0, tiled=True)  73.5 us
    psum x1, waiting for transfers between devices, body(): lax.psum(projected.astype(jnp.bfloat16), 'head').astype(jnp.float32)  65.5 us
    psum x1, waiting for transfers between devices, body(): lax.psum(down_part.astype(jnp.bfloat16), 'head').astype(jnp.float32)  62.9 us
    pmax x1, blocking collectives, body(): global_peaks = lax.pmax(with_self, 'req')  58.4 us
    all_gather x1, blocking collectives, body(): all_queries = lax.all_gather(queries, 'req', axis=0, tiled=True)  41.1 us
  transfers between devices with their start and end apart: 5, of which 5 were waited for; matrix products, arithmetic and copies ran while one was open for 1% of the time, Pallas kernels for 0%

commit v1 on v0

v1 whole, which is shorter than its diff:
```python
import functools
import math

import jax
import jax.numpy as jnp
from jax import lax
from jax.experimental import pallas as pl
from jax.experimental.pallas import tpu as pltpu
from jax.sharding import PartitionSpec as P

EPSILON = 1e-06
ROPE_BASE = 1000000.0
LOW_SCORE = -1e30
LOG_TWO = math.log(2.0)
MESH_IDS = pl.DeviceIdType.MESH


def rms_inv(values):
    return lax.rsqrt(jnp.mean(values * values, axis=-1, keepdims=True) + EPSILON)


def rotate(values, position):
    half_dim = values.shape[-1] // 2
    exponent = jnp.arange(half_dim, dtype=jnp.float32) * (2.0 / values.shape[-1])
    frequency = ROPE_BASE ** (-exponent)
    angles = position[:, None] * frequency[None, :]
    ones_tail = (1,) * (values.ndim - 2)
    angles = angles.reshape((angles.shape[0],) + ones_tail + (half_dim,))
    cosine = jnp.cos(angles)
    sine_vals = jnp.sin(angles)
    front_half = values[..., :half_dim]
    back_half = values[..., half_dim:]
    return jnp.concatenate(
        [front_half * cosine - back_half * sine_vals, back_half * cosine + front_half * sine_vals],
        axis=-1,
    )


def norm_rotate(values, gain_vec, position):
    return rotate(values * rms_inv(values) * gain_vec, position)


def exchange_kernel(axis, count, spread, src_ref, out_ref, send_sems, recv_sems):
    me = lax.axis_index(axis)
    barrier = pltpu.get_barrier_semaphore()
    for offset in range(1, count):
        peer = lax.rem(me + offset, count)
        pl.semaphore_signal(barrier, inc=1, device_id={axis: peer}, device_id_type=MESH_IDS)
    pl.semaphore_wait(barrier, count - 1)
    copies = []
    for offset in range(1, count):
        peer = lax.rem(me + offset, count)
        copy = pltpu.make_async_remote_copy(
            src_ref=src_ref.at[peer] if spread else src_ref,
            dst_ref=out_ref.at[me],
            send_sem=send_sems.at[offset],
            recv_sem=recv_sems.at[offset],
            device_id={axis: peer},
            device_id_type=MESH_IDS,
        )
        copy.start()
        copies.append(copy)
    out_ref[me] = src_ref[me] if spread else src_ref[...]
    for copy in copies:
        copy.wait()


def exchange(values, axis, count, spread, ident):
    block = values.shape[1:] if spread else values.shape
    return pl.pallas_call(
        functools.partial(exchange_kernel, axis, count, spread),
        out_shape=jax.ShapeDtypeStruct((count,) + tuple(block), values.dtype),
        in_specs=[pl.BlockSpec(memory_space=pltpu.VMEM)],
        out_specs=pl.BlockSpec(memory_space=pltpu.VMEM),
        scratch_shapes=[pltpu.SemaphoreType.DMA((count,)), pltpu.SemaphoreType.DMA((count,))],
        compiler_params=pltpu.CompilerParams(collective_id=ident, has_side_effects=True),
    )(values)


def body(
    req_count,
    head_count,
    hidden,
    deal_order,
    lengths,
    page_table,
    key_cache,
    value_cache,
    attn_gain,
    w_query,
    w_key,
    w_value,
    w_gate,
    w_out,
    query_gain,
    key_gain,
    mlp_gain,
    mlp_gate,
    mlp_up,
    mlp_down,
):
    local_rows, model_width = hidden.shape
    req_index = lax.axis_index("req")
    head_index = lax.axis_index("head")
    all_rows = local_rows * req_count
    head_width = query_gain.shape[0]
    pool_pages, page_size, local_kv = key_cache.shape[:3]
    group_size = w_query.shape[1] // (local_kv * head_width)
    head_cols = local_kv * group_size * head_width
    pairs = local_kv * group_size
    chunk = model_width // head_count
    scale_factor = 1.0 / math.sqrt(head_width)
    first_own = req_index * local_rows

    with jax.named_scope("projections"):
        hidden_f = hidden.astype(jnp.float32)
        normed = (hidden_f * rms_inv(hidden_f) * attn_gain).astype(jnp.bfloat16)
        own_requests = lax.dynamic_slice_in_dim(deal_order, first_own, local_rows)
        position = lengths[own_requests].astype(jnp.float32)
        queries = jnp.dot(normed, w_query, preferred_element_type=jnp.float32).reshape(
            local_rows, local_kv, group_size, head_width
        )
        queries = norm_rotate(queries, query_gain, position).astype(jnp.bfloat16)
        new_keys = jnp.dot(normed, w_key, preferred_element_type=jnp.float32).reshape(
            local_rows, local_kv, head_width
        )
        new_keys = norm_rotate(new_keys, key_gain, position).astype(jnp.bfloat16)
        new_values = (
            jnp.dot(normed, w_value, preferred_element_type=jnp.float32)
            .astype(jnp.bfloat16)
            .reshape(local_rows, local_kv, head_width)
        )
        gate_logits = jnp.dot(normed, w_gate, preferred_element_type=jnp.float32)

    all_queries = exchange(queries.reshape(local_rows, head_cols), "req", req_count, False, 0)
    all_queries = all_queries.reshape(all_rows, head_cols)

    with jax.named_scope("page_owners"):
        dealt_lengths = lengths[deal_order]
        dealt_tables = page_table[deal_order]
        page_counts = (dealt_lengths + page_size - 1) // page_size
        slot_ids = jnp.arange(dealt_tables.shape[1], dtype=jnp.int32)
        local_ids = dealt_tables - req_index * pool_pages
        usable = (
            (slot_ids[None, :] < page_counts[:, None]) & (local_ids >= 0) & (local_ids < pool_pages)
        )
        keyed = jnp.where(usable, local_ids, pool_pages)
        page_ids = jnp.arange(pool_pages, dtype=jnp.int32)
        match = keyed[None, :, :] == page_ids[:, None, None]
        owned = jnp.any(match, axis=2)
        owner_slot = jnp.sum(jnp.where(match, slot_ids[None, None, :], 0), axis=(1, 2))
        owner_length = jnp.sum(jnp.where(owned, dealt_lengths[None, :], 0), axis=1)
        filled = jnp.clip(owner_length - owner_slot * page_size, 0, page_size)
        filled = jnp.where(jnp.any(owned, axis=1), filled, 0)
        page_queries = (
            jnp.dot(owned.astype(jnp.bfloat16), all_queries, preferred_element_type=jnp.float32)
            .astype(jnp.bfloat16)
            .reshape(pool_pages, local_kv, group_size, head_width)
        )

    with jax.named_scope("page_attention"):
        scores = (
            jnp.einsum("pkgd,ptkd->pkgt", page_queries, key_cache, preferred_element_type=jnp.float32)
            * scale_factor
        )
        live_mask = (
            jnp.arange(page_size, dtype=jnp.int32)[None, None, None, :] < filled[:, None, None, None]
        )
        scores = jnp.where(live_mask, scores, LOW_SCORE)
        page_peaks = jnp.max(scores, axis=-1)
        owned_b = owned[:, :, None, None]
        row_peaks = jnp.max(jnp.where(owned_b, page_peaks[:, None], LOW_SCORE), axis=0)
        row_shift = LOG_TWO * jnp.ceil(row_peaks / LOG_TWO)
        page_shift = jnp.max(jnp.where(owned_b, row_shift[None], LOW_SCORE), axis=1)
        weights = jnp.where(live_mask, jnp.exp(scores - page_shift[..., None]), 0.0)
        page_totals = jnp.sum(weights, axis=-1)
        page_numerators = jnp.einsum(
            "pkgt,ptkd->pkgd",
            weights.astype(jnp.bfloat16),
            value_cache,
            preferred_element_type=jnp.float32,
        )
        owned_f = owned.astype(jnp.float32)
        row_totals = jnp.dot(
            owned_f.T, page_totals.reshape(pool_pages, pairs), precision=lax.Precision.HIGHEST
        )
        row_numerators = jnp.dot(
            owned_f.T,
            page_numerators.reshape(pool_pages, head_cols),
            precision=lax.Precision.HIGHEST,
        )
        pad = (-(head_cols + 2 * pairs)) % 128
        message = jnp.concatenate(
            [
                row_numerators,
                row_shift.reshape(all_rows, pairs),
                row_totals,
                jnp.zeros((all_rows, pad), jnp.float32),
            ],
            axis=1,
        ).reshape(req_count, local_rows, -1)

    arrived = exchange(message, "req", req_count, True, 1)

    with jax.named_scope("combine"):
        got_numerators = arrived[:, :, :head_cols].reshape(
            req_count, local_rows, local_kv, group_size, head_width
        )
        got_shift = arrived[:, :, head_cols : head_cols + pairs].reshape(
            req_count, local_rows, local_kv, group_size
        )
        got_totals = arrived[:, :, head_cols + pairs : head_cols + 2 * pairs].reshape(
            req_count, local_rows, local_kv, group_size
        )
        self_scores = (
            jnp.einsum("rkgd,rkd->rkg", queries, new_keys, preferred_element_type=jnp.float32)
            * scale_factor
        )
        self_shift = LOG_TWO * jnp.ceil(self_scores / LOG_TWO)
        shift = jnp.maximum(jnp.max(got_shift, axis=0), self_shift)
        factor = jnp.exp(got_shift - shift[None])
        self_weight = jnp.exp(self_scores - shift)
        totals = jnp.sum(got_totals * factor, axis=0) + self_weight
        self_rounded = self_weight.astype(jnp.bfloat16).astype(jnp.float32)
        numerators = (
            jnp.sum(got_numerators * factor[..., None], axis=0)
            + self_rounded[..., None] * new_values.astype(jnp.float32)[:, :, None, :]
        )
        heads_out = (numerators / totals[..., None]).reshape(local_rows, head_cols)
        attended = (heads_out * jax.nn.sigmoid(gate_logits)).astype(jnp.bfloat16)
        projected = jnp.dot(attended, w_out, preferred_element_type=jnp.float32)
        projected = projected.reshape(local_rows, head_count, chunk).transpose(1, 0, 2)

    attn_parts = exchange(projected, "head", head_count, True, 2)

    with jax.named_scope("residual"):
        hidden_chunk = lax.dynamic_slice_in_dim(hidden_f, head_index * chunk, chunk, axis=1)
        mixed_chunk = (hidden_chunk + jnp.sum(attn_parts, axis=0)).astype(jnp.bfloat16)

    mixed_all = exchange(mixed_chunk, "head", head_count, False, 3)

    with jax.named_scope("mlp"):
        mixed_rows = mixed_all.transpose(1, 0, 2).reshape(local_rows, model_width)
        mixed_f = mixed_rows.astype(jnp.float32)
        normed_two = (mixed_f * rms_inv(mixed_f) * mlp_gain).astype(jnp.bfloat16)
        gate_part = jnp.dot(normed_two, mlp_gate, preferred_element_type=jnp.float32)
        up_part = jnp.dot(normed_two, mlp_up, preferred_element_type=jnp.float32)
        inner_act = (jax.nn.silu(gate_part) * up_part).astype(jnp.bfloat16)
        down_part = jnp.dot(inner_act, mlp_down, preferred_element_type=jnp.float32)
        down_part = down_part.reshape(local_rows, head_count, chunk).transpose(1, 0, 2)

    mlp_parts = exchange(down_part, "head", head_count, True, 4)

    with jax.named_scope("result"):
        result_chunk = (mixed_chunk.astype(jnp.float32) + jnp.sum(mlp_parts, axis=0)).astype(
            jnp.bfloat16
        )

    result_all = exchange(result_chunk, "req", req_count, False, 5).reshape(all_rows, chunk)

    with jax.named_scope("reorder"):
        wanted = first_own + jnp.arange(local_rows, dtype=jnp.int32)
        selector = (deal_order[None, :] == wanted[:, None]).astype(jnp.bfloat16)
        picked = jnp.dot(selector, result_all, preferred_element_type=jnp.float32).astype(
            jnp.bfloat16
        )

    output_parts = exchange(picked, "head", head_count, False, 6)
    return output_parts.transpose(1, 0, 2).reshape(local_rows, model_width)


def solution(mesh):
    return jax.shard_map(
        functools.partial(body, mesh.shape["req"], mesh.shape["head"]),
        mesh=mesh,
        in_specs=(
            P("req", None),
            P(),
            P(),
            P(),
            P("req", None, "head", None),
            P("req", None, "head", None),
            P(),
            P(None, "head"),
            P(None, "head"),
            P(None, "head"),
            P(None, "head"),
            P("head", None),
            P(),
            P(),
            P(),
            P(None, "head"),
            P(None, "head"),
            P("head", None),
        ),
        out_specs=P("req", None),
        check_vma=False,
    )
```

time: 1040 us -> 141 us (0.14)
  waiting for transfers between devices: 641 us -> 0 us
  local copies, waits for them, and re-layouts: 254 us -> 13.2 us
  blocking collectives: 99.5 us -> 0 us
  Pallas kernels: 0 us -> 92.8 us
  between operations: 13.5 us -> 0.47 us
    unnamed x7 -> x0, waiting for transfers between devices: 439 us -> none
    scatter x3 -> x0, local copies, waits for them, and re-layouts: 242 us -> none  [the longest x1 120 us: body(): jnp.full((pool_pages,), all_rows, jnp.int32).at[targets]]
    psum x2 -> x0, waiting for transfers between devices: 128 us -> none  [the longest x1 65.5 us: body(): lax.psum(projected.astype(jnp.bfloat16), 'head').astype(jnp.float32)]
    pallas_call x0 -> x7, Pallas kernels: none -> 92.8 us  [exchange(): pl.pallas_call(functools.partial(exchange_kernel, axis, count, spread), o...]
    all_gather x1 -> x0, waiting for transfers between devices: 73.5 us -> none  [body(): lax.all_gather(result, 'req', axis=0, tiled=True)]
    pmax x1 -> x0, blocking collectives: 58.4 us -> none  [body(): global_peaks = lax.pmax(with_self, 'req')]
    all_gather x1 -> x0, blocking collectives: 41.1 us -> none  [body(): all_queries = lax.all_gather(queries, 'req', axis=0, tiled=True)]
  transfers between devices with their start and end apart: 5 -> 0, of which waited for: 5 -> 0; matrix products, arithmetic and copies ran while one was open for 1% -> 0% of each run, Pallas kernels for 0% -> 0%
where the time goes in v1:
time: 141 us; the launch traced here: 140 us
  Pallas kernels  92.8 us (66%)
  matrix products  17.3 us (12%)
  other arithmetic  16 us (11%)
  local copies, waits for them, and re-layouts  13.2 us (9%)
    pallas_call x7, Pallas kernels, exchange(): pl.pallas_call(functools.partial(exchange_kernel, axis, count, spread), o...  92.8 us
    gather x1, local copies, waits for them, and re-layouts, body(): dealt_lengths = lengths[deal_order]  3.49 us
    mul x2, local copies, waits for them, and re-layouts, body(): got_numerators * factor[..., None]  2.87 us

profile of v1, /device:TPU:1, one launch (start us, length us, event | category | flops | bytes accessed | tf_op | source)
XLA Modules:
  0.0 139.8 jit_solution(16259092735656992440)
XLA Ops:
  0.9 1.4 gather_fusion.2
  3.4 1.6 %fusion.61 = f32[16,256]{1,0:T(8,128)S(1)} fusion(bf16[2048,256]{1,0:T(8,128)(2,1)} %param.25, f32[2048]{0:T(1024)} %param.24, f32[16]{0:T(128)S(1)} %add_rsqrt_fusion.3, bf16[16,2048]{1,0:T(8,128)(2,1)} %param.18), kind=kOutput, calls=%fused_computation.124 | convolution fusion | flops 16908288 | bytes 1138752 | tf_op jit(solution)/shard_map/projections/dot_general | solution.py:120
  6.7 18.4 %shard_map.172 = bf16[32,16,256]{2,1,0:T(8,128)(2,1)} custom-call(bf16[16,256]{1,0:T(8,128)(2,1)} %bitcast.103), custom_call_target="tpu_custom_call" | custom-call | tf_op jit(solution)/shard_map/pallas_call | solution.py:70
  25.2 3.5 %gather_fusion = s32[512]{0:T(512)S(1)} fusion(s32[512]{0:T(512)S(1)} %copy-done.1, s32[1024]{0:T(1024)S(1)} %pad_clamp_fusion.1), kind=kCustom, calls=%fused_computation | custom fusion | bytes 6144 | tf_op jit(solution)/shard_map/page_owners/gather | solution.py:139
  30.1 2.2 %fusion = (pred[64]{0:T(512)(128)(4,1)S(1)}, pred[64,512]{1,0:T(8,128)(4,1)S(1)}) fusion(s32[512,64]{0,1:T(8,128)S(1)} %copy.50), kind=kLoop, calls=%fused_computation.5 | loop fusion | flops 6258624 | bytes 163904 | tf_op jit(solution)/shard_map/page_owners/reduce_or | solution.py:154
  32.7 1.3 select_reduce_fusion
  34.0 1.3 fusion.62
  35.7 2.3 %fusion.2 = f32[64,2,128]{2,1,0:T(2,128)S(1)} fusion(bf16[64,128,1,128]{3,1,2,0:T(8,128)(2,1)} %param.23, f32[64,2,128]{2,1,0:T(2,128)S(1)} %get-tuple-element.20, pred[64,128]{1,0:T(8,128)(4,1)S(1)} %iota_compare_fusion.2, f32[64,2]{1,0:T(8,128)S(1)} %copy.53), kind=kOutput, calls=%fused_computation.7 | convolution fusion | flops 4243456 | bytes 2236928 | tf_op jit(solution)/shard_map/page_attention/pkgt,ptkd->pkgd/dot_general | solution.py:177
  40.4 26.2 %shard_map.173 = f32[32,16,384]{2,1,0:T(8,128)} custom-call(f32[32,16,384]{2,1,0:T(8,128)} %maximum_maximum_fusion.src_ref), custom_call_target="tpu_custom_call" | custom-call | tf_op jit(solution)/shard_map/pallas_call | solution.py:70
  67.7 1.4 multiply_reduce_fusion.4
  69.6 1.2 multiply_reduce_fusion.1
  70.8 1.4 %mul.338 = f32[32,16,2,128]{3,2,1,0:T(2,128)} broadcast(f32[32,16,2]{2,1,0:T(8,128)S(1)} %get-tuple-element.8), dimensions={0,1,2} | broadcast | bytes 528384 | tf_op jit(solution)/shard_map/combine/mul | solution.py:226
  72.2 1.5 %mul.339 = f32[32,16,256]{2,1,0:T(8,128)S(1)} reshape(f32[32,16,2,128]{3,2,1,0:T(2,128)} %mul.338) | data formatting | bytes 1048576 | tf_op jit(solution)/shard_map/combine/mul | solution.py:226
  73.8 1.3 fusion.20
  75.2 2.3 %fusion.19 = f32[16,2048]{1,0:T(8,128)S(1)} fusion(bf16[256,2048]{1,0:T(8,128)(2,1)} %param.29, bf16[2048,256]{1,0:T(8,128)(2,1)} %param.28, f32[2,8,2,128]{3,2,1,0:T(2,128)S(1)} %bitcast.100, f32[16,256]{1,0:T(8,128)S(1)} %multiply_reduce_fusion, f32[2,8,2,128]{3,2,1,0:T(2,128)S(1)} %bitcast.99, f32[2048]{0:T(1024)S(1)} %copy-done.5, ...), kind=kOutput, calls=%fused_computation.24 | convolution fusion | flops 33714176 | bytes 2351168 | tf_op jit(solution)/shard_map/combine/dot_general | solution.py:231
  78.2 9.6 %shard_map.174 = f32[8,16,256]{2,1,0:T(8,128)} custom-call(f32[8,16,256]{2,1,0:T(8,128)} %bitcast.95), custom_call_target="tpu_custom_call" | custom-call | tf_op jit(solution)/shard_map/pallas_call | solution.py:70
  89.4 6.8 %shard_map.175 = bf16[8,16,256]{2,1,0:T(8,128)(2,1)} custom-call(bf16[16,256]{1,0:T(8,128)(2,1)} %add_convert_fusion.1.src_ref), custom_call_target="tpu_custom_call" | custom-call | tf_op jit(solution)/shard_map/pallas_call | solution.py:70
  98.0 1.8 %fusion.59 = f32[16,384]{1,0:T(8,128)S(1)} fusion(bf16[2048,384]{1,0:T(8,128)(2,1)} %param.33, f32[16,2048]{1,0:T(8,128)S(1)} %bitcast.86, f32[2048]{0:T(1024)S(1)} %copy-done.8, f32[16]{0:T(128)S(1)} %add_rsqrt_fusion.1), kind=kOutput, calls=%fused_computation.122 | convolution fusion | flops 25264128 | bytes 1736768 | tf_op jit(solution)/shard_map/mlp/dot_general | solution.py:246
  99.8 2.7 %fusion.17 = f32[16,2048]{1,0:T(8,128)S(1)} fusion(bf16[384,2048]{1,0:T(8,128)(2,1)} %param.35, bf16[2048,384]{1,0:T(8,128)(2,1)} %param.34, f32[16,384]{1,0:T(8,128)S(1)} %fusion.59, f32[16,2048]{1,0:T(8,128)S(1)} %bitcast.87, f32[2048]{0:T(1024)S(1)} %copy-done.8, f32[16]{0:T(128)S(1)} %add_rsqrt_fusion.1), kind=kOutput, calls=%fused_computation.21 | convolution fusion | flops 50466816 | bytes 3440704 | tf_op jit(solution)/shard_map/mlp/dot_general | solution.py:249
  103.1 7.5 %shard_map.176 = f32[8,16,256]{2,1,0:T(8,128)} custom-call(f32[8,16,256]{2,1,0:T(8,128)} %bitcast.96), custom_call_target="tpu_custom_call" | custom-call | tf_op jit(solution)/shard_map/pallas_call | solution.py:70
  112.1 16.2 %shard_map.177 = bf16[32,16,256]{2,1,0:T(8,128)(2,1)} custom-call(bf16[16,256]{1,0:T(8,128)(2,1)} %add_convert_fusion.src_ref), custom_call_target="tpu_custom_call" | custom-call | tf_op jit(solution)/shard_map/pallas_call | solution.py:70
  128.4 1.7 %convolution_convert_fusion.1.src_ref = bf16[16,256]{1,0:T(8,128)(2,1)} fusion(bf16[512,256]{1,0:T(8,128)(2,1)} %bitcast.97, s32[512]{0:T(512)S(1)} %copy-done.9, s32[16]{0:T(128)S(1)} %iota_add_fusion), kind=kOutput, calls=%fused_computation.23 | convolution fusion | flops 4206592 | bytes 272448 | tf_op jit(solution)/shard_map/reorder/dot_general | solution.py:264
  130.1 8.2 %shard_map.178 = bf16[8,16,256]{2,1,0:T(8,128)(2,1)} custom-call(bf16[16,256]{1,0:T(8,128)(2,1)} %convolution_convert_fusion.1.src_ref), custom_call_target="tpu_custom_call" | custom-call | tf_op jit(solution)/shard_map/pallas_call | solution.py:70
  138.3 1.5 %copy.69 = bf16[8,2,8,256]{3,2,0,1:T(8,128)(2,1)} copy(bf16[8,2,8,256]{3,2,1,0:T(8,128)(2,1)} %bitcast.98) | data formatting | bytes 131072 | tf_op jit(solution)/shard_map/reshape | solution.py:269
  (85 shorter events, 16.3 us)
Async XLA Ops:
  0.0 34.0 %copy-start = (bf16[64,128,1,128]{3,1,2,0:T(8,128)(2,1)S(1)}, bf16[64,128,1,128]{3,1,2,0:T(8,128)(2,1)}, u32[]{:S(2)}) copy-start(bf16[64,128,1,128]{3,1,2,0:T(8,128)(2,1)} %param.22) | copy-start | bytes 6291460
  0.0 25.1 %copy-start.9 = (s32[512]{0:T(512)S(1)}, s32[512]{0:T(512)}, u32[]{:S(2)}) copy-start(s32[512]{0:T(512)} %param.19) | copy-start | bytes 6148
  0.0 25.2 %copy-start.1 = (s32[512]{0:T(512)S(1)}, s32[512]{0:T(512)}, u32[]{:S(2)}) copy-start(s32[512]{0:T(512)} %param.20) | copy-start | bytes 6148
  0.9 27.8 %copy-start.6 = (s32[512,64]{0,1:T(8,128)S(1)}, s32[512,64]{0,1:T(8,128)}, u32[]{:S(2)}) copy-start(s32[512,64]{0,1:T(8,128)} %param.21) | copy-start | bytes 393220
  28.7 3.7 %copy-start.4 = (bf16[32,16,256]{2,1,0:T(8,128)(2,1)S(1)}, bf16[32,16,256]{2,1,0:T(8,128)(2,1)}, u32[]{:S(2)}) copy-start(bf16[32,16,256]{2,1,0:T(8,128)(2,1)} %shard_map.172) | copy-start | bytes 786436
  38.9 28.8 %copy-start.3 = (bf16[16,2048]{1,0:T(8,128)(2,1)S(1)}, bf16[16,2048]{1,0:T(8,128)(2,1)}, u32[]{:S(2)}) copy-start(bf16[16,2048]{1,0:T(8,128)(2,1)} %param.18) | copy-start | bytes 196612
  38.9 28.8 %copy-start.5 = (f32[2048]{0:T(1024)S(1)}, f32[2048]{0:T(1024)}, u32[]{:S(2)}) copy-start(f32[2048]{0:T(1024)} %param.24) | copy-start | bytes 24580
  39.4 29.7 %copy-start.10 = (f32[128]{0:T(128)S(1)}, f32[128]{0:T(128)}, u32[]{:S(2)}) copy-start(f32[128]{0:T(128)} %param.31) | copy-start | bytes 1540
  66.6 7.1 %copy-start.2 = (f32[32,16,384]{2,1,0:T(8,128)S(1)}, f32[32,16,384]{2,1,0:T(8,128)}, u32[]{:S(2)}) copy-start(f32[32,16,384]{2,1,0:T(8,128)} %shard_map.173) | copy-start | bytes 2359300
  75.0 23.0 %copy-start.8 = (f32[2048]{0:T(1024)S(1)}, f32[2048]{0:T(1024)}, u32[]{:S(2)}) copy-start(f32[2048]{0:T(1024)} %param.32) | copy-start | bytes 24580
  99.8 11.7 %copy-start.7 = (bf16[16,256]{1,0:T(8,128)(2,1)S(1)}, bf16[16,256]{1,0:T(8,128)(2,1)}, u32[]{:S(2)}) copy-start(bf16[16,256]{1,0:T(8,128)(2,1)} %add_convert_fusion.1.src_ref) | copy-start | bytes 24580

commit v2 on v1

--- a/solution.py
+++ b/solution.py
@@ -40,7 +40,10 @@
     return rotate(values * rms_inv(values) * gain_vec, position)
 
 
-def exchange_kernel(axis, count, spread, src_ref, out_ref, send_sems, recv_sems):
+def exchange_kernel(axis, count, spreads, *refs):
+    arrays = len(spreads)
+    sources, outputs = refs[:arrays], refs[arrays : 2 * arrays]
+    send_sems, recv_sems = refs[2 * arrays], refs[2 * arrays + 1]
     me = lax.axis_index(axis)
     barrier = pltpu.get_barrier_semaphore()
     for offset in range(1, count):
@@ -50,31 +53,45 @@
     copies = []
     for offset in range(1, count):
         peer = lax.rem(me + offset, count)
-        copy = pltpu.make_async_remote_copy(
-            src_ref=src_ref.at[peer] if spread else src_ref,
-            dst_ref=out_ref.at[me],
-            send_sem=send_sems.at[offset],
-            recv_sem=recv_sems.at[offset],
-            device_id={axis: peer},
-            device_id_type=MESH_IDS,
-        )
-        copy.start()
-        copies.append(copy)
-    out_ref[me] = src_ref[me] if spread else src_ref[...]
+        for which in range(arrays):
+            src_ref, out_ref = sources[which], outputs[which]
+            copy = pltpu.make_async_remote_copy(
+                src_ref=src_ref.at[peer] if spreads[which] else src_ref,
+                dst_ref=out_ref.at[me],
+                send_sem=send_sems.at[which, offset],
+                recv_sem=recv_sems.at[which, offset],
+                device_id={axis: peer},
+                device_id_type=MESH_IDS,
+            )
+            copy.start()
+            copies.append(copy)
+    for which in range(arrays):
+        src_ref, out_ref = sources[which], outputs[which]
+        out_ref[me] = src_ref[me] if spreads[which] else src_ref[...]
     for copy in copies:
         copy.wait()
 
 
+def exchange_many(arrays, spreads, axis, count, ident):
+    shapes = []
+    for values, spread in zip(arrays, spreads):
+        block = values.shape[1:] if spread else values.shape
+        shapes.append(jax.ShapeDtypeStruct((count,) + tuple(block), values.dtype))
+    return pl.pallas_call(
+        functools.partial(exchange_kernel, axis, count, tuple(spreads)),
+        out_shape=tuple(shapes),
+        in_specs=[pl.BlockSpec(memory_space=pltpu.VMEM)] * len(arrays),
+        out_specs=tuple(pl.BlockSpec(memory_space=pltpu.VMEM) for _ in arrays),
+        scratch_shapes=[
+            pltpu.SemaphoreType.DMA((len(arrays), count)),
+            pltpu.SemaphoreType.DMA((len(arrays), count)),
+        ],
+        compiler_params=pltpu.CompilerParams(collective_id=ident, has_side_effects=True),
+    )(*arrays)
+
+
 def exchange(values, axis, count, spread, ident):
-    block = values.shape[1:] if spread else values.shape
-    return pl.pallas_call(
-        functools.partial(exchange_kernel, axis, count, spread),
-        out_shape=jax.ShapeDtypeStruct((count,) + tuple(block), values.dtype),
-        in_specs=[pl.BlockSpec(memory_space=pltpu.VMEM)],
-        out_specs=pl.BlockSpec(memory_space=pltpu.VMEM),
-        scratch_shapes=[pltpu.SemaphoreType.DMA((count,)), pltpu.SemaphoreType.DMA((count,))],
-        compiler_params=pltpu.CompilerParams(collective_id=ident, has_side_effects=True),
-    )(values)
+    return exchange_many((values,), (spread,), axis, count, ident)[0]
 
 
 def body(
@@ -116,7 +133,9 @@
         hidden_f = hidden.astype(jnp.float32)
         normed = (hidden_f * rms_inv(hidden_f) * attn_gain).astype(jnp.bfloat16)
         own_requests = lax.dynamic_slice_in_dim(deal_order, first_own, local_rows)
-        position = lengths[own_requests].astype(jnp.float32)
+        request_ids = jnp.arange(all_rows, dtype=jnp.int32)
+        own_pick = own_requests[:, None] == request_ids[None, :]
+        position = jnp.sum(jnp.where(own_pick, lengths[None, :], 0), axis=1).astype(jnp.float32)
         queries = jnp.dot(normed, w_query, preferred_element_type=jnp.float32).reshape(
             local_rows, local_kv, group_size, head_width
         )
@@ -136,22 +155,25 @@
     all_queries = all_queries.reshape(all_rows, head_cols)
 
     with jax.named_scope("page_owners"):
-        dealt_lengths = lengths[deal_order]
-        dealt_tables = page_table[deal_order]
-        page_counts = (dealt_lengths + page_size - 1) // page_size
-        slot_ids = jnp.arange(dealt_tables.shape[1], dtype=jnp.int32)
-        local_ids = dealt_tables - req_index * pool_pages
+        page_counts = (lengths + page_size - 1) // page_size
+        slot_ids = jnp.arange(page_table.shape[1], dtype=jnp.int32)
+        local_ids = page_table - req_index * pool_pages
         usable = (
             (slot_ids[None, :] < page_counts[:, None]) & (local_ids >= 0) & (local_ids < pool_pages)
         )
         keyed = jnp.where(usable, local_ids, pool_pages)
         page_ids = jnp.arange(pool_pages, dtype=jnp.int32)
         match = keyed[None, :, :] == page_ids[:, None, None]
-        owned = jnp.any(match, axis=2)
+        owned_requests = jnp.any(match, axis=2)
         owner_slot = jnp.sum(jnp.where(match, slot_ids[None, None, :], 0), axis=(1, 2))
-        owner_length = jnp.sum(jnp.where(owned, dealt_lengths[None, :], 0), axis=1)
+        owner_length = jnp.sum(jnp.where(owned_requests, lengths[None, :], 0), axis=1)
         filled = jnp.clip(owner_length - owner_slot * page_size, 0, page_size)
-        filled = jnp.where(jnp.any(owned, axis=1), filled, 0)
+        filled = jnp.where(jnp.any(owned_requests, axis=1), filled, 0)
+        dealing = (request_ids[:, None] == deal_order[None, :]).astype(jnp.bfloat16)
+        owned = (
+            jnp.dot(owned_requests.astype(jnp.bfloat16), dealing, preferred_element_type=jnp.float32)
+            > 0.5
+        )
         page_queries = (
             jnp.dot(owned.astype(jnp.bfloat16), all_queries, preferred_element_type=jnp.float32)
             .astype(jnp.bfloat16)
@@ -189,29 +211,23 @@
             page_numerators.reshape(pool_pages, head_cols),
             precision=lax.Precision.HIGHEST,
         )
-        pad = (-(head_cols + 2 * pairs)) % 128
-        message = jnp.concatenate(
-            [
-                row_numerators,
-                row_shift.reshape(all_rows, pairs),
-                row_totals,
-                jnp.zeros((all_rows, pad), jnp.float32),
-            ],
-            axis=1,
-        ).reshape(req_count, local_rows, -1)
-
-    arrived = exchange(message, "req", req_count, True, 1)
+        numerator_message = row_numerators.astype(jnp.bfloat16).reshape(req_count, local_rows, head_cols)
+        stats_message = jnp.concatenate(
+            [row_shift.reshape(req_count, local_rows, pairs), row_totals.reshape(req_count, local_rows, pairs)],
+            axis=2,
+        ).transpose(0, 2, 1)
+
+    got_numerators, got_stats = exchange_many(
+        (numerator_message, stats_message), (True, True), "req", req_count, 1
+    )
 
     with jax.named_scope("combine"):
-        got_numerators = arrived[:, :, :head_cols].reshape(
+        got_numerators = got_numerators.astype(jnp.float32).reshape(
             req_count, local_rows, local_kv, group_size, head_width
         )
-        got_shift = arrived[:, :, head_cols : head_cols + pairs].reshape(
-            req_count, local_rows, local_kv, group_size
-        )
-        got_totals = arrived[:, :, head_cols + pairs : head_cols + 2 * pairs].reshape(
-            req_count, local_rows, local_kv, group_size
-        )
+        got_stats = got_stats.transpose(0, 2, 1)
+        got_shift = got_stats[:, :, :pairs].reshape(req_count, local_rows, local_kv, group_size)
+        got_totals = got_stats[:, :, pairs:].reshape(req_count, local_rows, local_kv, group_size)
         self_scores = (
             jnp.einsum("rkgd,rkd->rkg", queries, new_keys, preferred_element_type=jnp.float32)
             * scale_factor

time: 141 us -> 127 us (0.901)
  Pallas kernels: 92.8 us -> 83.3 us
  local copies, waits for them, and re-layouts: 13.2 us -> 6.46 us
  matrix products: 17.3 us -> 19 us
    pallas_call x7, Pallas kernels: 92.8 us -> 83.3 us  [exchange_many(): pl.pallas_call(functools.partial(exchange_kernel, axis, count, tuple(spre...]
    gather x3 -> x0, local copies, waits for them, and re-layouts: 5.91 us -> none  [the longest x1 3.49 us: body(): dealt_lengths = lengths[deal_order]]
    mul x2, local copies, waits for them, and re-layouts: 2.87 us -> 1.02 us  [body(): got_numerators * factor[..., None]]
where the time goes in v2:
time: 127 us; the launch traced here: 126 us
  Pallas kernels  83.3 us (66%)
  matrix products  19 us (15%)
  other arithmetic  16.7 us (13%)
  local copies, waits for them, and re-layouts  6.46 us (5%)
    pallas_call x7, Pallas kernels, exchange_many(): pl.pallas_call(functools.partial(exchange_kernel, axis, count, tuple(spre...  83.3 us
    dot_general x1, matrix products, body(): down_part = jnp.dot(inner_act, mlp_down, preferred_element_type=jnp.float32)  2.68 us

profile of v2, /device:TPU:1, one launch (start us, length us, event | category | flops | bytes accessed | tf_op | source)
XLA Modules:
  0.0 125.9 jit_solution(9283521077083829822)
XLA Ops:
  1.9 1.0 multiply_reduce_fusion.1
  2.9 1.6 %fusion.70 = f32[16,256]{1,0:T(8,128)S(1)} fusion(bf16[2048,256]{1,0:T(8,128)(2,1)} %param.25, f32[2048]{0:T(1024)} %param.24, f32[16]{0:T(128)S(1)} %add_rsqrt_fusion.3, bf16[16,2048]{1,0:T(8,128)(2,1)} %param.18), kind=kOutput, calls=%fused_computation.131 | convolution fusion | flops 16908288 | bytes 1138752 | tf_op jit(solution)/shard_map/projections/dot_general | solution.py:139
  6.2 18.4 %shard_map.172 = bf16[32,16,256]{2,1,0:T(8,128)(2,1)} custom-call(bf16[16,256]{1,0:T(8,128)(2,1)} %bitcast.131), custom_call_target="tpu_custom_call" | custom-call | tf_op jit(solution)/shard_map/pallas_call | solution.py:80
  26.2 2.2 %fusion = (pred[64]{0:T(512)(128)(4,1)S(1)}, pred[64,512]{1,0:T(8,128)(4,1)S(1)}) fusion(s32[512,64]{0,1:T(8,128)S(1)} %fusion.25), kind=kLoop, calls=%fused_computation.2 | loop fusion | flops 6258624 | bytes 163904 | tf_op jit(solution)/shard_map/page_owners/reduce_or | solution.py:171
  28.7 1.1 convolution_convert_fusion.1
  30.0 1.3 %select_reduce_fusion = s32[64]{0:T(128)S(1)} fusion(s32[512,64]{0,1:T(8,128)S(1)} %fusion.25), kind=kLoop, calls=%fused_computation | loop fusion | flops 6291392 | bytes 131328 | tf_op jit(solution)/shard_map/page_owners/reduce_sum | solution.py:168
  31.4 1.3 %fusion.71 = (f32[64,2]{1,0:T(8,128)S(1)}, f32[64,2,128]{2,1,0:T(2,128)S(1)}) fusion(bf16[64,2,128]{2,1,0:T(2,128)(2,1)S(1)} %reshape.460, bf16[64,128,1,128]{3,1,2,0:T(8,128)(2,1)S(1)} %copy-done, pred[64,128]{1,0:T(8,128)(4,1)S(1)} %iota_compare_fusion.5), kind=kOutput, calls=%fused_computation.132 | convolution fusion | flops 4243328 | bytes 2204160 | tf_op jit(solution)/shard_map/page_attention/pkgd,ptkd->pkgt/dot_general | solution.py:185
  33.5 1.0 fusion.29
  35.3 2.3 %fusion.2 = f32[64,2,128]{2,1,0:T(2,128)S(1)} fusion(bf16[64,128,1,128]{3,1,2,0:T(8,128)(2,1)} %param.23, f32[64,2,128]{2,1,0:T(2,128)S(1)} %get-tuple-element.24, pred[64,128]{1,0:T(8,128)(4,1)S(1)} %iota_compare_fusion.5, f32[64,2]{1,0:T(8,128)S(1)} %copy.62), kind=kOutput, calls=%fused_computation.4 | convolution fusion | flops 4243456 | bytes 2236928 | tf_op jit(solution)/shard_map/page_attention/pkgt,ptkd->pkgd/dot_general | solution.py:199
  37.6 1.1 convolution_convert_fusion
  38.8 15.8 %shard_map.173 = (bf16[32,16,256]{2,1,0:T(8,128)(2,1)}, f32[32,4,16]{2,1,0:T(4,128)}) custom-call(bf16[32,16,256]{2,1,0:T(8,128)(2,1)} %bitcast.117, f32[32,4,16]{2,1,0:T(4,128)} %maximum_bitcast_fusion.refs_1_), custom_call_target="tpu_custom_call" | custom-call | tf_op jit(solution)/shard_map/pallas_call | solution.py:80
  56.5 1.0 fusion.28
  59.0 1.3 %fusion.20 = f32[16,128]{1,0:T(8,128)S(1)} fusion(bf16[2048,128]{1,0:T(8,128)(2,1)} %param.27, f32[2048]{0:T(1024)S(1)} %copy-done.4, f32[16]{0:T(128)S(1)} %add_rsqrt_fusion.3, bf16[16,2048]{1,0:T(8,128)(2,1)S(1)} %copy-done.1), kind=kOutput, calls=%fused_computation.25 | convolution fusion | flops 8523776 | bytes 606272 | tf_op jit(solution)/shard_map/projections/dot_general | solution.py:148
  60.5 2.3 %fusion.19 = f32[16,2048]{1,0:T(8,128)S(1)} fusion(bf16[256,2048]{1,0:T(8,128)(2,1)} %param.29, bf16[2048,256]{1,0:T(8,128)(2,1)} %param.28, f32[2,8,2,128]{3,2,1,0:T(2,128)S(1)} %bitcast.128, f32[16,256]{1,0:T(8,128)S(1)} %multiply_reduce_fusion, f32[2,8,2,128]{3,2,1,0:T(2,128)S(1)} %bitcast.127, f32[2048]{0:T(1024)S(1)} %copy-done.4, ...), kind=kOutput, calls=%fused_computation.23 | convolution fusion | flops 33714176 | bytes 2351168 | tf_op jit(solution)/shard_map/combine/dot_general | solution.py:247
  63.5 11.1 %shard_map.174 = f32[8,16,256]{2,1,0:T(8,128)} custom-call(f32[8,16,256]{2,1,0:T(8,128)} %bitcast.121), custom_call_target="tpu_custom_call" | custom-call | tf_op jit(solution)/shard_map/pallas_call | solution.py:80
  76.2 6.8 %shard_map.175 = bf16[8,16,256]{2,1,0:T(8,128)(2,1)} custom-call(bf16[16,256]{1,0:T(8,128)(2,1)} %add_convert_fusion.1.refs_0_), custom_call_target="tpu_custom_call" | custom-call | tf_op jit(solution)/shard_map/pallas_call | solution.py:80
  83.8 1.0 fusion.22
  84.8 1.8 %fusion.68 = f32[16,384]{1,0:T(8,128)S(1)} fusion(bf16[2048,384]{1,0:T(8,128)(2,1)} %param.33, f32[16,2048]{1,0:T(8,128)S(1)} %bitcast.114, f32[2048]{0:T(1024)S(1)} %copy-done.6, f32[16]{0:T(128)S(1)} %add_rsqrt_fusion.1), kind=kOutput, calls=%fused_computation.129 | convolution fusion | flops 25264128 | bytes 1736768 | tf_op jit(solution)/shard_map/mlp/dot_general | solution.py:262
  86.6 2.7 %fusion.17 = f32[16,2048]{1,0:T(8,128)S(1)} fusion(bf16[384,2048]{1,0:T(8,128)(2,1)} %param.35, bf16[2048,384]{1,0:T(8,128)(2,1)} %param.34, f32[16,384]{1,0:T(8,128)S(1)} %fusion.68, f32[16,2048]{1,0:T(8,128)S(1)} %bitcast.115, f32[2048]{0:T(1024)S(1)} %copy-done.6, f32[16]{0:T(128)S(1)} %add_rsqrt_fusion.1), kind=kOutput, calls=%fused_computation.20 | convolution fusion | flops 50466816 | bytes 3440704 | tf_op jit(solution)/shard_map/mlp/dot_general | solution.py:265
  89.9 7.5 %shard_map.176 = f32[8,16,256]{2,1,0:T(8,128)} custom-call(f32[8,16,256]{2,1,0:T(8,128)} %bitcast.122), custom_call_target="tpu_custom_call" | custom-call | tf_op jit(solution)/shard_map/pallas_call | solution.py:80
  98.9 14.8 %shard_map.177 = bf16[32,16,256]{2,1,0:T(8,128)(2,1)} custom-call(bf16[16,256]{1,0:T(8,128)(2,1)} %add_convert_fusion.refs_0_), custom_call_target="tpu_custom_call" | custom-call | tf_op jit(solution)/shard_map/pallas_call | solution.py:80
  113.8 1.7 %convolution_convert_fusion.2.refs_0_ = bf16[16,256]{1,0:T(8,128)(2,1)} fusion(bf16[512,256]{1,0:T(8,128)(2,1)} %bitcast.123, s32[512]{0:T(512)S(1)} %copy-done.9, s32[16]{0:T(128)S(1)} %iota_add_fusion), kind=kOutput, calls=%fused_computation.22 | convolution fusion | flops 4206592 | bytes 272448 | tf_op jit(solution)/shard_map/reorder/dot_general | solution.py:280
  115.5 8.9 %shard_map.178 = bf16[8,16,256]{2,1,0:T(8,128)(2,1)} custom-call(bf16[16,256]{1,0:T(8,128)(2,1)} %convolution_convert_fusion.2.refs_0_), custom_call_target="tpu_custom_call" | custom-call | tf_op jit(solution)/shard_map/pallas_call | solution.py:80
  124.4 1.5 %copy.80 = bf16[8,2,8,256]{3,2,0,1:T(8,128)(2,1)} copy(bf16[8,2,8,256]{3,2,1,0:T(8,128)(2,1)} %bitcast.124) | data formatting | bytes 131072 | tf_op jit(solution)/shard_map/reshape | solution.py:285
  (79 shorter events, 16.2 us)
Async XLA Ops:
  0.0 31.4 %copy-start = (bf16[64,128,1,128]{3,1,2,0:T(8,128)(2,1)S(1)}, bf16[64,128,1,128]{3,1,2,0:T(8,128)(2,1)}, u32[]{:S(2)}) copy-start(bf16[64,128,1,128]{3,1,2,0:T(8,128)(2,1)} %param.22) | copy-start | bytes 6291460
  0.0 28.4 %copy-start.9 = (s32[512]{0:T(512)S(1)}, s32[512]{0:T(512)}, u32[]{:S(2)}) copy-start(s32[512]{0:T(512)} %param.19) | copy-start | bytes 6148
  0.0 29.9 %copy-start.7 = (s32[512]{0:T(512)S(1)}, s32[512]{0:T(512)}, u32[]{:S(2)}) copy-start(s32[512]{0:T(512)} %param.20) | copy-start | bytes 6148
  32.6 22.9 %copy-start.1 = (bf16[16,2048]{1,0:T(8,128)(2,1)S(1)}, bf16[16,2048]{1,0:T(8,128)(2,1)}, u32[]{:S(2)}) copy-start(bf16[16,2048]{1,0:T(8,128)(2,1)} %param.18) | copy-start | bytes 196612
  32.6 22.9 %copy-start.2 = (bf16[2048,128]{1,0:T(8,128)(2,1)S(1)}, bf16[2048,128]{1,0:T(8,128)(2,1)}, u32[]{:S(2)}) copy-start(bf16[2048,128]{1,0:T(8,128)(2,1)} %param.26) | copy-start | bytes 1572868
  32.7 22.9 %copy-start.4 = (f32[2048]{0:T(1024)S(1)}, f32[2048]{0:T(1024)}, u32[]{:S(2)}) copy-start(f32[2048]{0:T(1024)} %param.24) | copy-start | bytes 24580
  33.3 22.6 %copy-start.8 = (f32[128]{0:T(128)S(1)}, f32[128]{0:T(128)}, u32[]{:S(2)}) copy-start(f32[128]{0:T(128)} %param.31) | copy-start | bytes 1540
  54.6 4.2 %copy-start.3 = (bf16[32,16,256]{2,1,0:T(8,128)(2,1)S(1)}, bf16[32,16,256]{2,1,0:T(8,128)(2,1)}, u32[]{:S(2)}) copy-start(bf16[32,16,256]{2,1,0:T(8,128)(2,1)} %get-tuple-element.7) | copy-start | bytes 786436
  60.2 24.6 %copy-start.6 = (f32[2048]{0:T(1024)S(1)}, f32[2048]{0:T(1024)}, u32[]{:S(2)}) copy-start(f32[2048]{0:T(1024)} %param.32) | copy-start | bytes 24580
  86.6 11.7 %copy-start.5 = (bf16[16,256]{1,0:T(8,128)(2,1)S(1)}, bf16[16,256]{1,0:T(8,128)(2,1)}, u32[]{:S(2)}) copy-start(bf16[16,256]{1,0:T(8,128)(2,1)} %add_convert_fusion.1.refs_0_) | copy-start | bytes 24580

commit v3 on v2

--- a/solution.py
+++ b/solution.py
@@ -92,6 +92,96 @@
 
 def exchange(values, axis, count, spread, ident):
     return exchange_many((values,), (spread,), axis, count, ident)[0]
+
+
+def greet(peers):
+    barrier = pltpu.get_barrier_semaphore()
+    for axis, peer in peers:
+        pl.semaphore_signal(barrier, inc=1, device_id={axis: peer}, device_id_type=MESH_IDS)
+    pl.semaphore_wait(barrier, len(peers))
+
+
+def peers_of(axis, count):
+    me = lax.axis_index(axis)
+    return me, [(offset, lax.rem(me + offset, count)) for offset in range(1, count)]
+
+
+def send_all(axis, peers, src_of, dst, send_sems, recv_sems, phase):
+    copies = []
+    for offset, peer in peers:
+        copy = pltpu.make_async_remote_copy(
+            src_ref=src_of(peer),
+            dst_ref=dst,
+            send_sem=send_sems.at[phase, offset],
+            recv_sem=recv_sems.at[phase, offset],
+            device_id={axis: peer},
+            device_id_type=MESH_IDS,
+        )
+        copy.start()
+        copies.append(copy)
+    for copy in copies:
+        copy.wait()
+
+
+def residual_kernel(count, parts_ref, base_ref, out_ref, summed, send_sems, recv_sems):
+    me, peers = peers_of("head", count)
+    greet([("head", peer) for _, peer in peers])
+    summed[me] = parts_ref[me]
+    send_all("head", peers, lambda peer: parts_ref.at[peer], summed.at[me], send_sems, recv_sems, 0)
+    out_ref[me] = (base_ref[...] + jnp.sum(summed[...], axis=0)).astype(out_ref.dtype)
+    send_all("head", peers, lambda peer: out_ref.at[me], out_ref.at[me], send_sems, recv_sems, 1)
+
+
+def residual_exchange(parts, base, count, ident):
+    return pl.pallas_call(
+        functools.partial(residual_kernel, count),
+        out_shape=jax.ShapeDtypeStruct(parts.shape, jnp.bfloat16),
+        in_specs=[pl.BlockSpec(memory_space=pltpu.VMEM)] * 2,
+        out_specs=pl.BlockSpec(memory_space=pltpu.VMEM),
+        scratch_shapes=[
+            pltpu.VMEM(parts.shape, jnp.float32),
+            pltpu.SemaphoreType.DMA((2, count)),
+            pltpu.SemaphoreType.DMA((2, count)),
+        ],
+        compiler_params=pltpu.CompilerParams(collective_id=ident, has_side_effects=True),
+    )(parts, base)
+
+
+def tail_kernel(
+    head_count, req_count, parts_ref, base_ref, picker_ref, out_ref, summed, results, send_sems, recv_sems
+):
+    head_me, head_peers = peers_of("head", head_count)
+    req_me, req_peers = peers_of("req", req_count)
+    greet([("head", peer) for _, peer in head_peers] + [("req", peer) for _, peer in req_peers])
+    summed[head_me] = parts_ref[head_me]
+    send_all("head", head_peers, lambda peer: parts_ref.at[peer], summed.at[head_me], send_sems, recv_sems, 0)
+    results[req_me] = (base_ref[...].astype(jnp.float32) + jnp.sum(summed[...], axis=0)).astype(
+        results.dtype
+    )
+    send_all("req", req_peers, lambda peer: results.at[req_me], results.at[req_me], send_sems, recv_sems, 1)
+    rows, cols = base_ref.shape
+    out_ref[head_me] = jnp.dot(
+        picker_ref[...], results[...].reshape(req_count * rows, cols), preferred_element_type=jnp.float32
+    ).astype(out_ref.dtype)
+    send_all("head", head_peers, lambda peer: out_ref.at[head_me], out_ref.at[head_me], send_sems, recv_sems, 2)
+
+
+def tail_exchange(parts, base, picker, head_count, req_count, ident):
+    rows, cols = base.shape
+    most = max(head_count, req_count)
+    return pl.pallas_call(
+        functools.partial(tail_kernel, head_count, req_count),
+        out_shape=jax.ShapeDtypeStruct((head_count, rows, cols), jnp.bfloat16),
+        in_specs=[pl.BlockSpec(memory_space=pltpu.VMEM)] * 3,
+        out_specs=pl.BlockSpec(memory_space=pltpu.VMEM),
+        scratch_shapes=[
+            pltpu.VMEM(parts.shape, jnp.float32),
+            pltpu.VMEM((req_count, rows, cols), jnp.bfloat16),
+            pltpu.SemaphoreType.DMA((3, most)),
+            pltpu.SemaphoreType.DMA((3, most)),
+        ],
+        compiler_params=pltpu.CompilerParams(collective_id=ident, has_side_effects=True),
+    )(parts, base, picker)
 
 
 def body(
@@ -247,13 +337,9 @@
         projected = jnp.dot(attended, w_out, preferred_element_type=jnp.float32)
         projected = projected.reshape(local_rows, head_count, chunk).transpose(1, 0, 2)
 
-    attn_parts = exchange(projected, "head", head_count, True, 2)
-
-    with jax.named_scope("residual"):
-        hidden_chunk = lax.dynamic_slice_in_dim(hidden_f, head_index * chunk, chunk, axis=1)
-        mixed_chunk = (hidden_chunk + jnp.sum(attn_parts, axis=0)).astype(jnp.bfloat16)
-
-    mixed_all = exchange(mixed_chunk, "head", head_count, False, 3)
+    hidden_chunk = lax.dynamic_slice_in_dim(hidden_f, head_index * chunk, chunk, axis=1)
+    mixed_all = residual_exchange(projected, hidden_chunk, head_count, 2)
+    mixed_chunk = lax.dynamic_index_in_dim(mixed_all, head_index, axis=0, keepdims=False)
 
     with jax.named_scope("mlp"):
         mixed_rows = mixed_all.transpose(1, 0, 2).reshape(local_rows, model_width)
@@ -265,23 +351,11 @@
         down_part = jnp.dot(inner_act, mlp_down, preferred_element_type=jnp.float32)
         down_part = down_part.reshape(local_rows, head_count, chunk).transpose(1, 0, 2)
 
-    mlp_parts = exchange(down_part, "head", head_count, True, 4)
-
-    with jax.named_scope("result"):
-        result_chunk = (mixed_chunk.astype(jnp.float32) + jnp.sum(mlp_parts, axis=0)).astype(
-            jnp.bfloat16
-        )
-
-    result_all = exchange(result_chunk, "req", req_count, False, 5).reshape(all_rows, chunk)
-
     with jax.named_scope("reorder"):
         wanted = first_own + jnp.arange(local_rows, dtype=jnp.int32)
-        selector = (deal_order[None, :] == wanted[:, None]).astype(jnp.bfloat16)
-        picked = jnp.dot(selector, result_all, preferred_element_type=jnp.float32).astype(
-            jnp.bfloat16
-        )
-
-    output_parts = exchange(picked, "head", head_count, False, 6)
+        picker = (deal_order[None, :] == wanted[:, None]).astype(jnp.bfloat16)
+
+    output_parts = tail_exchange(down_part, mixed_chunk, picker, head_count, req_count, 3)
     return output_parts.transpose(1, 0, 2).reshape(local_rows, model_width)
 
 

time: 127 us -> 117 us (0.921)
  Pallas kernels: 83.3 us -> 75.7 us
  other arithmetic: 16.7 us -> 14.3 us
  local copies, waits for them, and re-layouts: 6.46 us -> 8.36 us
  matrix products: 19 us -> 17.3 us
    pallas_call x7 -> x2, Pallas kernels: 83.3 us -> 34.2 us  [exchange_many(): pl.pallas_call(functools.partial(exchange_kernel, axis, count, tuple(spre...]
    pallas_call x0 -> x2, Pallas kernels: none -> 41.4 us  [the longest x1 26.1 us: tail_exchange(): pl.pallas_call(functools.partial(tail_kernel, head_count, req_count), out...]
    reduce_sum x2 -> x0, other arithmetic: 1.84 us -> none  [the longest x1 0.92 us: body(): jnp.sum(attn_parts, axis=0)]
    dot_general x1 -> x0, matrix products: 1.74 us -> none  [body(): jnp.dot(selector, result_all, preferred_element_type=jnp.float32)]
    squeeze x0 -> x1, local copies, waits for them, and re-layouts: none -> 1.29 us  [body(): lax.dynamic_index_in_dim(mixed_all, head_index, axis=0, keepdims=False)]
where the time goes in v3:
time: 117 us; the launch traced here: 116 us
  Pallas kernels  75.7 us (65%)
  matrix products  17.3 us (15%)
  other arithmetic  14.3 us (12%)
  local copies, waits for them, and re-layouts  8.36 us (7%)
    pallas_call x2, Pallas kernels, exchange_many(): pl.pallas_call(functools.partial(exchange_kernel, axis, count, tuple(spre...  34.2 us
    pallas_call x1, Pallas kernels, tail_exchange(): pl.pallas_call(functools.partial(tail_kernel, head_count, req_count), out...  26.1 us
    pallas_call x1, Pallas kernels, residual_exchange(): pl.pallas_call(functools.partial(residual_kernel, count), out_shape=jax.S...  15.4 us
    dot_general x1, matrix products, body(): down_part = jnp.dot(inner_act, mlp_down, preferred_element_type=jnp.float32)  2.67 us

profile of v3, /device:TPU:1, one launch (start us, length us, event | category | flops | bytes accessed | tf_op | source)
XLA Modules:
  0.0 116.0 jit_solution(10016654192142343416)
XLA Ops:
  0.0 0.9 dynamic_slice.10
  1.9 1.0 multiply_reduce_fusion.1
  2.9 1.6 %fusion.67 = f32[16,256]{1,0:T(8,128)S(1)} fusion(bf16[2048,256]{1,0:T(8,128)(2,1)} %param.25, f32[2048]{0:T(1024)} %param.24, f32[16]{0:T(128)S(1)} %add_rsqrt_fusion.3, bf16[16,2048]{1,0:T(8,128)(2,1)} %param.18), kind=kOutput, calls=%fused_computation.128 | convolution fusion | flops 16908288 | bytes 1138752 | tf_op jit(solution)/shard_map/projections/dot_general | solution.py:229
  6.1 18.4 %shard_map.172 = bf16[32,16,256]{2,1,0:T(8,128)(2,1)} custom-call(bf16[16,256]{1,0:T(8,128)(2,1)} %bitcast.130), custom_call_target="tpu_custom_call" | custom-call | tf_op jit(solution)/shard_map/pallas_call | solution.py:80
  25.3 0.9 fusion.25
  26.2 2.2 %fusion = (pred[64]{0:T(512)(128)(4,1)S(1)}, pred[64,512]{1,0:T(8,128)(4,1)S(1)}) fusion(s32[512,64]{0,1:T(8,128)S(1)} %fusion.25), kind=kLoop, calls=%fused_computation.2 | loop fusion | flops 6258624 | bytes 163904 | tf_op jit(solution)/shard_map/page_owners/reduce_or | solution.py:261
  28.7 1.1 convolution_convert_fusion.1
  30.0 1.3 %select_reduce_fusion = s32[64]{0:T(128)S(1)} fusion(s32[512,64]{0,1:T(8,128)S(1)} %fusion.25), kind=kLoop, calls=%fused_computation | loop fusion | flops 6291392 | bytes 131328 | tf_op jit(solution)/shard_map/page_owners/reduce_sum | solution.py:258
  31.4 1.3 %fusion.68 = (f32[64,2]{1,0:T(8,128)S(1)}, f32[64,2,128]{2,1,0:T(2,128)S(1)}) fusion(bf16[64,2,128]{2,1,0:T(2,128)(2,1)S(1)} %reshape.457, bf16[64,128,1,128]{3,1,2,0:T(8,128)(2,1)S(1)} %copy-done, pred[64,128]{1,0:T(8,128)(4,1)S(1)} %iota_compare_fusion.5), kind=kOutput, calls=%fused_computation.129 | convolution fusion | flops 4243328 | bytes 2204160 | tf_op jit(solution)/shard_map/page_attention/pkgd,ptkd->pkgt/dot_general | solution.py:275
  33.5 1.0 fusion.29
  35.3 2.3 %fusion.2 = f32[64,2,128]{2,1,0:T(2,128)S(1)} fusion(bf16[64,128,1,128]{3,1,2,0:T(8,128)(2,1)} %param.23, f32[64,2,128]{2,1,0:T(2,128)S(1)} %get-tuple-element.24, pred[64,128]{1,0:T(8,128)(4,1)S(1)} %iota_compare_fusion.5, f32[64,2]{1,0:T(8,128)S(1)} %copy.62), kind=kOutput, calls=%fused_computation.4 | convolution fusion | flops 4243456 | bytes 2236928 | tf_op jit(solution)/shard_map/page_attention/pkgt,ptkd->pkgd/dot_general | solution.py:289
  37.6 1.1 convolution_convert_fusion
  38.8 15.8 %shard_map.173 = (bf16[32,16,256]{2,1,0:T(8,128)(2,1)}, f32[32,4,16]{2,1,0:T(4,128)}) custom-call(bf16[32,16,256]{2,1,0:T(8,128)(2,1)} %bitcast.117, f32[32,4,16]{2,1,0:T(4,128)} %maximum_bitcast_fusion.refs_1_), custom_call_target="tpu_custom_call" | custom-call | tf_op jit(solution)/shard_map/pallas_call | solution.py:80
  54.6 0.9 slice_reduce_fusion
  56.5 1.0 fusion.28
  59.0 1.3 %fusion.20 = f32[16,128]{1,0:T(8,128)S(1)} fusion(bf16[2048,128]{1,0:T(8,128)(2,1)} %param.27, f32[2048]{0:T(1024)S(1)} %copy-done.4, f32[16]{0:T(128)S(1)} %add_rsqrt_fusion.3, bf16[16,2048]{1,0:T(8,128)(2,1)S(1)} %copy-done.1), kind=kOutput, calls=%fused_computation.24 | convolution fusion | flops 8523776 | bytes 606272 | tf_op jit(solution)/shard_map/projections/dot_general | solution.py:238
  60.5 2.3 %fusion.19 = f32[16,2048]{1,0:T(8,128)S(1)} fusion(bf16[256,2048]{1,0:T(8,128)(2,1)} %param.29, bf16[2048,256]{1,0:T(8,128)(2,1)} %param.28, f32[2,8,2,128]{3,2,1,0:T(2,128)S(1)} %bitcast.127, f32[16,256]{1,0:T(8,128)S(1)} %multiply_reduce_fusion, f32[2,8,2,128]{3,2,1,0:T(2,128)S(1)} %bitcast.126, f32[2048]{0:T(1024)S(1)} %copy-done.4, ...), kind=kOutput, calls=%fused_computation.22 | convolution fusion | flops 33714176 | bytes 2351168 | tf_op jit(solution)/shard_map/combine/dot_general | solution.py:337
  64.1 15.4 %shard_map.174 = bf16[8,16,256]{2,1,0:T(8,128)(2,1)} custom-call(f32[8,16,256]{2,1,0:T(8,128)} %bitcast.122, f32[16,256]{1,0:T(8,128)} %constant_dynamic-slice_fusion.base_ref), custom_call_target="tpu_custom_call" | custom-call | tf_op jit(solution)/shard_map/pallas_call | solution.py:136
  80.4 1.0 fusion.22
  81.4 1.8 %fusion.65 = f32[16,384]{1,0:T(8,128)S(1)} fusion(bf16[2048,384]{1,0:T(8,128)(2,1)} %param.33, f32[16,2048]{1,0:T(8,128)S(1)} %bitcast.114, f32[2048]{0:T(1024)S(1)} %copy-done.5, f32[16]{0:T(128)S(1)} %add_rsqrt_fusion.1), kind=kOutput, calls=%fused_computation.126 | convolution fusion | flops 25264128 | bytes 1736768 | tf_op jit(solution)/shard_map/mlp/dot_general | solution.py:348
  83.1 2.7 %fusion.17 = f32[16,2048]{1,0:T(8,128)S(1)} fusion(bf16[384,2048]{1,0:T(8,128)(2,1)} %param.35, bf16[2048,384]{1,0:T(8,128)(2,1)} %param.34, f32[16,384]{1,0:T(8,128)S(1)} %fusion.65, f32[16,2048]{1,0:T(8,128)S(1)} %bitcast.115, f32[2048]{0:T(1024)S(1)} %copy-done.5, f32[16]{0:T(128)S(1)} %add_rsqrt_fusion.1), kind=kOutput, calls=%fused_computation.20 | convolution fusion | flops 50466816 | bytes 3440704 | tf_op jit(solution)/shard_map/mlp/dot_general | solution.py:351
  86.5 1.3 %dynamic-slice_bitcast_fusion.base_ref = bf16[16,256]{1,0:T(8,128)(2,1)} fusion(bf16[8,16,256]{2,1,0:T(8,128)(2,1)} %shard_map.174, s32[]{:T(128)S(6)} %select_n.84), kind=kLoop, calls=%fused_computation.87 | loop fusion | bytes 16388 | tf_op jit(solution)/shard_map/jit(dynamic_index_in_dim)/squeeze | solution.py:342
  88.4 26.1 %shard_map.175 = bf16[8,16,256]{2,1,0:T(8,128)(2,1)} custom-call(f32[8,16,256]{2,1,0:T(8,128)} %bitcast.121, bf16[16,256]{1,0:T(8,128)(2,1)} %dynamic-slice_bitcast_fusion.base_ref, bf16[16,512]{1,0:T(8,128)(2,1)} %compare_convert_fusion.picker_ref), custom_call_target="tpu_custom_call" | custom-call | tf_op jit(solution)/shard_map/pallas_call | solution.py:172
  114.5 1.5 %copy.80 = bf16[8,2,8,256]{3,2,0,1:T(8,128)(2,1)} copy(bf16[8,2,8,256]{3,2,1,0:T(8,128)(2,1)} %bitcast.123) | data formatting | bytes 131072 | tf_op jit(solution)/shard_map/reshape | solution.py:359
  (72 shorter events, 11.6 us)
Async XLA Ops:
  0.0 31.4 %copy-start = (bf16[64,128,1,128]{3,1,2,0:T(8,128)(2,1)S(1)}, bf16[64,128,1,128]{3,1,2,0:T(8,128)(2,1)}, u32[]{:S(2)}) copy-start(bf16[64,128,1,128]{3,1,2,0:T(8,128)(2,1)} %param.22) | copy-start | bytes 6291460
  0.0 28.4 %copy-start.7 = (s32[512]{0:T(512)S(1)}, s32[512]{0:T(512)}, u32[]{:S(2)}) copy-start(s32[512]{0:T(512)} %param.19) | copy-start | bytes 6148
  0.0 29.9 %copy-start.6 = (s32[512]{0:T(512)S(1)}, s32[512]{0:T(512)}, u32[]{:S(2)}) copy-start(s32[512]{0:T(512)} %param.20) | copy-start | bytes 6148
  32.6 22.9 %copy-start.1 = (bf16[16,2048]{1,0:T(8,128)(2,1)S(1)}, bf16[16,2048]{1,0:T(8,128)(2,1)}, u32[]{:S(2)}) copy-start(bf16[16,2048]{1,0:T(8,128)(2,1)} %param.18) | copy-start | bytes 196612
  32.6 22.9 %copy-start.2 = (bf16[2048,128]{1,0:T(8,128)(2,1)S(1)}, bf16[2048,128]{1,0:T(8,128)(2,1)}, u32[]{:S(2)}) copy-start(bf16[2048,128]{1,0:T(8,128)(2,1)} %param.26) | copy-start | bytes 1572868
  32.7 22.9 %copy-start.4 = (f32[2048]{0:T(1024)S(1)}, f32[2048]{0:T(1024)}, u32[]{:S(2)}) copy-start(f32[2048]{0:T(1024)} %param.24) | copy-start | bytes 24580
  33.3 22.6 %copy-start.8 = (f32[128]{0:T(128)S(1)}, f32[128]{0:T(128)}, u32[]{:S(2)}) copy-start(f32[128]{0:T(128)} %param.31) | copy-start | bytes 1540
  54.6 4.2 %copy-start.3 = (bf16[32,16,256]{2,1,0:T(8,128)(2,1)S(1)}, bf16[32,16,256]{2,1,0:T(8,128)(2,1)}, u32[]{:S(2)}) copy-start(bf16[32,16,256]{2,1,0:T(8,128)(2,1)} %get-tuple-element.7) | copy-start | bytes 786436
  59.0 22.4 %copy-start.5 = (f32[2048]{0:T(1024)S(1)}, f32[2048]{0:T(1024)}, u32[]{:S(2)}) copy-start(f32[2048]{0:T(1024)} %param.32) | copy-start | bytes 24580

commit v4 on v3

--- a/solution.py
+++ b/solution.py
@@ -123,6 +123,44 @@
         copy.wait()
 
 
+def two_level_peers(count, inner):
+    me = lax.axis_index("req")
+    outer_index, inner_index = me // inner, me % inner
+    near = [(k, outer_index * inner + lax.rem(inner_index + k, inner)) for k in range(1, inner)]
+    far = [(k, lax.rem(outer_index + k, count // inner) * inner + inner_index) for k in range(1, count // inner)]
+    return me, outer_index, near, far
+
+
+def two_level_gather(count, inner, me, outer_index, near, far, own_ref, out_ref, local_sem, send_sems, recv_sems, phase):
+    local = pltpu.make_async_copy(own_ref, out_ref.at[me], local_sem)
+    local.start()
+    send_all("req", near, lambda peer: own_ref, out_ref.at[me], send_sems, recv_sems, phase)
+    local.wait()
+    group = pl.ds(outer_index * inner, inner)
+    send_all("req", far, lambda peer: out_ref.at[group], out_ref.at[group], send_sems, recv_sems, phase + 1)
+
+
+def gather_kernel(count, inner, src_ref, out_ref, local_sem, send_sems, recv_sems):
+    me, outer_index, near, far = two_level_peers(count, inner)
+    greet([("req", peer) for _, peer in near + far])
+    two_level_gather(count, inner, me, outer_index, near, far, src_ref, out_ref, local_sem, send_sems, recv_sems, 0)
+
+
+def req_gather(values, count, inner, ident):
+    return pl.pallas_call(
+        functools.partial(gather_kernel, count, inner),
+        out_shape=jax.ShapeDtypeStruct((count,) + values.shape, values.dtype),
+        in_specs=[pl.BlockSpec(memory_space=pltpu.VMEM)],
+        out_specs=pl.BlockSpec(memory_space=pltpu.VMEM),
+        scratch_shapes=[
+            pltpu.SemaphoreType.DMA(()),
+            pltpu.SemaphoreType.DMA((2, count)),
+            pltpu.SemaphoreType.DMA((2, count)),
+        ],
+        compiler_params=pltpu.CompilerParams(collective_id=ident, has_side_effects=True),
+    )(values)
+
+
 def residual_kernel(count, parts_ref, base_ref, out_ref, summed, send_sems, recv_sems):
     me, peers = peers_of("head", count)
     greet([("head", peer) for _, peer in peers])
@@ -148,45 +186,58 @@
 
 
 def tail_kernel(
-    head_count, req_count, parts_ref, base_ref, picker_ref, out_ref, summed, results, send_sems, recv_sems
+    head_count, req_count, inner, parts_ref, base_ref, picker_ref, out_ref, summed, own, results, local_sem,
+    send_sems, recv_sems,
 ):
     head_me, head_peers = peers_of("head", head_count)
-    req_me, req_peers = peers_of("req", req_count)
-    greet([("head", peer) for _, peer in head_peers] + [("req", peer) for _, peer in req_peers])
+    req_me, outer_index, near, far = two_level_peers(req_count, inner)
+    greet([("head", peer) for _, peer in head_peers] + [("req", peer) for _, peer in near + far])
     summed[head_me] = parts_ref[head_me]
     send_all("head", head_peers, lambda peer: parts_ref.at[peer], summed.at[head_me], send_sems, recv_sems, 0)
-    results[req_me] = (base_ref[...].astype(jnp.float32) + jnp.sum(summed[...], axis=0)).astype(
-        results.dtype
+    own[...] = (base_ref[...].astype(jnp.float32) + jnp.sum(summed[...], axis=0)).astype(own.dtype)
+    two_level_gather(
+        req_count, inner, req_me, outer_index, near, far, own, results, local_sem, send_sems, recv_sems, 1
     )
-    send_all("req", req_peers, lambda peer: results.at[req_me], results.at[req_me], send_sems, recv_sems, 1)
     rows, cols = base_ref.shape
     out_ref[head_me] = jnp.dot(
         picker_ref[...], results[...].reshape(req_count * rows, cols), preferred_element_type=jnp.float32
     ).astype(out_ref.dtype)
-    send_all("head", head_peers, lambda peer: out_ref.at[head_me], out_ref.at[head_me], send_sems, recv_sems, 2)
-
-
-def tail_exchange(parts, base, picker, head_count, req_count, ident):
+    send_all("head", head_peers, lambda peer: out_ref.at[head_me], out_ref.at[head_me], send_sems, recv_sems, 3)
+
+
+def tail_exchange(parts, base, picker, head_count, req_count, inner, ident):
     rows, cols = base.shape
     most = max(head_count, req_count)
     return pl.pallas_call(
-        functools.partial(tail_kernel, head_count, req_count),
+        functools.partial(tail_kernel, head_count, req_count, inner),
         out_shape=jax.ShapeDtypeStruct((head_count, rows, cols), jnp.bfloat16),
         in_specs=[pl.BlockSpec(memory_space=pltpu.VMEM)] * 3,
         out_specs=pl.BlockSpec(memory_space=pltpu.VMEM),
         scratch_shapes=[
             pltpu.VMEM(parts.shape, jnp.float32),
+            pltpu.VMEM((rows, cols), jnp.bfloat16),
             pltpu.VMEM((req_count, rows, cols), jnp.bfloat16),
-            pltpu.SemaphoreType.DMA((3, most)),
-            pltpu.SemaphoreType.DMA((3, most)),
+            pltpu.SemaphoreType.DMA(()),
+            pltpu.SemaphoreType.DMA((4, most)),
+            pltpu.SemaphoreType.DMA((4, most)),
         ],
         compiler_params=pltpu.CompilerParams(collective_id=ident, has_side_effects=True),
     )(parts, base, picker)
 
 
+def req_groups(mesh):
+    try:
+        column = mesh.devices[:, 0]
+        inner = len({device.coords[1] for device in column})
+    except (AttributeError, IndexError, TypeError):
+        inner = 1
+    return inner if inner > 1 and mesh.shape["req"] % inner == 0 else 1
+
+
 def body(
     req_count,
     head_count,
+    inner,
     hidden,
     deal_order,
     lengths,
@@ -241,7 +292,7 @@
         )
         gate_logits = jnp.dot(normed, w_gate, preferred_element_type=jnp.float32)
 
-    all_queries = exchange(queries.reshape(local_rows, head_cols), "req", req_count, False, 0)
+    all_queries = req_gather(queries.reshape(local_rows, head_cols), req_count, inner, 0)
     all_queries = all_queries.reshape(all_rows, head_cols)
 
     with jax.named_scope("page_owners"):
@@ -355,13 +406,13 @@
         wanted = first_own + jnp.arange(local_rows, dtype=jnp.int32)
         picker = (deal_order[None, :] == wanted[:, None]).astype(jnp.bfloat16)
 
-    output_parts = tail_exchange(down_part, mixed_chunk, picker, head_count, req_count, 3)
+    output_parts = tail_exchange(down_part, mixed_chunk, picker, head_count, req_count, inner, 3)
     return output_parts.transpose(1, 0, 2).reshape(local_rows, model_width)
 
 
 def solution(mesh):
     return jax.shard_map(
-        functools.partial(body, mesh.shape["req"], mesh.shape["head"]),
+        functools.partial(body, mesh.shape["req"], mesh.shape["head"], req_groups(mesh)),
         mesh=mesh,
         in_specs=(
             P("req", None),

time: 117 us -> 119 us (1.017)
  Pallas kernels: 75.7 us -> 77.6 us
    pallas_call x1 -> x2, Pallas kernels: 26.1 us -> 47.1 us  [the longest x1 27.4 us: tail_exchange(): pl.pallas_call(functools.partial(tail_kernel, head_count, req_count, inne...]
    pallas_call x2 -> x1, Pallas kernels: 34.2 us -> 14.5 us  [exchange_many(): pl.pallas_call(functools.partial(exchange_kernel, axis, count, tuple(spre...]
where the time goes in v4:
time: 119 us; the launch traced here: 118 us
  Pallas kernels  77.6 us (65%)
  matrix products  17.3 us (15%)
  other arithmetic  14.3 us (12%)
  local copies, waits for them, and re-layouts  8.36 us (7%)
    pallas_call x1, Pallas kernels, tail_exchange(): pl.pallas_call(functools.partial(tail_kernel, head_count, req_count, inne...  27.4 us
    pallas_call x1, Pallas kernels, req_gather(): pl.pallas_call(functools.partial(gather_kernel, count, inner), out_shape=...  19.6 us
    pallas_call x1, Pallas kernels, residual_exchange(): pl.pallas_call(functools.partial(residual_kernel, count), out_shape=jax.S...  16.1 us
    pallas_call x1, Pallas kernels, exchange_many(): pl.pallas_call(functools.partial(exchange_kernel, axis, count, tuple(spre...  14.5 us
    dot_general x1, matrix products, body(): down_part = jnp.dot(inner_act, mlp_down, preferred_element_type=jnp.float32)  2.67 us

profile of v4, /device:TPU:1, one launch (start us, length us, event | category | flops | bytes accessed | tf_op | source)
XLA Modules:
  0.0 117.9 jit_solution(15234176727429528276)
XLA Ops:
  0.0 0.9 dynamic_slice.10
  1.9 1.0 multiply_reduce_fusion.1
  2.9 1.6 %fusion.67 = f32[16,256]{1,0:T(8,128)S(1)} fusion(bf16[2048,256]{1,0:T(8,128)(2,1)} %param.25, f32[2048]{0:T(1024)} %param.24, f32[16]{0:T(128)S(1)} %add_rsqrt_fusion.3, bf16[16,2048]{1,0:T(8,128)(2,1)} %param.18), kind=kOutput, calls=%fused_computation.128 | convolution fusion | flops 16908288 | bytes 1138752 | tf_op jit(solution)/shard_map/projections/dot_general | solution.py:280
  6.1 19.6 %shard_map.172 = bf16[32,16,256]{2,1,0:T(8,128)(2,1)} custom-call(bf16[16,256]{1,0:T(8,128)(2,1)} %bitcast.130), custom_call_target="tpu_custom_call" | custom-call | tf_op jit(solution)/shard_map/pallas_call | solution.py:150
  26.5 0.9 fusion.25
  27.4 2.2 %fusion = (pred[64]{0:T(512)(128)(4,1)S(1)}, pred[64,512]{1,0:T(8,128)(4,1)S(1)}) fusion(s32[512,64]{0,1:T(8,128)S(1)} %fusion.25), kind=kLoop, calls=%fused_computation.2 | loop fusion | flops 6258624 | bytes 163904 | tf_op jit(solution)/shard_map/page_owners/reduce_or | solution.py:312
  29.9 1.1 convolution_convert_fusion.1
  31.2 1.3 %select_reduce_fusion = s32[64]{0:T(128)S(1)} fusion(s32[512,64]{0,1:T(8,128)S(1)} %fusion.25), kind=kLoop, calls=%fused_computation | loop fusion | flops 6291392 | bytes 131328 | tf_op jit(solution)/shard_map/page_owners/reduce_sum | solution.py:309
  32.6 1.3 %fusion.68 = (f32[64,2]{1,0:T(8,128)S(1)}, f32[64,2,128]{2,1,0:T(2,128)S(1)}) fusion(bf16[64,2,128]{2,1,0:T(2,128)(2,1)S(1)} %reshape.457, bf16[64,128,1,128]{3,1,2,0:T(8,128)(2,1)S(1)} %copy-done, pred[64,128]{1,0:T(8,128)(4,1)S(1)} %iota_compare_fusion.5), kind=kOutput, calls=%fused_computation.129 | convolution fusion | flops 4243328 | bytes 2204160 | tf_op jit(solution)/shard_map/page_attention/pkgd,ptkd->pkgt/dot_general | solution.py:326
  34.7 1.0 fusion.29
  36.5 2.3 %fusion.2 = f32[64,2,128]{2,1,0:T(2,128)S(1)} fusion(bf16[64,128,1,128]{3,1,2,0:T(8,128)(2,1)} %param.23, f32[64,2,128]{2,1,0:T(2,128)S(1)} %get-tuple-element.24, pred[64,128]{1,0:T(8,128)(4,1)S(1)} %iota_compare_fusion.5, f32[64,2]{1,0:T(8,128)S(1)} %copy.62), kind=kOutput, calls=%fused_computation.4 | convolution fusion | flops 4243456 | bytes 2236928 | tf_op jit(solution)/shard_map/page_attention/pkgt,ptkd->pkgd/dot_general | solution.py:340
  38.8 1.1 convolution_convert_fusion
  39.9 14.5 %shard_map.173 = (bf16[32,16,256]{2,1,0:T(8,128)(2,1)}, f32[32,4,16]{2,1,0:T(4,128)}) custom-call(bf16[32,16,256]{2,1,0:T(8,128)(2,1)} %bitcast.117, f32[32,4,16]{2,1,0:T(4,128)} %maximum_bitcast_fusion.refs_1_), custom_call_target="tpu_custom_call" | custom-call | tf_op jit(solution)/shard_map/pallas_call | solution.py:80
  54.4 0.9 slice_reduce_fusion
  56.3 1.0 fusion.28
  58.8 1.3 %fusion.20 = f32[16,128]{1,0:T(8,128)S(1)} fusion(bf16[2048,128]{1,0:T(8,128)(2,1)} %param.27, f32[2048]{0:T(1024)S(1)} %copy-done.4, f32[16]{0:T(128)S(1)} %add_rsqrt_fusion.3, bf16[16,2048]{1,0:T(8,128)(2,1)S(1)} %copy-done.1), kind=kOutput, calls=%fused_computation.24 | convolution fusion | flops 8523776 | bytes 606272 | tf_op jit(solution)/shard_map/projections/dot_general | solution.py:289
  60.4 2.3 %fusion.19 = f32[16,2048]{1,0:T(8,128)S(1)} fusion(bf16[256,2048]{1,0:T(8,128)(2,1)} %param.29, bf16[2048,256]{1,0:T(8,128)(2,1)} %param.28, f32[2,8,2,128]{3,2,1,0:T(2,128)S(1)} %bitcast.127, f32[16,256]{1,0:T(8,128)S(1)} %multiply_reduce_fusion, f32[2,8,2,128]{3,2,1,0:T(2,128)S(1)} %bitcast.126, f32[2048]{0:T(1024)S(1)} %copy-done.4, ...), kind=kOutput, calls=%fused_computation.22 | convolution fusion | flops 33714176 | bytes 2351168 | tf_op jit(solution)/shard_map/combine/dot_general | solution.py:388
  64.0 16.1 %shard_map.174 = bf16[8,16,256]{2,1,0:T(8,128)(2,1)} custom-call(f32[8,16,256]{2,1,0:T(8,128)} %bitcast.122, f32[16,256]{1,0:T(8,128)} %constant_dynamic-slice_fusion.base_ref), custom_call_target="tpu_custom_call" | custom-call | tf_op jit(solution)/shard_map/pallas_call | solution.py:174
  80.9 1.0 fusion.22
  81.9 1.8 %fusion.65 = f32[16,384]{1,0:T(8,128)S(1)} fusion(bf16[2048,384]{1,0:T(8,128)(2,1)} %param.33, f32[16,2048]{1,0:T(8,128)S(1)} %bitcast.114, f32[2048]{0:T(1024)S(1)} %copy-done.5, f32[16]{0:T(128)S(1)} %add_rsqrt_fusion.1), kind=kOutput, calls=%fused_computation.126 | convolution fusion | flops 25264128 | bytes 1736768 | tf_op jit(solution)/shard_map/mlp/dot_general | solution.py:399
  83.7 2.7 %fusion.17 = f32[16,2048]{1,0:T(8,128)S(1)} fusion(bf16[384,2048]{1,0:T(8,128)(2,1)} %param.35, bf16[2048,384]{1,0:T(8,128)(2,1)} %param.34, f32[16,384]{1,0:T(8,128)S(1)} %fusion.65, f32[16,2048]{1,0:T(8,128)S(1)} %bitcast.115, f32[2048]{0:T(1024)S(1)} %copy-done.5, f32[16]{0:T(128)S(1)} %add_rsqrt_fusion.1), kind=kOutput, calls=%fused_computation.20 | convolution fusion | flops 50466816 | bytes 3440704 | tf_op jit(solution)/shard_map/mlp/dot_general | solution.py:402
  87.0 1.3 %dynamic-slice_bitcast_fusion.base_ref = bf16[16,256]{1,0:T(8,128)(2,1)} fusion(bf16[8,16,256]{2,1,0:T(8,128)(2,1)} %shard_map.174, s32[]{:T(128)S(6)} %select_n.84), kind=kLoop, calls=%fused_computation.87 | loop fusion | bytes 16388 | tf_op jit(solution)/shard_map/jit(dynamic_index_in_dim)/squeeze | solution.py:393
  89.0 27.4 %shard_map.175 = bf16[8,16,256]{2,1,0:T(8,128)(2,1)} custom-call(f32[8,16,256]{2,1,0:T(8,128)} %bitcast.121, bf16[16,256]{1,0:T(8,128)(2,1)} %dynamic-slice_bitcast_fusion.base_ref, bf16[16,512]{1,0:T(8,128)(2,1)} %compare_convert_fusion.picker_ref), custom_call_target="tpu_custom_call" | custom-call | tf_op jit(solution)/shard_map/pallas_call | solution.py:211
  116.5 1.5 %copy.80 = bf16[8,2,8,256]{3,2,0,1:T(8,128)(2,1)} copy(bf16[8,2,8,256]{3,2,1,0:T(8,128)(2,1)} %bitcast.123) | data formatting | bytes 131072 | tf_op jit(solution)/shard_map/reshape | solution.py:410
  (72 shorter events, 11.6 us)
Async XLA Ops:
  0.0 32.5 %copy-start = (bf16[64,128,1,128]{3,1,2,0:T(8,128)(2,1)S(1)}, bf16[64,128,1,128]{3,1,2,0:T(8,128)(2,1)}, u32[]{:S(2)}) copy-start(bf16[64,128,1,128]{3,1,2,0:T(8,128)(2,1)} %param.22) | copy-start | bytes 6291460
  0.0 29.6 %copy-start.7 = (s32[512]{0:T(512)S(1)}, s32[512]{0:T(512)}, u32[]{:S(2)}) copy-start(s32[512]{0:T(512)} %param.19) | copy-start | bytes 6148
  0.0 31.1 %copy-start.6 = (s32[512]{0:T(512)S(1)}, s32[512]{0:T(512)}, u32[]{:S(2)}) copy-start(s32[512]{0:T(512)} %param.20) | copy-start | bytes 6148
  33.8 21.5 %copy-start.1 = (bf16[16,2048]{1,0:T(8,128)(2,1)S(1)}, bf16[16,2048]{1,0:T(8,128)(2,1)}, u32[]{:S(2)}) copy-start(bf16[16,2048]{1,0:T(8,128)(2,1)} %param.18) | copy-start | bytes 196612
  33.8 21.5 %copy-start.2 = (bf16[2048,128]{1,0:T(8,128)(2,1)S(1)}, bf16[2048,128]{1,0:T(8,128)(2,1)}, u32[]{:S(2)}) copy-start(bf16[2048,128]{1,0:T(8,128)(2,1)} %param.26) | copy-start | bytes 1572868
  33.8 21.6 %copy-start.4 = (f32[2048]{0:T(1024)S(1)}, f32[2048]{0:T(1024)}, u32[]{:S(2)}) copy-start(f32[2048]{0:T(1024)} %param.24) | copy-start | bytes 24580
  34.5 21.3 %copy-start.8 = (f32[128]{0:T(128)S(1)}, f32[128]{0:T(128)}, u32[]{:S(2)}) copy-start(f32[128]{0:T(128)} %param.31) | copy-start | bytes 1540
  54.4 4.2 %copy-start.3 = (bf16[32,16,256]{2,1,0:T(8,128)(2,1)S(1)}, bf16[32,16,256]{2,1,0:T(8,128)(2,1)}, u32[]{:S(2)}) copy-start(bf16[32,16,256]{2,1,0:T(8,128)(2,1)} %get-tuple-element.7) | copy-start | bytes 786436
  58.8 23.1 %copy-start.5 = (f32[2048]{0:T(1024)S(1)}, f32[2048]{0:T(1024)}, u32[]{:S(2)}) copy-start(f32[2048]{0:T(1024)} %param.32) | copy-start | bytes 24580

commit v5 on v3

--- a/solution.py
+++ b/solution.py
@@ -123,65 +123,84 @@
         copy.wait()
 
 
-def residual_kernel(count, parts_ref, base_ref, out_ref, summed, send_sems, recv_sems):
+def residual_kernel(count, parts_ref, hidden_ref, out_ref, summed, send_sems, recv_sems):
     me, peers = peers_of("head", count)
+    cols = out_ref.shape[1] // count
+    mine = pl.ds(pl.multiple_of(me * cols, cols), cols)
     greet([("head", peer) for _, peer in peers])
-    summed[me] = parts_ref[me]
-    send_all("head", peers, lambda peer: parts_ref.at[peer], summed.at[me], send_sems, recv_sems, 0)
-    out_ref[me] = (base_ref[...] + jnp.sum(summed[...], axis=0)).astype(out_ref.dtype)
-    send_all("head", peers, lambda peer: out_ref.at[me], out_ref.at[me], send_sems, recv_sems, 1)
-
-
-def residual_exchange(parts, base, count, ident):
+    summed[me] = parts_ref[:, mine]
+    send_all(
+        "head", peers, lambda peer: parts_ref.at[:, pl.ds(peer * cols, cols)], summed.at[me], send_sems, recv_sems, 0
+    )
+    out_ref[:, mine] = (hidden_ref[:, mine].astype(jnp.float32) + jnp.sum(summed[...], axis=0)).astype(
+        out_ref.dtype
+    )
+    send_all("head", peers, lambda peer: out_ref.at[:, mine], out_ref.at[:, mine], send_sems, recv_sems, 1)
+
+
+def residual_exchange(parts, hidden, count, ident):
+    rows, width = parts.shape
     return pl.pallas_call(
         functools.partial(residual_kernel, count),
-        out_shape=jax.ShapeDtypeStruct(parts.shape, jnp.bfloat16),
+        out_shape=jax.ShapeDtypeStruct((rows, width), jnp.bfloat16),
         in_specs=[pl.BlockSpec(memory_space=pltpu.VMEM)] * 2,
         out_specs=pl.BlockSpec(memory_space=pltpu.VMEM),
         scratch_shapes=[
-            pltpu.VMEM(parts.shape, jnp.float32),
+            pltpu.VMEM((count, rows, width // count), jnp.float32),
             pltpu.SemaphoreType.DMA((2, count)),
             pltpu.SemaphoreType.DMA((2, count)),
         ],
         compiler_params=pltpu.CompilerParams(collective_id=ident, has_side_effects=True),
-    )(parts, base)
+    )(parts, hidden)
 
 
 def tail_kernel(
-    head_count, req_count, parts_ref, base_ref, picker_ref, out_ref, summed, results, send_sems, recv_sems
+    head_count, req_count, parts_ref, mixed_ref, order_ref, out_ref, summed, results, send_sems, recv_sems
 ):
     head_me, head_peers = peers_of("head", head_count)
     req_me, req_peers = peers_of("req", req_count)
+    rows, width = out_ref.shape
+    cols = width // head_count
+    mine = pl.ds(pl.multiple_of(head_me * cols, cols), cols)
     greet([("head", peer) for _, peer in head_peers] + [("req", peer) for _, peer in req_peers])
-    summed[head_me] = parts_ref[head_me]
-    send_all("head", head_peers, lambda peer: parts_ref.at[peer], summed.at[head_me], send_sems, recv_sems, 0)
-    results[req_me] = (base_ref[...].astype(jnp.float32) + jnp.sum(summed[...], axis=0)).astype(
+    summed[head_me] = parts_ref[:, mine]
+    send_all(
+        "head",
+        head_peers,
+        lambda peer: parts_ref.at[:, pl.ds(peer * cols, cols)],
+        summed.at[head_me],
+        send_sems,
+        recv_sems,
+        0,
+    )
+    results[req_me] = (mixed_ref[:, mine].astype(jnp.float32) + jnp.sum(summed[...], axis=0)).astype(
         results.dtype
     )
     send_all("req", req_peers, lambda peer: results.at[req_me], results.at[req_me], send_sems, recv_sems, 1)
-    rows, cols = base_ref.shape
-    out_ref[head_me] = jnp.dot(
-        picker_ref[...], results[...].reshape(req_count * rows, cols), preferred_element_type=jnp.float32
+    wanted = req_me * rows + lax.broadcasted_iota(jnp.int32, (rows, req_count * rows), 0)
+    picker = (order_ref[...] == wanted).astype(jnp.bfloat16)
+    out_ref[:, mine] = jnp.dot(
+        picker, results[...].reshape(req_count * rows, cols), preferred_element_type=jnp.float32
     ).astype(out_ref.dtype)
-    send_all("head", head_peers, lambda peer: out_ref.at[head_me], out_ref.at[head_me], send_sems, recv_sems, 2)
-
-
-def tail_exchange(parts, base, picker, head_count, req_count, ident):
-    rows, cols = base.shape
+    send_all("head", head_peers, lambda peer: out_ref.at[:, mine], out_ref.at[:, mine], send_sems, recv_sems, 2)
+
+
+def tail_exchange(parts, mixed, order, head_count, req_count, ident):
+    rows, width = parts.shape
     most = max(head_count, req_count)
     return pl.pallas_call(
         functools.partial(tail_kernel, head_count, req_count),
-        out_shape=jax.ShapeDtypeStruct((head_count, rows, cols), jnp.bfloat16),
+        out_shape=jax.ShapeDtypeStruct((rows, width), jnp.bfloat16),
         in_specs=[pl.BlockSpec(memory_space=pltpu.VMEM)] * 3,
         out_specs=pl.BlockSpec(memory_space=pltpu.VMEM),
         scratch_shapes=[
-            pltpu.VMEM(parts.shape, jnp.float32),
-            pltpu.VMEM((req_count, rows, cols), jnp.bfloat16),
+            pltpu.VMEM((head_count, rows, width // head_count), jnp.float32),
+            pltpu.VMEM((req_count, rows, width // head_count), jnp.bfloat16),
             pltpu.SemaphoreType.DMA((3, most)),
             pltpu.SemaphoreType.DMA((3, most)),
         ],
         compiler_params=pltpu.CompilerParams(collective_id=ident, has_side_effects=True),
-    )(parts, base, picker)
+    )(parts, mixed, order)
 
 
 def body(
@@ -335,28 +354,18 @@
         heads_out = (numerators / totals[..., None]).reshape(local_rows, head_cols)
         attended = (heads_out * jax.nn.sigmoid(gate_logits)).astype(jnp.bfloat16)
         projected = jnp.dot(attended, w_out, preferred_element_type=jnp.float32)
-        projected = projected.reshape(local_rows, head_count, chunk).transpose(1, 0, 2)
-
-    hidden_chunk = lax.dynamic_slice_in_dim(hidden_f, head_index * chunk, chunk, axis=1)
-    mixed_all = residual_exchange(projected, hidden_chunk, head_count, 2)
-    mixed_chunk = lax.dynamic_index_in_dim(mixed_all, head_index, axis=0, keepdims=False)
+
+    mixed_rows = residual_exchange(projected, hidden, head_count, 2)
 
     with jax.named_scope("mlp"):
-        mixed_rows = mixed_all.transpose(1, 0, 2).reshape(local_rows, model_width)
         mixed_f = mixed_rows.astype(jnp.float32)
         normed_two = (mixed_f * rms_inv(mixed_f) * mlp_gain).astype(jnp.bfloat16)
         gate_part = jnp.dot(normed_two, mlp_gate, preferred_element_type=jnp.float32)
         up_part = jnp.dot(normed_two, mlp_up, preferred_element_type=jnp.float32)
         inner_act = (jax.nn.silu(gate_part) * up_part).astype(jnp.bfloat16)
         down_part = jnp.dot(inner_act, mlp_down, preferred_element_type=jnp.float32)
-        down_part = down_part.reshape(local_rows, head_count, chunk).transpose(1, 0, 2)
-
-    with jax.named_scope("reorder"):
-        wanted = first_own + jnp.arange(local_rows, dtype=jnp.int32)
-        picker = (deal_order[None, :] == wanted[:, None]).astype(jnp.bfloat16)
-
-    output_parts = tail_exchange(down_part, mixed_chunk, picker, head_count, req_count, 3)
-    return output_parts.transpose(1, 0, 2).reshape(local_rows, model_width)
+
+    return tail_exchange(down_part, mixed_rows, deal_order.reshape(1, all_rows), head_count, req_count, 3)
 
 
 def solution(mesh):

time: 117 us -> 113 us (0.966)
  local copies, waits for them, and re-layouts: 8.36 us -> 5.13 us
  other arithmetic: 14.3 us -> 12.8 us
  matrix products: 17.3 us -> 18.7 us
    reshape x3 -> x0, local copies, waits for them, and re-layouts: 2.79 us -> none  [the longest x1 1.47 us: body(): return output_parts.transpose(1, 0, 2).reshape(local_rows, model_width)]
    unnamed x19 -> x20, local copies, waits for them, and re-layouts: 0.64 us -> 2.12 us
    squeeze x1 -> x0, local copies, waits for them, and re-layouts: 1.29 us -> none  [body(): lax.dynamic_index_in_dim(mixed_all, head_index, axis=0, keepdims=False)]
where the time goes in v5:
time: 113 us
  Pallas kernels  75.7 us (67%)
  matrix products  18.7 us (17%)
  other arithmetic  12.8 us (11%)
  local copies, waits for them, and re-layouts  5.13 us (5%)
    pallas_call x2, Pallas kernels, exchange_many(): pl.pallas_call(functools.partial(exchange_kernel, axis, count, tuple(spre...  34.2 us
    pallas_call x1, Pallas kernels, tail_exchange(): pl.pallas_call(functools.partial(tail_kernel, head_count, req_count), out...  26.1 us
    pallas_call x1, Pallas kernels, residual_exchange(): pl.pallas_call(functools.partial(residual_kernel, count), out_shape=jax.S...  15.4 us
    dot_general x1, matrix products, body(): down_part = jnp.dot(inner_act, mlp_down, preferred_element_type=jnp.float32)  3.34 us
    dot_general x1, matrix products, body(): projected = jnp.dot(attended, w_out, preferred_element_type=jnp.float32)  2.98 us
    dot_general x1, matrix products, body(): jnp.einsum('pkgt,ptkd->pkgd', weights.astype(jnp.bfloat16), value_cache,...  2.29 us

profile of v5, /device:TPU:1, one launch (start us, length us, event | category | flops | bytes accessed | tf_op | source)
XLA Modules:
  0.0 112.6 jit_solution(5770557640894789118)
XLA Ops:
  0.0 0.9 dynamic_slice.3
  0.9 0.9 select_reduce_fusion.4
  1.9 1.0 fusion.22
  2.9 1.6 %fusion.79 = f32[16,256]{1,0:T(8,128)S(1)} fusion(bf16[2048,256]{1,0:T(8,128)(2,1)} %param.25, bf16[16,2048]{1,0:T(8,128)(2,1)} %hidden_ref.1, f32[2048]{0:T(1024)} %param.24, f32[16]{0:T(128)S(1)} %add_rsqrt_fusion.3), kind=kOutput, calls=%fused_computation.126 | convolution fusion | flops 16908288 | bytes 1138752 | tf_op jit(solution)/shard_map/projections/dot_general | solution.py:248
  6.2 18.4 %shard_map.172 = bf16[32,16,256]{2,1,0:T(8,128)(2,1)} custom-call(bf16[16,256]{1,0:T(8,128)(2,1)} %bitcast.101), custom_call_target="tpu_custom_call" | custom-call | tf_op jit(solution)/shard_map/pallas_call | solution.py:80
  25.3 0.9 fusion.30
  26.2 2.2 %fusion = (pred[64]{0:T(512)(128)(4,1)S(1)}, pred[64,512]{1,0:T(8,128)(4,1)S(1)}) fusion(s32[512,64]{0,1:T(8,128)S(1)} %fusion.30), kind=kLoop, calls=%fused_computation.2 | loop fusion | flops 6258624 | bytes 163904 | tf_op jit(solution)/shard_map/page_owners/reduce_or | solution.py:280
  28.7 1.1 convolution_convert_fusion.1
  30.0 1.3 %select_reduce_fusion = s32[64]{0:T(128)S(1)} fusion(s32[512,64]{0,1:T(8,128)S(1)} %fusion.30), kind=kLoop, calls=%fused_computation | loop fusion | flops 6291392 | bytes 131328 | tf_op jit(solution)/shard_map/page_owners/reduce_sum | solution.py:277
  31.4 1.3 %fusion.81 = (f32[64,2]{1,0:T(8,128)S(1)}, f32[64,2,128]{2,1,0:T(2,128)S(1)}) fusion(bf16[64,2,128]{2,1,0:T(2,128)(2,1)S(1)} %reshape.442, bf16[64,128,1,128]{3,1,2,0:T(8,128)(2,1)S(1)} %copy-done, pred[64,128]{1,0:T(8,128)(4,1)S(1)} %iota_compare_fusion.5), kind=kOutput, calls=%fused_computation.127 | convolution fusion | flops 4243328 | bytes 2204160 | tf_op jit(solution)/shard_map/page_attention/pkgd,ptkd->pkgt/dot_general | solution.py:294
  33.5 1.0 fusion.34
  35.3 2.3 %fusion.2 = f32[64,2,128]{2,1,0:T(2,128)S(1)} fusion(bf16[64,128,1,128]{3,1,2,0:T(8,128)(2,1)} %param.23, f32[64,2,128]{2,1,0:T(2,128)S(1)} %get-tuple-element.24, pred[64,128]{1,0:T(8,128)(4,1)S(1)} %iota_compare_fusion.5, f32[64,2]{1,0:T(8,128)S(1)} %copy.50), kind=kOutput, calls=%fused_computation.4 | convolution fusion | flops 4243456 | bytes 2236928 | tf_op jit(solution)/shard_map/page_attention/pkgt,ptkd->pkgd/dot_general | solution.py:308
  37.6 1.1 %convolution_convert_fusion = bf16[512,256]{1,0:T(8,128)(2,1)} fusion(pred[64,512]{1,0:T(8,128)(4,1)S(1)} %convolution_compare_fusion, f32[8,8,2,128]{3,2,1,0:T(2,128)S(1)} %bitcast.100), kind=kOutput, calls=%fused_computation.8 | convolution fusion | flops 100794368 | bytes 360448 | tf_op jit(solution)/shard_map/page_attention/dot_general | solution.py:318
  38.8 15.8 %shard_map.173 = (bf16[32,16,256]{2,1,0:T(8,128)(2,1)}, f32[32,4,16]{2,1,0:T(4,128)}) custom-call(bf16[32,16,256]{2,1,0:T(8,128)(2,1)} %bitcast.93, f32[32,4,16]{2,1,0:T(4,128)} %maximum_bitcast_fusion.refs_1_), custom_call_target="tpu_custom_call" | custom-call | tf_op jit(solution)/shard_map/pallas_call | solution.py:80
  54.6 0.9 slice_reduce_fusion
  56.5 1.0 fusion.33
  59.0 1.3 %fusion.20 = f32[16,128]{1,0:T(8,128)S(1)} fusion(bf16[2048,128]{1,0:T(8,128)(2,1)} %param.27, bf16[16,2048]{1,0:T(8,128)(2,1)S(1)} %copy-done.1, f32[2048]{0:T(1024)S(1)} %copy-done.4, f32[16]{0:T(128)S(1)} %add_rsqrt_fusion.3), kind=kOutput, calls=%fused_computation.24 | convolution fusion | flops 8523776 | bytes 606272 | tf_op jit(solution)/shard_map/projections/dot_general | solution.py:257
  60.5 3.0 %fusion.19.parts_ref = f32[16,2048]{1,0:T(8,128)} fusion(bf16[256,2048]{1,0:T(8,128)(2,1)} %param.29, bf16[2048,256]{1,0:T(8,128)(2,1)} %param.28, f32[2,8,2,128]{3,2,1,0:T(2,128)S(1)} %bitcast.98, f32[16,256]{1,0:T(8,128)S(1)} %multiply_reduce_fusion, f32[2,8,2,128]{3,2,1,0:T(2,128)S(1)} %bitcast.97, bf16[16,2048]{1,0:T(8,128)(2,1)S(1)} %copy-done.1, ...), kind=kOutput, calls=%fused_computation.22 | convolution fusion | flops 33714176 | bytes 2351168 | tf_op jit(solution)/shard_map/combine/dot_general | solution.py:356
  63.5 15.4 %shard_map.174.mixed_ref = bf16[16,2048]{1,0:T(8,128)(2,1)} custom-call(f32[16,2048]{1,0:T(8,128)} %fusion.19.parts_ref, bf16[16,2048]{1,0:T(8,128)(2,1)} %hidden_ref.1), custom_call_target="tpu_custom_call" | custom-call | tf_op jit(solution)/shard_map/pallas_call | solution.py:143
  78.9 1.0 fusion.25
  79.9 1.8 %fusion.46 = f32[16,384]{1,0:T(8,128)S(1)} fusion(bf16[2048,384]{1,0:T(8,128)(2,1)} %param.33, bf16[16,2048]{1,0:T(8,128)(2,1)} %shard_map.174.mixed_ref, f32[2048]{0:T(1024)S(1)} %copy-done.5, f32[16]{0:T(128)S(1)} %add_rsqrt_fusion.1), kind=kOutput, calls=%fused_computation.72 | convolution fusion | flops 25296896 | bytes 1671232 | tf_op jit(solution)/shard_map/mlp/dot_general | solution.py:363
  81.7 3.3 %fusion.17.parts_ref = f32[16,2048]{1,0:T(8,128)} fusion(bf16[384,2048]{1,0:T(8,128)(2,1)} %param.35, bf16[2048,384]{1,0:T(8,128)(2,1)} %param.34, f32[16,384]{1,0:T(8,128)S(1)} %fusion.46, bf16[16,2048]{1,0:T(8,128)(2,1)} %shard_map.174.mixed_ref, f32[2048]{0:T(1024)S(1)} %copy-done.5, f32[16]{0:T(128)S(1)} %add_rsqrt_fusion.1), kind=kOutput, calls=%fused_computation.20 | convolution fusion | flops 50499584 | bytes 3375168 | tf_op jit(solution)/shard_map/mlp/dot_general | solution.py:366
  85.0 26.1 %shard_map.175 = bf16[16,2048]{1,0:T(8,128)(2,1)} custom-call(f32[16,2048]{1,0:T(8,128)} %fusion.17.parts_ref, bf16[16,2048]{1,0:T(8,128)(2,1)} %shard_map.174.mixed_ref, s32[1,512]{1,0:T(1,128)} %bitcast.105), custom_call_target="tpu_custom_call" | custom-call | tf_op jit(solution)/shard_map/pallas_call | solution.py:191
  111.1 1.5 %copy.82 = bf16[16,2048]{1,0:T(8,128)(2,1)} copy(bf16[16,2048]{1,0:T(8,128)(2,1)} %shard_map.175) | data formatting | bytes 131072
  (63 shorter events, 7.3 us)
Async XLA Ops:
  0.0 31.4 %copy-start = (bf16[64,128,1,128]{3,1,2,0:T(8,128)(2,1)S(1)}, bf16[64,128,1,128]{3,1,2,0:T(8,128)(2,1)}, u32[]{:S(2)}) copy-start(bf16[64,128,1,128]{3,1,2,0:T(8,128)(2,1)} %param.22) | copy-start | bytes 6291460
  0.0 28.4 %copy-start.7 = (s32[512]{0:T(512)S(1)}, s32[512]{0:T(512)}, u32[]{:S(2)}) copy-start(s32[512]{0:T(512)} %param.19) | copy-start | bytes 6148
  0.0 29.9 %copy-start.6 = (s32[512]{0:T(512)S(1)}, s32[512]{0:T(512)}, u32[]{:S(2)}) copy-start(s32[512]{0:T(512)} %param.20) | copy-start | bytes 6148
  32.7 22.9 %copy-start.1 = (bf16[16,2048]{1,0:T(8,128)(2,1)S(1)}, bf16[16,2048]{1,0:T(8,128)(2,1)}, u32[]{:S(2)}) copy-start(bf16[16,2048]{1,0:T(8,128)(2,1)} %hidden_ref.1) | copy-start | bytes 196612
  32.7 22.9 %copy-start.2 = (bf16[2048,128]{1,0:T(8,128)(2,1)S(1)}, bf16[2048,128]{1,0:T(8,128)(2,1)}, u32[]{:S(2)}) copy-start(bf16[2048,128]{1,0:T(8,128)(2,1)} %param.26) | copy-start | bytes 1572868
  32.7 22.9 %copy-start.4 = (f32[2048]{0:T(1024)S(1)}, f32[2048]{0:T(1024)}, u32[]{:S(2)}) copy-start(f32[2048]{0:T(1024)} %param.24) | copy-start | bytes 24580
  33.3 22.6 %copy-start.8 = (f32[128]{0:T(128)S(1)}, f32[128]{0:T(128)}, u32[]{:S(2)}) copy-start(f32[128]{0:T(128)} %param.31) | copy-start | bytes 1540
  54.6 4.2 %copy-start.3 = (bf16[32,16,256]{2,1,0:T(8,128)(2,1)S(1)}, bf16[32,16,256]{2,1,0:T(8,128)(2,1)}, u32[]{:S(2)}) copy-start(bf16[32,16,256]{2,1,0:T(8,128)(2,1)} %get-tuple-element.7) | copy-start | bytes 786436
  58.8 21.1 %copy-start.5 = (f32[2048]{0:T(1024)S(1)}, f32[2048]{0:T(1024)}, u32[]{:S(2)}) copy-start(f32[2048]{0:T(1024)} %param.32) | copy-start | bytes 24580

commit v6 on v5

--- a/solution.py
+++ b/solution.py
@@ -152,6 +152,103 @@
         ],
         compiler_params=pltpu.CompilerParams(collective_id=ident, has_side_effects=True),
     )(parts, hidden)
+
+
+def attend_kernel(
+    req_count, head_count, group_size, scale_factor, num_ref, stats_ref, query_ref, key_ref, value_ref, gate_ref,
+    w_out_ref, hidden_ref, out_ref, got_num, got_stats, projected, summed, send_sems, recv_sems,
+):
+    req_me, req_peers = peers_of("req", req_count)
+    head_me, head_peers = peers_of("head", head_count)
+    rows, width = out_ref.shape
+    cols = width // head_count
+    pairs = stats_ref.shape[1] // 2
+    head_width = query_ref.shape[1] // pairs
+    mine = pl.ds(pl.multiple_of(head_me * cols, cols), cols)
+    greet([("req", peer) for _, peer in req_peers] + [("head", peer) for _, peer in head_peers])
+    got_num[req_me] = num_ref[req_me]
+    got_stats[req_me] = stats_ref[req_me]
+    copies = []
+    for offset, peer in req_peers:
+        for which, (src_ref, dst_ref) in enumerate(((num_ref, got_num), (stats_ref, got_stats))):
+            copy = pltpu.make_async_remote_copy(
+                src_ref=src_ref.at[peer],
+                dst_ref=dst_ref.at[req_me],
+                send_sem=send_sems.at[which, offset],
+                recv_sem=recv_sems.at[which, offset],
+                device_id={"req": peer},
+                device_id_type=MESH_IDS,
+            )
+            copy.start()
+            copies.append(copy)
+    for copy in copies:
+        copy.wait()
+    eye = (
+        lax.broadcasted_iota(jnp.int32, (rows, rows), 0) == lax.broadcasted_iota(jnp.int32, (rows, rows), 1)
+    ).astype(jnp.float32)
+    flip = (((1,), (1,)), ((), ()))
+    heads = []
+    for pair in range(pairs):
+        kv = pair // group_size
+        lanes = slice(pair * head_width, (pair + 1) * head_width)
+        kv_lanes = slice(kv * head_width, (kv + 1) * head_width)
+        shifts = lax.dot_general(
+            eye, got_stats[:, pair, :], flip, precision=lax.Precision.HIGHEST, preferred_element_type=jnp.float32
+        )
+        totals = lax.dot_general(
+            eye,
+            got_stats[:, pairs + pair, :],
+            flip,
+            precision=lax.Precision.HIGHEST,
+            preferred_element_type=jnp.float32,
+        )
+        query = query_ref[:, lanes].astype(jnp.float32)
+        self_score = jnp.sum(query * key_ref[:, kv_lanes].astype(jnp.float32), axis=1, keepdims=True) * scale_factor
+        self_shift = LOG_TWO * jnp.ceil(self_score / LOG_TWO)
+        shift = jnp.maximum(jnp.max(shifts, axis=1, keepdims=True), self_shift)
+        factor = jnp.exp(shifts - shift)
+        self_weight = jnp.exp(self_score - shift)
+        total = jnp.sum(totals * factor, axis=1, keepdims=True) + self_weight
+        acc = self_weight.astype(jnp.bfloat16).astype(jnp.float32) * value_ref[:, kv_lanes].astype(jnp.float32)
+        for source in range(req_count):
+            acc = acc + factor[:, source : source + 1] * got_num[source, :, lanes].astype(jnp.float32)
+        heads.append(acc / total)
+    heads_out = jnp.concatenate(heads, axis=1)
+    gate = gate_ref[...]
+    attended = (heads_out * (1.0 / (1.0 + jnp.exp(-gate)))).astype(jnp.bfloat16)
+    projected[...] = jnp.dot(attended, w_out_ref[...], preferred_element_type=jnp.float32)
+    summed[head_me] = projected[:, mine]
+    send_all(
+        "head", head_peers, lambda peer: projected.at[:, pl.ds(peer * cols, cols)], summed.at[head_me],
+        send_sems, recv_sems, 2,
+    )
+    out_ref[:, mine] = (hidden_ref[:, mine].astype(jnp.float32) + jnp.sum(summed[...], axis=0)).astype(
+        out_ref.dtype
+    )
+    send_all("head", head_peers, lambda peer: out_ref.at[:, mine], out_ref.at[:, mine], send_sems, recv_sems, 3)
+
+
+def attend_exchange(
+    num, stats, queries, keys, values, gate, w_out, hidden, head_count, group_size, scale_factor, ident
+):
+    req_count = num.shape[0]
+    rows, width = hidden.shape
+    most = max(head_count, req_count)
+    return pl.pallas_call(
+        functools.partial(attend_kernel, req_count, head_count, group_size, scale_factor),
+        out_shape=jax.ShapeDtypeStruct((rows, width), jnp.bfloat16),
+        in_specs=[pl.BlockSpec(memory_space=pltpu.VMEM)] * 8,
+        out_specs=pl.BlockSpec(memory_space=pltpu.VMEM),
+        scratch_shapes=[
+            pltpu.VMEM(num.shape, num.dtype),
+            pltpu.VMEM(stats.shape, stats.dtype),
+            pltpu.VMEM((rows, width), jnp.float32),
+            pltpu.VMEM((head_count, rows, width // head_count), jnp.float32),
+            pltpu.SemaphoreType.DMA((4, most)),
+            pltpu.SemaphoreType.DMA((4, most)),
+        ],
+        compiler_params=pltpu.CompilerParams(collective_id=ident, has_side_effects=True),
+    )(num, stats, queries, keys, values, gate, w_out, hidden)
 
 
 def tail_kernel(
@@ -326,36 +423,20 @@
             axis=2,
         ).transpose(0, 2, 1)
 
-    got_numerators, got_stats = exchange_many(
-        (numerator_message, stats_message), (True, True), "req", req_count, 1
-    )
-
-    with jax.named_scope("combine"):
-        got_numerators = got_numerators.astype(jnp.float32).reshape(
-            req_count, local_rows, local_kv, group_size, head_width
-        )
-        got_stats = got_stats.transpose(0, 2, 1)
-        got_shift = got_stats[:, :, :pairs].reshape(req_count, local_rows, local_kv, group_size)
-        got_totals = got_stats[:, :, pairs:].reshape(req_count, local_rows, local_kv, group_size)
-        self_scores = (
-            jnp.einsum("rkgd,rkd->rkg", queries, new_keys, preferred_element_type=jnp.float32)
-            * scale_factor
-        )
-        self_shift = LOG_TWO * jnp.ceil(self_scores / LOG_TWO)
-        shift = jnp.maximum(jnp.max(got_shift, axis=0), self_shift)
-        factor = jnp.exp(got_shift - shift[None])
-        self_weight = jnp.exp(self_scores - shift)
-        totals = jnp.sum(got_totals * factor, axis=0) + self_weight
-        self_rounded = self_weight.astype(jnp.bfloat16).astype(jnp.float32)
-        numerators = (
-            jnp.sum(got_numerators * factor[..., None], axis=0)
-            + self_rounded[..., None] * new_values.astype(jnp.float32)[:, :, None, :]
-        )
-        heads_out = (numerators / totals[..., None]).reshape(local_rows, head_cols)
-        attended = (heads_out * jax.nn.sigmoid(gate_logits)).astype(jnp.bfloat16)
-        projected = jnp.dot(attended, w_out, preferred_element_type=jnp.float32)
-
-    mixed_rows = residual_exchange(projected, hidden, head_count, 2)
+    mixed_rows = attend_exchange(
+        numerator_message,
+        stats_message,
+        queries.reshape(local_rows, head_cols),
+        new_keys.reshape(local_rows, local_kv * head_width),
+        new_values.reshape(local_rows, local_kv * head_width),
+        gate_logits,
+        w_out,
+        hidden,
+        head_count,
+        group_size,
+        scale_factor,
+        1,
+    )
 
     with jax.named_scope("mlp"):
         mixed_f = mixed_rows.astype(jnp.float32)

time: 113 us -> 107 us (0.947)
  other arithmetic: 12.8 us -> 10.5 us
  Pallas kernels: 75.7 us -> 73.8 us
  local copies, waits for them, and re-layouts: 5.13 us -> 3.52 us
    pallas_call x2 -> x1, Pallas kernels: 34.2 us -> 18.4 us  [exchange_many(): pl.pallas_call(functools.partial(exchange_kernel, axis, count, tuple(spre...]
    pallas_call x1, Pallas kernels: 15.4 us -> 30.9 us  [attend_exchange(): pl.pallas_call(functools.partial(attend_kernel, req_count, head_count, gr...]
    pallas_call x1, Pallas kernels: 26.1 us -> 24.5 us  [tail_exchange(): pl.pallas_call(functools.partial(tail_kernel, head_count, req_count), out...]
    dot_general x1, matrix products: 1.57 us -> 0.29 us  [body(): jnp.dot(normed, w_query, preferred_element_type=jnp.float32)]
    dot_general x2 -> x1, matrix products: 3.18 us -> 2.17 us  [body(): gate_logits = jnp.dot(normed, w_gate, preferred_element_type=jnp.float32)]
where the time goes in v6:
time: 107 us; the launch traced here: 106 us
  Pallas kernels  73.8 us (69%)
  matrix products  18.1 us (17%)
  other arithmetic  10.5 us (10%)
  local copies, waits for them, and re-layouts  3.52 us (3%)
    pallas_call x1, Pallas kernels, attend_exchange(): pl.pallas_call(functools.partial(attend_kernel, req_count, head_count, gr...  30.9 us
    pallas_call x1, Pallas kernels, tail_exchange(): pl.pallas_call(functools.partial(tail_kernel, head_count, req_count), out...  24.5 us
    pallas_call x1, Pallas kernels, exchange_many(): pl.pallas_call(functools.partial(exchange_kernel, axis, count, tuple(spre...  18.4 us
    dot_general x1, matrix products, body(): down_part = jnp.dot(inner_act, mlp_down, preferred_element_type=jnp.float32)  3.34 us
    dot_general x1, matrix products, body(): jnp.einsum('pkgt,ptkd->pkgd', weights.astype(jnp.bfloat16), value_cache,...  2.33 us
    reduce_or x1, other arithmetic, body(): filled = jnp.where(jnp.any(owned_requests, axis=1), filled, 0)  2.23 us
    dot_general x1, matrix products, body(): gate_logits = jnp.dot(normed, w_gate, preferred_element_type=jnp.float32)  2.17 us

profile of v6, /device:TPU:1, one launch (start us, length us, event | category | flops | bytes accessed | tf_op | source)
XLA Modules:
  0.0 106.2 jit_solution(484279519017061950)
XLA Ops:
  0.0 0.9 dynamic_slice.3
  1.0 0.9 select_reduce_fusion.4
  1.9 1.0 fusion.15
  2.9 0.7 add_select_fusion
  3.6 1.9 %convolution_convert_fusion.2.value_ref = bf16[16,128]{1,0:T(8,128)(2,1)} fusion(bf16[2048,128]{1,0:T(8,128)(2,1)} %param.27, bf16[16,2048]{1,0:T(8,128)(2,1)} %hidden_ref.1, f32[2048]{0:T(1024)} %param.24, f32[16]{0:T(128)S(1)} %add_rsqrt_fusion.3), kind=kOutput, calls=%fused_computation.16 | convolution fusion | flops 8521728 | bytes 602176 | tf_op jit(solution)/shard_map/projections/dot_general | solution.py:354
  5.6 1.4 %multiply_reduce_fusion.1 = (f32[16]{0:T(128)S(1)}, f32[16,128]{1,0:T(8,128)S(1)}) fusion(bf16[2048,128]{1,0:T(8,128)(2,1)} %param.26, bf16[16,2048]{1,0:T(8,128)(2,1)} %hidden_ref.1, f32[2048]{0:T(1024)} %param.24, f32[16]{0:T(128)S(1)} %add_rsqrt_fusion.3), kind=kOutput, calls=%fused_computation.72 | convolution fusion | flops 8523760 | bytes 606336 | tf_op jit(solution)/shard_map/projections/dot_general | solution.py:349
  7.0 0.7 multiply_bitcast_fusion
  7.9 0.7 pad_maximum_fusion.1.key_ref
  8.7 2.2 %fusion.53.gate_ref = f32[16,256]{1,0:T(8,128)} fusion(bf16[2048,256]{1,0:T(8,128)(2,1)} %param.28, bf16[16,2048]{1,0:T(8,128)(2,1)} %hidden_ref.1, f32[2048]{0:T(1024)} %param.24, f32[16]{0:T(128)S(1)} %add_rsqrt_fusion.3), kind=kOutput, calls=%fused_computation.92 | convolution fusion | flops 16908288 | bytes 1138752 | tf_op jit(solution)/shard_map/projections/dot_general | solution.py:358
  12.2 1.3 %select_reduce_fusion = s32[64]{0:T(128)S(1)} fusion(s32[512,64]{0,1:T(8,128)S(1)} %fusion.23), kind=kLoop, calls=%fused_computation | loop fusion | flops 6291392 | bytes 131328 | tf_op jit(solution)/shard_map/page_owners/reduce_sum | solution.py:374
  13.5 2.2 %fusion = (pred[64]{0:T(512)(128)(4,1)S(1)}, pred[64,512]{1,0:T(8,128)(4,1)S(1)}) fusion(s32[512,64]{0,1:T(8,128)S(1)} %fusion.23), kind=kLoop, calls=%fused_computation.2 | loop fusion | flops 6258624 | bytes 163904 | tf_op jit(solution)/shard_map/page_owners/reduce_or | solution.py:377
  16.4 18.4 %shard_map.172 = bf16[32,16,256]{2,1,0:T(8,128)(2,1)} custom-call(bf16[16,256]{1,0:T(8,128)(2,1)} %bitcast.56), custom_call_target="tpu_custom_call" | custom-call | tf_op jit(solution)/shard_map/pallas_call | solution.py:80
  34.8 1.1 %convolution_convert_fusion.1 = bf16[64,256]{1,0:T(8,128)(2,1)S(1)} fusion(pred[64,512]{1,0:T(8,128)(4,1)S(1)} %convolution_compare_fusion, bf16[512,256]{1,0:T(8,128)(2,1)} %bitcast.53), kind=kOutput, calls=%fused_computation.12 | convolution fusion | flops 16793600 | bytes 327680 | tf_op jit(solution)/shard_map/page_owners/dot_general | solution.py:384
  36.0 1.3 %fusion.60 = (f32[64,2]{1,0:T(8,128)S(1)}, f32[64,2,128]{2,1,0:T(2,128)S(1)}) fusion(bf16[64,2,128]{2,1,0:T(2,128)(2,1)S(1)} %reshape.377, bf16[64,128,1,128]{3,1,2,0:T(8,128)(2,1)S(1)} %copy-done, pred[64,128]{1,0:T(8,128)(4,1)S(1)} %iota_compare_fusion.5), kind=kOutput, calls=%fused_computation.95 | convolution fusion | flops 4243328 | bytes 2204160 | tf_op jit(solution)/shard_map/page_attention/pkgd,ptkd->pkgt/dot_general | solution.py:391
  38.0 1.0 fusion.26
  39.1 2.3 %fusion.2 = f32[64,2,128]{2,1,0:T(2,128)S(1)} fusion(bf16[64,128,1,128]{3,1,2,0:T(8,128)(2,1)} %param.23, f32[64,2,128]{2,1,0:T(2,128)S(1)} %get-tuple-element.14, pred[64,128]{1,0:T(8,128)(4,1)S(1)} %iota_compare_fusion.5, f32[64,2]{1,0:T(8,128)S(1)} %copy.38), kind=kOutput, calls=%fused_computation.4 | convolution fusion | flops 4243456 | bytes 2236928 | tf_op jit(solution)/shard_map/page_attention/pkgt,ptkd->pkgd/dot_general | solution.py:405
  41.4 0.7 maximum_bitcast_fusion.stats_ref
  42.1 1.1 %convolution_convert_fusion = bf16[512,256]{1,0:T(8,128)(2,1)} fusion(pred[64,512]{1,0:T(8,128)(4,1)S(1)} %convolution_compare_fusion, f32[8,8,2,128]{3,2,1,0:T(2,128)S(1)} %bitcast.59), kind=kOutput, calls=%fused_computation.8 | convolution fusion | flops 100794368 | bytes 360448 | tf_op jit(solution)/shard_map/page_attention/dot_general | solution.py:415
  43.2 30.9 %shard_map.173.mixed_ref = bf16[16,2048]{1,0:T(8,128)(2,1)} custom-call(bf16[32,16,256]{2,1,0:T(8,128)(2,1)} %bitcast.54, f32[32,4,16]{2,1,0:T(4,128)} %maximum_bitcast_fusion.stats_ref, bf16[16,256]{1,0:T(8,128)(2,1)} %bitcast.57, bf16[16,128]{1,0:T(8,128)(2,1)} %pad_maximum_fusion.1.key_ref, bf16[16,128]{1,0:T(8,128)(2,1)} %convolution_convert_fusion.2.value_ref, ...), custom_call_target="tpu_custom_call" | custom-call | tf_op jit(solution)/shard_map/pallas_call | solution.py:237
  74.1 1.0 fusion.18
  75.1 1.8 %fusion.36 = f32[16,384]{1,0:T(8,128)S(1)} fusion(bf16[2048,384]{1,0:T(8,128)(2,1)} %param.33, bf16[16,2048]{1,0:T(8,128)(2,1)} %shard_map.173.mixed_ref, f32[2048]{0:T(1024)S(1)} %copy-done.5, f32[16]{0:T(128)S(1)} %add_rsqrt_fusion.1), kind=kOutput, calls=%fused_computation.55 | convolution fusion | flops 25296896 | bytes 1671232 | tf_op jit(solution)/shard_map/mlp/dot_general | solution.py:444
  76.9 3.3 %fusion.13.parts_ref = f32[16,2048]{1,0:T(8,128)} fusion(bf16[384,2048]{1,0:T(8,128)(2,1)} %param.35, bf16[2048,384]{1,0:T(8,128)(2,1)} %param.34, f32[16,384]{1,0:T(8,128)S(1)} %fusion.36, bf16[16,2048]{1,0:T(8,128)(2,1)} %shard_map.173.mixed_ref, f32[2048]{0:T(1024)S(1)} %copy-done.5, f32[16]{0:T(128)S(1)} %add_rsqrt_fusion.1), kind=kOutput, calls=%fused_computation.15 | convolution fusion | flops 50499584 | bytes 3375168 | tf_op jit(solution)/shard_map/mlp/dot_general | solution.py:447
  80.2 24.5 %shard_map.174 = bf16[16,2048]{1,0:T(8,128)(2,1)} custom-call(f32[16,2048]{1,0:T(8,128)} %fusion.13.parts_ref, bf16[16,2048]{1,0:T(8,128)(2,1)} %shard_map.173.mixed_ref, s32[1,512]{1,0:T(1,128)} %bitcast.61), custom_call_target="tpu_custom_call" | custom-call | tf_op jit(solution)/shard_map/pallas_call | solution.py:288
  104.7 1.5 %copy.53 = bf16[16,2048]{1,0:T(8,128)(2,1)} copy(bf16[16,2048]{1,0:T(8,128)(2,1)} %shard_map.174) | data formatting | bytes 131072
  (48 shorter events, 3.0 us)
Async XLA Ops:
  0.0 36.0 %copy-start = (bf16[64,128,1,128]{3,1,2,0:T(8,128)(2,1)S(1)}, bf16[64,128,1,128]{3,1,2,0:T(8,128)(2,1)}, u32[]{:S(2)}) copy-start(bf16[64,128,1,128]{3,1,2,0:T(8,128)(2,1)} %param.22) | copy-start | bytes 6291460
  0.0 10.8 %copy-start.1 = (bf16[16,2048]{1,0:T(8,128)(2,1)S(1)}, bf16[16,2048]{1,0:T(8,128)(2,1)}, u32[]{:S(2)}) copy-start(bf16[16,2048]{1,0:T(8,128)(2,1)} %hidden_ref.1) | copy-start | bytes 196612
  0.0 10.8 %copy-start.3 = (f32[2048]{0:T(1024)S(1)}, f32[2048]{0:T(1024)}, u32[]{:S(2)}) copy-start(f32[2048]{0:T(1024)} %param.24) | copy-start | bytes 24580
  0.0 11.2 %copy-start.8 = (f32[128]{0:T(128)S(1)}, f32[128]{0:T(128)}, u32[]{:S(2)}) copy-start(f32[128]{0:T(128)} %param.30) | copy-start | bytes 1540
  0.0 10.8 %copy-start.2 = (bf16[2048,256]{1,0:T(8,128)(2,1)S(1)}, bf16[2048,256]{1,0:T(8,128)(2,1)}, u32[]{:S(2)}) copy-start(bf16[2048,256]{1,0:T(8,128)(2,1)} %param.25) | copy-start | bytes 3145732
  0.0 12.1 %copy-start.4 = (s32[512,64]{0,1:T(8,128)S(1)}, s32[512,64]{0,1:T(8,128)}, u32[]{:S(2)}) copy-start(s32[512,64]{0,1:T(8,128)} %param.21) | copy-start | bytes 393220
  3.6 12.1 %copy-start.6 = (s32[512]{0:T(512)S(1)}, s32[512]{0:T(512)}, u32[]{:S(2)}) copy-start(s32[512]{0:T(512)} %param.20) | copy-start | bytes 6148
  3.6 12.2 %copy-start.7 = (s32[512]{0:T(512)S(1)}, s32[512]{0:T(512)}, u32[]{:S(2)}) copy-start(s32[512]{0:T(512)} %param.19) | copy-start | bytes 6148
  39.1 36.0 %copy-start.5 = (f32[2048]{0:T(1024)S(1)}, f32[2048]{0:T(1024)}, u32[]{:S(2)}) copy-start(f32[2048]{0:T(1024)} %param.32) | copy-start | bytes 24580

commit v7 on v6

--- a/solution.py
+++ b/solution.py
@@ -152,6 +152,45 @@
         ],
         compiler_params=pltpu.CompilerParams(collective_id=ident, has_side_effects=True),
     )(parts, hidden)
+
+
+def query_kernel(count, query_ref, normed_ref, w_gate_ref, w_value_ref, out_ref, gate_ref, value_ref, send_sems, recv_sems):
+    me, peers = peers_of("req", count)
+    greet([("req", peer) for _, peer in peers])
+    copies = []
+    for offset, peer in peers:
+        copy = pltpu.make_async_remote_copy(
+            src_ref=query_ref,
+            dst_ref=out_ref.at[me],
+            send_sem=send_sems.at[offset],
+            recv_sem=recv_sems.at[offset],
+            device_id={"req": peer},
+            device_id_type=MESH_IDS,
+        )
+        copy.start()
+        copies.append(copy)
+    out_ref[me] = query_ref[...]
+    normed = normed_ref[...]
+    gate_ref[...] = jnp.dot(normed, w_gate_ref[...], preferred_element_type=jnp.float32)
+    value_ref[...] = jnp.dot(normed, w_value_ref[...], preferred_element_type=jnp.float32).astype(value_ref.dtype)
+    for copy in copies:
+        copy.wait()
+
+
+def query_exchange(queries, normed, w_gate, w_value, count, ident):
+    rows = queries.shape[0]
+    return pl.pallas_call(
+        functools.partial(query_kernel, count),
+        out_shape=(
+            jax.ShapeDtypeStruct((count,) + queries.shape, queries.dtype),
+            jax.ShapeDtypeStruct((rows, w_gate.shape[1]), jnp.float32),
+            jax.ShapeDtypeStruct((rows, w_value.shape[1]), jnp.bfloat16),
+        ),
+        in_specs=[pl.BlockSpec(memory_space=pltpu.VMEM)] * 4,
+        out_specs=tuple(pl.BlockSpec(memory_space=pltpu.VMEM) for _ in range(3)),
+        scratch_shapes=[pltpu.SemaphoreType.DMA((count,)), pltpu.SemaphoreType.DMA((count,))],
+        compiler_params=pltpu.CompilerParams(collective_id=ident, has_side_effects=True),
+    )(queries, normed, w_gate, w_value)
 
 
 def attend_kernel(
@@ -252,14 +291,25 @@
 
 
 def tail_kernel(
-    head_count, req_count, parts_ref, mixed_ref, order_ref, out_ref, summed, results, send_sems, recv_sems
+    head_count, req_count, mixed_ref, gain_ref, w_gate_ref, w_up_ref, w_down_ref, order_ref, out_ref, parts_ref,
+    summed, results, send_sems, recv_sems,
 ):
     head_me, head_peers = peers_of("head", head_count)
     req_me, req_peers = peers_of("req", req_count)
     rows, width = out_ref.shape
     cols = width // head_count
     mine = pl.ds(pl.multiple_of(head_me * cols, cols), cols)
-    greet([("head", peer) for _, peer in head_peers] + [("req", peer) for _, peer in req_peers])
+    barrier = pltpu.get_barrier_semaphore()
+    everyone = [("head", peer) for _, peer in head_peers] + [("req", peer) for _, peer in req_peers]
+    for axis, peer in everyone:
+        pl.semaphore_signal(barrier, inc=1, device_id={axis: peer}, device_id_type=MESH_IDS)
+    mixed = mixed_ref[...].astype(jnp.float32)
+    normed = (mixed * rms_inv(mixed) * gain_ref[...]).astype(jnp.bfloat16)
+    gate_part = jnp.dot(normed, w_gate_ref[...], preferred_element_type=jnp.float32)
+    up_part = jnp.dot(normed, w_up_ref[...], preferred_element_type=jnp.float32)
+    inner_act = (gate_part / (1.0 + jnp.exp(-gate_part)) * up_part).astype(jnp.bfloat16)
+    parts_ref[...] = jnp.dot(inner_act, w_down_ref[...], preferred_element_type=jnp.float32)
+    pl.semaphore_wait(barrier, len(everyone))
     summed[head_me] = parts_ref[:, mine]
     send_all(
         "head",
@@ -282,22 +332,23 @@
     send_all("head", head_peers, lambda peer: out_ref.at[:, mine], out_ref.at[:, mine], send_sems, recv_sems, 2)
 
 
-def tail_exchange(parts, mixed, order, head_count, req_count, ident):
-    rows, width = parts.shape
+def tail_exchange(mixed, gain, w_gate, w_up, w_down, order, head_count, req_count, ident):
+    rows, width = mixed.shape
     most = max(head_count, req_count)
     return pl.pallas_call(
         functools.partial(tail_kernel, head_count, req_count),
         out_shape=jax.ShapeDtypeStruct((rows, width), jnp.bfloat16),
-        in_specs=[pl.BlockSpec(memory_space=pltpu.VMEM)] * 3,
+        in_specs=[pl.BlockSpec(memory_space=pltpu.VMEM)] * 6,
         out_specs=pl.BlockSpec(memory_space=pltpu.VMEM),
         scratch_shapes=[
+            pltpu.VMEM((rows, width), jnp.float32),
             pltpu.VMEM((head_count, rows, width // head_count), jnp.float32),
             pltpu.VMEM((req_count, rows, width // head_count), jnp.bfloat16),
             pltpu.SemaphoreType.DMA((3, most)),
             pltpu.SemaphoreType.DMA((3, most)),
         ],
         compiler_params=pltpu.CompilerParams(collective_id=ident, has_side_effects=True),
-    )(parts, mixed, order)
+    )(mixed, gain, w_gate, w_up, w_down, order)
 
 
 def body(
@@ -350,15 +401,12 @@
             local_rows, local_kv, head_width
         )
         new_keys = norm_rotate(new_keys, key_gain, position).astype(jnp.bfloat16)
-        new_values = (
-            jnp.dot(normed, w_value, preferred_element_type=jnp.float32)
-            .astype(jnp.bfloat16)
-            .reshape(local_rows, local_kv, head_width)
-        )
-        gate_logits = jnp.dot(normed, w_gate, preferred_element_type=jnp.float32)
-
-    all_queries = exchange(queries.reshape(local_rows, head_cols), "req", req_count, False, 0)
+
+    all_queries, gate_logits, new_values = query_exchange(
+        queries.reshape(local_rows, head_cols), normed, w_gate, w_value, req_count, 0
+    )
     all_queries = all_queries.reshape(all_rows, head_cols)
+    new_values = new_values.reshape(local_rows, local_kv, head_width)
 
     with jax.named_scope("page_owners"):
         page_counts = (lengths + page_size - 1) // page_size
@@ -438,15 +486,17 @@
         1,
     )
 
-    with jax.named_scope("mlp"):
-        mixed_f = mixed_rows.astype(jnp.float32)
-        normed_two = (mixed_f * rms_inv(mixed_f) * mlp_gain).astype(jnp.bfloat16)
-        gate_part = jnp.dot(normed_two, mlp_gate, preferred_element_type=jnp.float32)
-        up_part = jnp.dot(normed_two, mlp_up, preferred_element_type=jnp.float32)
-        inner_act = (jax.nn.silu(gate_part) * up_part).astype(jnp.bfloat16)
-        down_part = jnp.dot(inner_act, mlp_down, preferred_element_type=jnp.float32)
-
-    return tail_exchange(down_part, mixed_rows, deal_order.reshape(1, all_rows), head_count, req_count, 3)
+    return tail_exchange(
+        mixed_rows,
+        mlp_gain.reshape(1, model_width),
+        mlp_gate,
+        mlp_up,
+        mlp_down,
+        deal_order.reshape(1, all_rows),
+        head_count,
+        req_count,
+        3,
+    )
 
 
 def solution(mesh):

time: 107 us -> 101 us (0.944)
  matrix products: 18.1 us -> 10 us
  Pallas kernels: 73.8 us -> 76 us
    dot_general x4 -> x0, matrix products: 9.25 us -> none  [the longest x1 3.34 us: body(): down_part = jnp.dot(inner_act, mlp_down, preferred_element_type=jnp.float32)]
    pallas_call x1, Pallas kernels: 24.5 us -> 26 us  [tail_exchange(): pl.pallas_call(functools.partial(tail_kernel, head_count, req_count), out...]
    dot_general x1, matrix products: 0.29 us -> 1.47 us  [body(): jnp.dot(normed, w_query, preferred_element_type=jnp.float32)]
where the time goes in v7:
time: 101 us; the launch traced here: 100 us
  Pallas kernels  76 us (75%)
  other arithmetic  10.4 us (10%)
  matrix products  10 us (10%)
  local copies, waits for them, and re-layouts  3.49 us (3%)
    pallas_call x1, Pallas kernels, attend_exchange(): pl.pallas_call(functools.partial(attend_kernel, req_count, head_count, gr...  30.9 us
    pallas_call x1, Pallas kernels, tail_exchange(): pl.pallas_call(functools.partial(tail_kernel, head_count, req_count), out...  26 us
    pallas_call x1, Pallas kernels, query_exchange(): pl.pallas_call(functools.partial(query_kernel, count), out_shape=(jax.Sha...  19.2 us
    dot_general x1, matrix products, body(): jnp.einsum('pkgt,ptkd->pkgd', weights.astype(jnp.bfloat16), value_cache,...  2.32 us
    reduce_or x1, other arithmetic, body(): filled = jnp.where(jnp.any(owned_requests, axis=1), filled, 0)  2.23 us
    unnamed x14, local copies, waits for them, and re-layouts  2.1 us

profile of v7, /device:TPU:1, one launch (start us, length us, event | category | flops | bytes accessed | tf_op | source)
XLA Modules:
  0.0 100.1 jit_solution(3063048125776319565)
XLA Ops:
  0.0 0.9 dynamic_slice.3
  0.9 0.9 select_reduce_fusion.4
  1.8 1.0 fusion.13
  2.8 0.7 add_select_fusion
  3.6 0.9 fusion.15.normed_ref
  4.6 1.4 %multiply_reduce_fusion.1 = (f32[16]{0:T(128)S(1)}, f32[16,128]{1,0:T(8,128)S(1)}) fusion(bf16[16,2048]{1,0:T(8,128)(2,1)S(1)} %fusion.15.normed_ref, bf16[2048,128]{1,0:T(8,128)(2,1)} %param.26), kind=kOutput, calls=%fused_computation.56 | convolution fusion | flops 8392688 | bytes 598080 | tf_op jit(solution)/shard_map/projections/dot_general | solution.py:400
  5.9 0.7 multiply_bitcast_fusion
  6.8 0.7 pad_maximum_fusion.1.key_ref
  7.5 1.5 %fusion.38 = f32[16,256]{1,0:T(8,128)S(1)} fusion(bf16[16,2048]{1,0:T(8,128)(2,1)S(1)} %fusion.15.normed_ref, bf16[2048,256]{1,0:T(8,128)(2,1)} %param.25), kind=kOutput, calls=%fused_computation.75 | convolution fusion | flops 16777216 | bytes 1130496 | tf_op jit(solution)/shard_map/projections/dot_general | solution.py:396
  9.4 0.6 copy.51
  10.0 1.3 %select_reduce_fusion = s32[64]{0:T(128)S(1)} fusion(s32[512,64]{0,1:T(8,128)S(1)} %fusion.18), kind=kLoop, calls=%fused_computation | loop fusion | flops 6291392 | bytes 131328 | tf_op jit(solution)/shard_map/page_owners/reduce_sum | solution.py:422
  11.3 2.2 %fusion = (pred[64]{0:T(512)(128)(4,1)S(1)}, pred[64,512]{1,0:T(8,128)(4,1)S(1)}) fusion(s32[512,64]{0,1:T(8,128)S(1)} %fusion.18), kind=kLoop, calls=%fused_computation.2 | loop fusion | flops 6258624 | bytes 163904 | tf_op jit(solution)/shard_map/page_owners/reduce_or | solution.py:425
  13.7 0.3 convolution_compare_fusion
  14.2 19.2 %shard_map.172 = (bf16[32,16,256]{2,1,0:T(8,128)(2,1)}, f32[16,256]{1,0:T(8,128)}, bf16[16,128]{1,0:T(8,128)(2,1)}) custom-call(bf16[16,256]{1,0:T(8,128)(2,1)} %bitcast.54, bf16[16,2048]{1,0:T(8,128)(2,1)} %copy-done.1, bf16[2048,256]{1,0:T(8,128)(2,1)} %w_gate_ref.2, bf16[2048,128]{1,0:T(8,128)(2,1)} %w_value_ref.1), custom_call_target="tpu_custom_call" | custom-call | tf_op jit(solution)/shard_map/pallas_call | solution.py:182
  33.4 1.1 %convolution_convert_fusion.1 = bf16[64,256]{1,0:T(8,128)(2,1)S(1)} fusion(pred[64,512]{1,0:T(8,128)(4,1)S(1)} %convolution_compare_fusion, bf16[512,256]{1,0:T(8,128)(2,1)} %bitcast.53), kind=kOutput, calls=%fused_computation.12 | convolution fusion | flops 16793600 | bytes 327680 | tf_op jit(solution)/shard_map/page_owners/dot_general | solution.py:432
  34.5 1.3 %fusion.37 = (f32[64,2]{1,0:T(8,128)S(1)}, f32[64,2,128]{2,1,0:T(2,128)S(1)}) fusion(bf16[64,2,128]{2,1,0:T(2,128)(2,1)S(1)} %reshape.371, bf16[64,128,1,128]{3,1,2,0:T(8,128)(2,1)S(1)} %copy-done, pred[64,128]{1,0:T(8,128)(4,1)S(1)} %iota_compare_fusion.5), kind=kOutput, calls=%fused_computation.74 | convolution fusion | flops 4243328 | bytes 2204160 | tf_op jit(solution)/shard_map/page_attention/pkgd,ptkd->pkgt/dot_general | solution.py:439
  36.4 0.2 fusion.36
  36.6 1.0 %fusion.21 = f32[32,16,2]{1,2,0:T(2,128)S(1)} fusion(pred[32,16,64]{2,1,0:T(8,128)(4,1)S(1)} %bitcast.56, f32[64,2]{1,0:T(8,128)S(1)} %fusion.36), kind=kOutput, calls=%fused_computation.31 | convolution fusion | flops 786432 | bytes 37376 | tf_op jit(solution)/shard_map/page_attention/dot_general | solution.py:460
  37.6 2.3 %fusion.2 = f32[64,2,128]{2,1,0:T(2,128)S(1)} fusion(bf16[64,128,1,128]{3,1,2,0:T(8,128)(2,1)} %param.23, f32[64,2,128]{2,1,0:T(2,128)S(1)} %get-tuple-element.20, pred[64,128]{1,0:T(8,128)(4,1)S(1)} %iota_compare_fusion.5, f32[64,2]{1,0:T(8,128)S(1)} %copy.38), kind=kOutput, calls=%fused_computation.4 | convolution fusion | flops 4243456 | bytes 2236928 | tf_op jit(solution)/shard_map/page_attention/pkgt,ptkd->pkgd/dot_general | solution.py:453
  39.9 0.7 maximum_bitcast_fusion.stats_ref
  40.6 1.1 %convolution_convert_fusion = bf16[512,256]{1,0:T(8,128)(2,1)} fusion(pred[64,512]{1,0:T(8,128)(4,1)S(1)} %convolution_compare_fusion, f32[8,8,2,128]{3,2,1,0:T(2,128)S(1)} %bitcast.57), kind=kOutput, calls=%fused_computation.8 | convolution fusion | flops 100794368 | bytes 360448 | tf_op jit(solution)/shard_map/page_attention/dot_general | solution.py:463
  41.8 30.9 %shard_map.173.mixed_ref = bf16[16,2048]{1,0:T(8,128)(2,1)} custom-call(bf16[32,16,256]{2,1,0:T(8,128)(2,1)} %bitcast.51, f32[32,4,16]{2,1,0:T(4,128)} %maximum_bitcast_fusion.stats_ref, bf16[16,256]{1,0:T(8,128)(2,1)} %bitcast.55, bf16[16,128]{1,0:T(8,128)(2,1)} %pad_maximum_fusion.1.key_ref, bf16[16,128]{1,0:T(8,128)(2,1)} %get-tuple-element.9.value_ref, ...), custom_call_target="tpu_custom_call" | custom-call | tf_op jit(solution)/shard_map/pallas_call | solution.py:276
  72.6 26.0 %shard_map.174 = bf16[16,2048]{1,0:T(8,128)(2,1)} custom-call(bf16[16,2048]{1,0:T(8,128)(2,1)} %shard_map.173.mixed_ref, f32[1,2048]{1,0:T(1,128)} %bitcast.59, bf16[2048,384]{1,0:T(8,128)(2,1)} %w_gate_ref.3, bf16[2048,384]{1,0:T(8,128)(2,1)} %w_up_ref.1, bf16[384,2048]{1,0:T(8,128)(2,1)} %w_down_ref.1, s32[1,512]{1,0:T(1,128)} %bitcast.60), custom_call_target="tpu_custom_call" | custom-call | tf_op jit(solution)/shard_map/pallas_call | solution.py:338
  98.6 1.5 %copy.53 = bf16[16,2048]{1,0:T(8,128)(2,1)} copy(bf16[16,2048]{1,0:T(8,128)(2,1)} %shard_map.174) | data formatting | bytes 131072
  (37 shorter events, 1.6 us)
Async XLA Ops:
  0.0 34.5 %copy-start = (bf16[64,128,1,128]{3,1,2,0:T(8,128)(2,1)S(1)}, bf16[64,128,1,128]{3,1,2,0:T(8,128)(2,1)}, u32[]{:S(2)}) copy-start(bf16[64,128,1,128]{3,1,2,0:T(8,128)(2,1)} %param.22) | copy-start | bytes 6291460
  0.0 13.5 %copy-start.3 = (s32[512]{0:T(512)S(1)}, s32[512]{0:T(512)}, u32[]{:S(2)}) copy-start(s32[512]{0:T(512)} %param.20) | copy-start | bytes 6148
  0.0 13.6 %copy-start.4 = (s32[512]{0:T(512)S(1)}, s32[512]{0:T(512)}, u32[]{:S(2)}) copy-start(s32[512]{0:T(512)} %param.19) | copy-start | bytes 6148
  0.0 9.1 %copy-start.5 = (f32[128]{0:T(128)S(1)}, f32[128]{0:T(128)}, u32[]{:S(2)}) copy-start(f32[128]{0:T(128)} %param.30) | copy-start | bytes 1540
  0.0 9.9 %copy-start.2 = (s32[512,64]{0,1:T(8,128)S(1)}, s32[512,64]{0,1:T(8,128)}, u32[]{:S(2)}) copy-start(s32[512,64]{0,1:T(8,128)} %param.21) | copy-start | bytes 393220
  4.6 9.7 %copy-start.1 = (bf16[16,2048]{1,0:T(8,128)(2,1)}, bf16[16,2048]{1,0:T(8,128)(2,1)S(1)}, u32[]{:S(2)}) copy-start(bf16[16,2048]{1,0:T(8,128)(2,1)S(1)} %fusion.15.normed_ref) | copy-start | bytes 196612

commit v8 on v7

--- a/solution.py
+++ b/solution.py
@@ -154,7 +154,10 @@
     )(parts, hidden)
 
 
-def query_kernel(count, query_ref, normed_ref, w_gate_ref, w_value_ref, out_ref, gate_ref, value_ref, send_sems, recv_sems):
+def query_kernel(
+    count, query_ref, normed_ref, w_gate_ref, w_value_ref, w_key_ref, key_gain_ref, cos_ref, sin_ref, swap_ref,
+    out_ref, gate_ref, value_ref, key_ref, send_sems, recv_sems,
+):
     me, peers = peers_of("req", count)
     greet([("req", peer) for _, peer in peers])
     copies = []
@@ -173,11 +176,20 @@
     normed = normed_ref[...]
     gate_ref[...] = jnp.dot(normed, w_gate_ref[...], preferred_element_type=jnp.float32)
     value_ref[...] = jnp.dot(normed, w_value_ref[...], preferred_element_type=jnp.float32).astype(value_ref.dtype)
+    head_width = swap_ref.shape[0]
+    keys = jnp.dot(normed, w_key_ref[...], preferred_element_type=jnp.float32)
+    for kv in range(keys.shape[1] // head_width):
+        key = keys[:, kv * head_width : (kv + 1) * head_width]
+        key = key * rms_inv(key) * key_gain_ref[...]
+        swapped = jnp.dot(key, swap_ref[...], precision=lax.Precision.HIGHEST, preferred_element_type=jnp.float32)
+        key_ref[:, kv * head_width : (kv + 1) * head_width] = (key * cos_ref[...] + swapped * sin_ref[...]).astype(
+            key_ref.dtype
+        )
     for copy in copies:
         copy.wait()
 
 
-def query_exchange(queries, normed, w_gate, w_value, count, ident):
+def query_exchange(queries, normed, w_gate, w_value, w_key, key_gain, cosine, sine, swap, count, ident):
     rows = queries.shape[0]
     return pl.pallas_call(
         functools.partial(query_kernel, count),
@@ -185,12 +197,13 @@
             jax.ShapeDtypeStruct((count,) + queries.shape, queries.dtype),
             jax.ShapeDtypeStruct((rows, w_gate.shape[1]), jnp.float32),
             jax.ShapeDtypeStruct((rows, w_value.shape[1]), jnp.bfloat16),
+            jax.ShapeDtypeStruct((rows, w_key.shape[1]), jnp.bfloat16),
         ),
-        in_specs=[pl.BlockSpec(memory_space=pltpu.VMEM)] * 4,
-        out_specs=tuple(pl.BlockSpec(memory_space=pltpu.VMEM) for _ in range(3)),
+        in_specs=[pl.BlockSpec(memory_space=pltpu.VMEM)] * 9,
+        out_specs=tuple(pl.BlockSpec(memory_space=pltpu.VMEM) for _ in range(4)),
         scratch_shapes=[pltpu.SemaphoreType.DMA((count,)), pltpu.SemaphoreType.DMA((count,))],
         compiler_params=pltpu.CompilerParams(collective_id=ident, has_side_effects=True),
-    )(queries, normed, w_gate, w_value)
+    )(queries, normed, w_gate, w_value, w_key, key_gain, cosine, sine, swap)
 
 
 def attend_kernel(
@@ -397,16 +410,34 @@
             local_rows, local_kv, group_size, head_width
         )
         queries = norm_rotate(queries, query_gain, position).astype(jnp.bfloat16)
-        new_keys = jnp.dot(normed, w_key, preferred_element_type=jnp.float32).reshape(
-            local_rows, local_kv, head_width
-        )
-        new_keys = norm_rotate(new_keys, key_gain, position).astype(jnp.bfloat16)
-
-    all_queries, gate_logits, new_values = query_exchange(
-        queries.reshape(local_rows, head_cols), normed, w_gate, w_value, req_count, 0
+        half = head_width // 2
+        frequency = ROPE_BASE ** (-(jnp.arange(half, dtype=jnp.float32) * (2.0 / head_width)))
+        angles = position[:, None] * frequency[None, :]
+        cosine = jnp.concatenate([jnp.cos(angles)] * 2, axis=1)
+        sine = jnp.concatenate([jnp.sin(angles)] * 2, axis=1)
+        lanes = jnp.arange(head_width, dtype=jnp.int32)
+        swap = jnp.where(
+            lanes[:, None] == (lanes[None, :] + half) % head_width,
+            jnp.where(lanes[None, :] < half, -1.0, 1.0),
+            0.0,
+        ).astype(jnp.float32)
+
+    all_queries, gate_logits, new_values, new_keys = query_exchange(
+        queries.reshape(local_rows, head_cols),
+        normed,
+        w_gate,
+        w_value,
+        w_key,
+        key_gain.reshape(1, head_width),
+        cosine,
+        sine,
+        swap,
+        req_count,
+        0,
     )
     all_queries = all_queries.reshape(all_rows, head_cols)
     new_values = new_values.reshape(local_rows, local_kv, head_width)
+    new_keys = new_keys.reshape(local_rows, local_kv, head_width)
 
     with jax.named_scope("page_owners"):
         page_counts = (lengths + page_size - 1) // page_size

time: 101 us -> 99.2 us (0.982)
  matrix products: 10 us -> 8.66 us
    dot_general x1 -> x0, matrix products: 1.36 us -> none  [body(): jnp.dot(normed, w_key, preferred_element_type=jnp.float32)]
    unnamed x14 -> x12, local copies, waits for them, and re-layouts: 2.1 us -> 2.1 us
where the time goes in v8:
time: 99.2 us; the launch traced here: 98.8 us
  Pallas kernels  76.3 us (77%)
  other arithmetic  10.1 us (10%)
  matrix products  8.66 us (9%)
  local copies, waits for them, and re-layouts  3.51 us (4%)
    pallas_call x1, Pallas kernels, attend_exchange(): pl.pallas_call(functools.partial(attend_kernel, req_count, head_count, gr...  30.9 us
    pallas_call x1, Pallas kernels, tail_exchange(): pl.pallas_call(functools.partial(tail_kernel, head_count, req_count), out...  26.1 us
    pallas_call x1, Pallas kernels, query_exchange(): pl.pallas_call(functools.partial(query_kernel, count), out_shape=(jax.Sha...  19.4 us
    dot_general x1, matrix products, body(): jnp.einsum('pkgt,ptkd->pkgd', weights.astype(jnp.bfloat16), value_cache,...  2.3 us
    reduce_or x1, other arithmetic, body(): filled = jnp.where(jnp.any(owned_requests, axis=1), filled, 0)  2.21 us
    unnamed x12, local copies, waits for them, and re-layouts  2.1 us

profile of v8, /device:TPU:1, one launch (start us, length us, event | category | flops | bytes accessed | tf_op | source)
XLA Modules:
  0.0 98.8 jit_solution(9884672958429296732)
XLA Ops:
  0.0 0.9 dynamic_slice.3
  0.9 0.9 select_reduce_fusion.4
  1.9 1.0 fusion.13
  2.9 0.9 fusion.15.normed_ref
  3.9 1.5 %fusion.30 = f32[16,256]{1,0:T(8,128)S(1)} fusion(bf16[16,2048]{1,0:T(8,128)(2,1)S(1)} %fusion.15.normed_ref, bf16[2048,256]{1,0:T(8,128)(2,1)} %param.25), kind=kOutput, calls=%fused_computation.68 | convolution fusion | flops 16777216 | bytes 1130496 | tf_op jit(solution)/shard_map/projections/dot_general | solution.py:409
  5.5 0.7 multiply_multiply_fusion
  6.4 0.6 copy.51
  7.0 0.7 pad_maximum_fusion.1
  7.7 0.6 fusion.21.swap_ref
  8.4 19.4 %shard_map.172 = (bf16[32,16,256]{2,1,0:T(8,128)(2,1)}, f32[16,256]{1,0:T(8,128)}, bf16[16,128]{1,0:T(8,128)(2,1)}, bf16[16,128]{1,0:T(8,128)(2,1)}) custom-call(bf16[16,256]{1,0:T(8,128)(2,1)} %bitcast.47, bf16[16,2048]{1,0:T(8,128)(2,1)} %copy-done.1, bf16[2048,256]{1,0:T(8,128)(2,1)} %w_gate_ref.2, bf16[2048,128]{1,0:T(8,128)(2,1)} %w_value_ref.1, ...), custom_call_target="tpu_custom_call" | custom-call | tf_op jit(solution)/shard_map/pallas_call | solution.py:194
  27.8 2.2 %fusion = (pred[64]{0:T(512)(128)(4,1)S(1)}, pred[64,512]{1,0:T(8,128)(4,1)S(1)}) fusion(s32[512,64]{0,1:T(8,128)S(1)} %fusion.18), kind=kLoop, calls=%fused_computation.2 | loop fusion | flops 6258624 | bytes 163904 | tf_op jit(solution)/shard_map/page_owners/reduce_or | solution.py:456
  30.0 0.3 convolution_compare_fusion
  30.4 1.1 %convolution_convert_fusion.1 = bf16[64,256]{1,0:T(8,128)(2,1)S(1)} fusion(pred[64,512]{1,0:T(8,128)(4,1)S(1)} %convolution_compare_fusion, bf16[512,256]{1,0:T(8,128)(2,1)} %bitcast.46), kind=kOutput, calls=%fused_computation.12 | convolution fusion | flops 16793600 | bytes 327680 | tf_op jit(solution)/shard_map/page_owners/dot_general | solution.py:463
  31.6 1.3 %select_reduce_fusion = s32[64]{0:T(128)S(1)} fusion(s32[512,64]{0,1:T(8,128)S(1)} %fusion.18), kind=kLoop, calls=%fused_computation | loop fusion | flops 6291392 | bytes 131328 | tf_op jit(solution)/shard_map/page_owners/reduce_sum | solution.py:453
  33.0 1.3 %fusion.29 = (f32[64,2]{1,0:T(8,128)S(1)}, f32[64,2,128]{2,1,0:T(2,128)S(1)}) fusion(bf16[64,2,128]{2,1,0:T(2,128)(2,1)S(1)} %reshape.286, bf16[64,128,1,128]{3,1,2,0:T(8,128)(2,1)S(1)} %copy-done, pred[64,128]{1,0:T(8,128)(4,1)S(1)} %iota_compare_fusion.6), kind=kOutput, calls=%fused_computation.67 | convolution fusion | flops 4243328 | bytes 2204160 | tf_op jit(solution)/shard_map/page_attention/pkgd,ptkd->pkgt/dot_general | solution.py:470
  34.7 0.2 fusion.28
  34.9 0.2 copy.39
  35.1 1.0 %fusion.22 = f32[32,16,2]{1,2,0:T(2,128)S(1)} fusion(pred[32,16,64]{2,1,0:T(8,128)(4,1)S(1)} %bitcast.49, f32[64,2]{1,0:T(8,128)S(1)} %fusion.28), kind=kOutput, calls=%fused_computation.33 | convolution fusion | flops 786432 | bytes 37376 | tf_op jit(solution)/shard_map/page_attention/dot_general | solution.py:491
  36.3 0.7 maximum_bitcast_fusion.stats_ref
  36.9 2.3 %fusion.2 = f32[64,2,128]{2,1,0:T(2,128)S(1)} fusion(bf16[64,128,1,128]{3,1,2,0:T(8,128)(2,1)} %param.23, f32[64,2,128]{2,1,0:T(2,128)S(1)} %get-tuple-element.20, pred[64,128]{1,0:T(8,128)(4,1)S(1)} %iota_compare_fusion.6, f32[64,2]{1,0:T(8,128)S(1)} %copy.38), kind=kOutput, calls=%fused_computation.4 | convolution fusion | flops 4243456 | bytes 2236928 | tf_op jit(solution)/shard_map/page_attention/pkgt,ptkd->pkgd/dot_general | solution.py:484
  39.2 1.1 %convolution_convert_fusion = bf16[512,256]{1,0:T(8,128)(2,1)} fusion(pred[64,512]{1,0:T(8,128)(4,1)S(1)} %convolution_compare_fusion, f32[8,8,2,128]{3,2,1,0:T(2,128)S(1)} %bitcast.50), kind=kOutput, calls=%fused_computation.8 | convolution fusion | flops 100794368 | bytes 360448 | tf_op jit(solution)/shard_map/page_attention/dot_general | solution.py:494
  40.4 30.9 %shard_map.173.mixed_ref = bf16[16,2048]{1,0:T(8,128)(2,1)} custom-call(bf16[32,16,256]{2,1,0:T(8,128)(2,1)} %bitcast.44, f32[32,4,16]{2,1,0:T(4,128)} %maximum_bitcast_fusion.stats_ref, bf16[16,256]{1,0:T(8,128)(2,1)} %bitcast.48, bf16[16,128]{1,0:T(8,128)(2,1)} %get-tuple-element.10.key_ref, bf16[16,128]{1,0:T(8,128)(2,1)} %get-tuple-element.11.value_ref, ...), custom_call_target="tpu_custom_call" | custom-call | tf_op jit(solution)/shard_map/pallas_call | solution.py:289
  71.3 26.1 %shard_map.174 = bf16[16,2048]{1,0:T(8,128)(2,1)} custom-call(bf16[16,2048]{1,0:T(8,128)(2,1)} %shard_map.173.mixed_ref, f32[1,2048]{1,0:T(1,128)} %bitcast.52, bf16[2048,384]{1,0:T(8,128)(2,1)} %w_gate_ref.3, bf16[2048,384]{1,0:T(8,128)(2,1)} %w_up_ref.1, bf16[384,2048]{1,0:T(8,128)(2,1)} %w_down_ref.1, s32[1,512]{1,0:T(1,128)} %bitcast.53), custom_call_target="tpu_custom_call" | custom-call | tf_op jit(solution)/shard_map/pallas_call | solution.py:351
  97.3 1.5 %copy.53 = bf16[16,2048]{1,0:T(8,128)(2,1)} copy(bf16[16,2048]{1,0:T(8,128)(2,1)} %shard_map.174) | data formatting | bytes 131072
  (34 shorter events, 1.3 us)
Async XLA Ops:
  0.0 33.0 %copy-start = (bf16[64,128,1,128]{3,1,2,0:T(8,128)(2,1)S(1)}, bf16[64,128,1,128]{3,1,2,0:T(8,128)(2,1)}, u32[]{:S(2)}) copy-start(bf16[64,128,1,128]{3,1,2,0:T(8,128)(2,1)} %param.22) | copy-start | bytes 6291460
  0.0 27.7 %copy-start.3 = (s32[512]{0:T(512)S(1)}, s32[512]{0:T(512)}, u32[]{:S(2)}) copy-start(s32[512]{0:T(512)} %param.20) | copy-start | bytes 6148
  0.0 27.8 %copy-start.2 = (s32[512,64]{0,1:T(8,128)S(1)}, s32[512,64]{0,1:T(8,128)}, u32[]{:S(2)}) copy-start(s32[512,64]{0,1:T(8,128)} %param.21) | copy-start | bytes 393220
  3.9 4.5 %copy-start.1 = (bf16[16,2048]{1,0:T(8,128)(2,1)}, bf16[16,2048]{1,0:T(8,128)(2,1)S(1)}, u32[]{:S(2)}) copy-start(bf16[16,2048]{1,0:T(8,128)(2,1)S(1)} %fusion.15.normed_ref) | copy-start | bytes 196612
  3.9 26.2 %copy-start.4 = (s32[512]{0:T(512)S(1)}, s32[512]{0:T(512)}, u32[]{:S(2)}) copy-start(s32[512]{0:T(512)} %param.19) | copy-start | bytes 6148

commit v9 on v8

--- a/solution.py
+++ b/solution.py
@@ -154,12 +154,36 @@
     )(parts, hidden)
 
 
+def rope(values, cos_ref, sin_ref, swap):
+    swapped = jnp.dot(values, swap, precision=lax.Precision.HIGHEST, preferred_element_type=jnp.float32)
+    return values * cos_ref[...] + swapped * sin_ref[...]
+
+
 def query_kernel(
-    count, query_ref, normed_ref, w_gate_ref, w_value_ref, w_key_ref, key_gain_ref, cos_ref, sin_ref, swap_ref,
-    out_ref, gate_ref, value_ref, key_ref, send_sems, recv_sems,
+    count, hidden_ref, attn_gain_ref, w_query_ref, query_gain_ref, w_gate_ref, w_value_ref, w_key_ref,
+    key_gain_ref, cos_ref, sin_ref, out_ref, query_ref, gate_ref, value_ref, key_ref, send_sems, recv_sems,
 ):
     me, peers = peers_of("req", count)
-    greet([("req", peer) for _, peer in peers])
+    barrier = pltpu.get_barrier_semaphore()
+    for _, peer in peers:
+        pl.semaphore_signal(barrier, inc=1, device_id={"req": peer}, device_id_type=MESH_IDS)
+    head_width = cos_ref.shape[1]
+    lanes_in = lax.broadcasted_iota(jnp.int32, (head_width, head_width), 0)
+    lanes_out = lax.broadcasted_iota(jnp.int32, (head_width, head_width), 1)
+    swap = jnp.where(
+        lanes_in == lax.rem(lanes_out + head_width // 2, head_width),
+        jnp.where(lanes_out < head_width // 2, -1.0, 1.0),
+        0.0,
+    ).astype(jnp.float32)
+    hidden = hidden_ref[...].astype(jnp.float32)
+    normed = (hidden * rms_inv(hidden) * attn_gain_ref[...]).astype(jnp.bfloat16)
+    queries = jnp.dot(normed, w_query_ref[...], preferred_element_type=jnp.float32)
+    for pair in range(queries.shape[1] // head_width):
+        lanes = slice(pair * head_width, (pair + 1) * head_width)
+        query = queries[:, lanes]
+        query = query * rms_inv(query) * query_gain_ref[...]
+        query_ref[:, lanes] = rope(query, cos_ref, sin_ref, swap).astype(query_ref.dtype)
+    pl.semaphore_wait(barrier, len(peers))
     copies = []
     for offset, peer in peers:
         copy = pltpu.make_async_remote_copy(
@@ -173,37 +197,36 @@
         copy.start()
         copies.append(copy)
     out_ref[me] = query_ref[...]
-    normed = normed_ref[...]
     gate_ref[...] = jnp.dot(normed, w_gate_ref[...], preferred_element_type=jnp.float32)
     value_ref[...] = jnp.dot(normed, w_value_ref[...], preferred_element_type=jnp.float32).astype(value_ref.dtype)
-    head_width = swap_ref.shape[0]
     keys = jnp.dot(normed, w_key_ref[...], preferred_element_type=jnp.float32)
     for kv in range(keys.shape[1] // head_width):
-        key = keys[:, kv * head_width : (kv + 1) * head_width]
+        lanes = slice(kv * head_width, (kv + 1) * head_width)
+        key = keys[:, lanes]
         key = key * rms_inv(key) * key_gain_ref[...]
-        swapped = jnp.dot(key, swap_ref[...], precision=lax.Precision.HIGHEST, preferred_element_type=jnp.float32)
-        key_ref[:, kv * head_width : (kv + 1) * head_width] = (key * cos_ref[...] + swapped * sin_ref[...]).astype(
-            key_ref.dtype
-        )
+        key_ref[:, lanes] = rope(key, cos_ref, sin_ref, swap).astype(key_ref.dtype)
     for copy in copies:
         copy.wait()
 
 
-def query_exchange(queries, normed, w_gate, w_value, w_key, key_gain, cosine, sine, swap, count, ident):
-    rows = queries.shape[0]
+def query_exchange(
+    hidden, attn_gain, w_query, query_gain, w_gate, w_value, w_key, key_gain, cosine, sine, count, ident
+):
+    rows = hidden.shape[0]
     return pl.pallas_call(
         functools.partial(query_kernel, count),
         out_shape=(
-            jax.ShapeDtypeStruct((count,) + queries.shape, queries.dtype),
+            jax.ShapeDtypeStruct((count, rows, w_query.shape[1]), jnp.bfloat16),
+            jax.ShapeDtypeStruct((rows, w_query.shape[1]), jnp.bfloat16),
             jax.ShapeDtypeStruct((rows, w_gate.shape[1]), jnp.float32),
             jax.ShapeDtypeStruct((rows, w_value.shape[1]), jnp.bfloat16),
             jax.ShapeDtypeStruct((rows, w_key.shape[1]), jnp.bfloat16),
         ),
-        in_specs=[pl.BlockSpec(memory_space=pltpu.VMEM)] * 9,
-        out_specs=tuple(pl.BlockSpec(memory_space=pltpu.VMEM) for _ in range(4)),
+        in_specs=[pl.BlockSpec(memory_space=pltpu.VMEM)] * 10,
+        out_specs=tuple(pl.BlockSpec(memory_space=pltpu.VMEM) for _ in range(5)),
         scratch_shapes=[pltpu.SemaphoreType.DMA((count,)), pltpu.SemaphoreType.DMA((count,))],
         compiler_params=pltpu.CompilerParams(collective_id=ident, has_side_effects=True),
-    )(queries, normed, w_gate, w_value, w_key, key_gain, cosine, sine, swap)
+    )(hidden, attn_gain, w_query, query_gain, w_gate, w_value, w_key, key_gain, cosine, sine)
 
 
 def attend_kernel(
@@ -399,39 +422,28 @@
     scale_factor = 1.0 / math.sqrt(head_width)
     first_own = req_index * local_rows
 
-    with jax.named_scope("projections"):
-        hidden_f = hidden.astype(jnp.float32)
-        normed = (hidden_f * rms_inv(hidden_f) * attn_gain).astype(jnp.bfloat16)
+    with jax.named_scope("rotary_tables"):
         own_requests = lax.dynamic_slice_in_dim(deal_order, first_own, local_rows)
         request_ids = jnp.arange(all_rows, dtype=jnp.int32)
         own_pick = own_requests[:, None] == request_ids[None, :]
         position = jnp.sum(jnp.where(own_pick, lengths[None, :], 0), axis=1).astype(jnp.float32)
-        queries = jnp.dot(normed, w_query, preferred_element_type=jnp.float32).reshape(
-            local_rows, local_kv, group_size, head_width
-        )
-        queries = norm_rotate(queries, query_gain, position).astype(jnp.bfloat16)
         half = head_width // 2
         frequency = ROPE_BASE ** (-(jnp.arange(half, dtype=jnp.float32) * (2.0 / head_width)))
         angles = position[:, None] * frequency[None, :]
         cosine = jnp.concatenate([jnp.cos(angles)] * 2, axis=1)
         sine = jnp.concatenate([jnp.sin(angles)] * 2, axis=1)
-        lanes = jnp.arange(head_width, dtype=jnp.int32)
-        swap = jnp.where(
-            lanes[:, None] == (lanes[None, :] + half) % head_width,
-            jnp.where(lanes[None, :] < half, -1.0, 1.0),
-            0.0,
-        ).astype(jnp.float32)
-
-    all_queries, gate_logits, new_values, new_keys = query_exchange(
-        queries.reshape(local_rows, head_cols),
-        normed,
+
+    all_queries, own_queries, gate_logits, new_values, new_keys = query_exchange(
+        hidden,
+        attn_gain.reshape(1, model_width),
+        w_query,
+        query_gain.reshape(1, head_width),
         w_gate,
         w_value,
         w_key,
         key_gain.reshape(1, head_width),
         cosine,
         sine,
-        swap,
         req_count,
         0,
     )
@@ -505,7 +517,7 @@
     mixed_rows = attend_exchange(
         numerator_message,
         stats_message,
-        queries.reshape(local_rows, head_cols),
+        own_queries,
         new_keys.reshape(local_rows, local_kv * head_width),
         new_values.reshape(local_rows, local_kv * head_width),
         gate_logits,

time: 99.2 us -> 96.6 us (0.974)
  other arithmetic: 10.1 us -> 8.8 us
    dot_general x1 -> x0, matrix products: 1.5 us -> none  [body(): jnp.dot(normed, w_query, preferred_element_type=jnp.float32)]
    reduce_sum x2 -> x0, other arithmetic: 1.06 us -> none  [rms_inv(): jnp.mean(values * values, axis=-1, keepdims=True) + EPSILON]
    unnamed x12 -> x3, local copies, waits for them, and re-layouts: 2.1 us -> 1.48 us
where the time goes in v9:
time: 96.6 us; the launch traced here: 96.3 us
  Pallas kernels  76.6 us (79%)
  other arithmetic  8.8 us (9%)
  matrix products  7.86 us (8%)
  local copies, waits for them, and re-layouts  2.85 us (3%)
    pallas_call x1, Pallas kernels, attend_exchange(): pl.pallas_call(functools.partial(attend_kernel, req_count, head_count, gr...  30.9 us
    pallas_call x1, Pallas kernels, tail_exchange(): pl.pallas_call(functools.partial(tail_kernel, head_count, req_count), out...  26 us
    pallas_call x1, Pallas kernels, query_exchange(): pl.pallas_call(functools.partial(query_kernel, count), out_shape=(jax.Sha...  19.7 us
    dot_general x1, matrix products, body(): jnp.einsum('pkgt,ptkd->pkgd', weights.astype(jnp.bfloat16), value_cache,...  2.32 us
    reduce_or x1, other arithmetic, body(): filled = jnp.where(jnp.any(owned_requests, axis=1), filled, 0)  2.19 us

profile of v9, /device:TPU:1, one launch (start us, length us, event | category | flops | bytes accessed | tf_op | source)
XLA Modules:
  0.0 96.3 jit_solution(17004559230734567894)
XLA Ops:
  0.0 0.9 dynamic_slice.3
  0.9 0.9 select_reduce_fusion.4
  1.8 0.7 add_select_fusion
  2.5 0.1 multiply_sine_fusion
  2.6 0.7 pad_maximum_fusion
  3.3 0.9 fusion.15
  4.2 1.3 %select_reduce_fusion = s32[64]{0:T(128)S(1)} fusion(s32[512,64]{0,1:T(8,128)S(1)} %fusion.15), kind=kLoop, calls=%fused_computation | loop fusion | flops 6291392 | bytes 131328 | tf_op jit(solution)/shard_map/page_owners/reduce_sum | solution.py:465
  5.5 2.2 %fusion = (pred[64]{0:T(512)(128)(4,1)S(1)}, pred[64,512]{1,0:T(8,128)(4,1)S(1)}) fusion(s32[512,64]{0,1:T(8,128)S(1)} %fusion.15), kind=kLoop, calls=%fused_computation.2 | loop fusion | flops 6258624 | bytes 163904 | tf_op jit(solution)/shard_map/page_owners/reduce_or | solution.py:468
  7.7 0.8 select_reduce_fusion.3
  8.5 1.0 %convolution_compare_fusion = pred[64,512]{1,0:T(8,128)(4,1)S(1)} fusion(pred[64,512]{1,0:T(8,128)(4,1)S(1)} %get-tuple-element.16, s32[512]{0:T(512)} %param.19), kind=kOutput, calls=%fused_computation.9 | convolution fusion | flops 33849344 | bytes 67584 | tf_op jit(solution)/shard_map/page_owners/dot_general | solution.py:471
  9.6 0.2 copy.39
  9.8 19.7 %shard_map.172 = (bf16[32,16,256]{2,1,0:T(8,128)(2,1)}, bf16[16,256]{1,0:T(8,128)(2,1)}, f32[16,256]{1,0:T(8,128)}, bf16[16,128]{1,0:T(8,128)(2,1)}, bf16[16,128]{1,0:T(8,128)(2,1)}) custom-call(bf16[16,2048]{1,0:T(8,128)(2,1)} %hidden_ref.3, f32[1,2048]{1,0:T(1,128)} %bitcast.43, bf16[2048,256]{1,0:T(8,128)(2,1)} %w_query_ref.1, f32[1,128]{1,0:T(1,128)} %bitcast.46, ...), custom_call_target="tpu_custom_call" | custom-call | tf_op jit(solution)/shard_map/pallas_call | solution.py:216
  29.4 1.1 %convolution_convert_fusion.1 = bf16[64,256]{1,0:T(8,128)(2,1)S(1)} fusion(pred[64,512]{1,0:T(8,128)(4,1)S(1)} %convolution_compare_fusion, bf16[512,256]{1,0:T(8,128)(2,1)} %bitcast.40), kind=kOutput, calls=%fused_computation.12 | convolution fusion | flops 16793600 | bytes 327680 | tf_op jit(solution)/shard_map/page_owners/dot_general | solution.py:475
  30.6 1.3 %fusion.24 = (f32[64,2]{1,0:T(8,128)S(1)}, f32[64,2,128]{2,1,0:T(2,128)S(1)}) fusion(bf16[64,2,128]{2,1,0:T(2,128)(2,1)S(1)} %reshape.143, bf16[64,128,1,128]{3,1,2,0:T(8,128)(2,1)S(1)} %copy-done, pred[64,128]{1,0:T(8,128)(4,1)S(1)} %iota_compare_fusion.5), kind=kOutput, calls=%fused_computation.47 | convolution fusion | flops 4243328 | bytes 2204160 | tf_op jit(solution)/shard_map/page_attention/pkgd,ptkd->pkgt/dot_general | solution.py:482
  31.9 0.1 select_reduce_fusion.2
  32.1 0.1 select_reduce_fusion.1
  32.4 0.2 fusion.23
  32.6 1.0 %fusion.18 = f32[32,16,2]{1,2,0:T(2,128)S(1)} fusion(pred[32,16,64]{2,1,0:T(8,128)(4,1)S(1)} %bitcast.41, f32[64,2]{1,0:T(8,128)S(1)} %fusion.23), kind=kOutput, calls=%fused_computation.26 | convolution fusion | flops 786432 | bytes 37376 | tf_op jit(solution)/shard_map/page_attention/dot_general | solution.py:503
  33.7 2.3 %fusion.2 = f32[64,2,128]{2,1,0:T(2,128)S(1)} fusion(bf16[64,128,1,128]{3,1,2,0:T(8,128)(2,1)} %param.23, f32[64,2,128]{2,1,0:T(2,128)S(1)} %get-tuple-element.20, pred[64,128]{1,0:T(8,128)(4,1)S(1)} %iota_compare_fusion.5, f32[64,2]{1,0:T(8,128)S(1)} %copy.38), kind=kOutput, calls=%fused_computation.4 | convolution fusion | flops 4243456 | bytes 2236928 | tf_op jit(solution)/shard_map/page_attention/pkgt,ptkd->pkgd/dot_general | solution.py:496
  36.0 0.7 maximum_bitcast_fusion.stats_ref
  36.7 1.1 %convolution_convert_fusion = bf16[512,256]{1,0:T(8,128)(2,1)} fusion(pred[64,512]{1,0:T(8,128)(4,1)S(1)} %convolution_compare_fusion, f32[8,8,2,128]{3,2,1,0:T(2,128)S(1)} %bitcast.42), kind=kOutput, calls=%fused_computation.8 | convolution fusion | flops 100794368 | bytes 360448 | tf_op jit(solution)/shard_map/page_attention/dot_general | solution.py:506
  37.8 30.9 %shard_map.173.mixed_ref = bf16[16,2048]{1,0:T(8,128)(2,1)} custom-call(bf16[32,16,256]{2,1,0:T(8,128)(2,1)} %bitcast.38, f32[32,4,16]{2,1,0:T(4,128)} %maximum_bitcast_fusion.stats_ref, bf16[16,256]{1,0:T(8,128)(2,1)} %get-tuple-element.11.query_ref, bf16[16,128]{1,0:T(8,128)(2,1)} %get-tuple-element.12.key_ref, ...), custom_call_target="tpu_custom_call" | custom-call | tf_op jit(solution)/shard_map/pallas_call | solution.py:312
  68.7 26.0 %shard_map.174 = bf16[16,2048]{1,0:T(8,128)(2,1)} custom-call(bf16[16,2048]{1,0:T(8,128)(2,1)} %shard_map.173.mixed_ref, f32[1,2048]{1,0:T(1,128)} %bitcast.44, bf16[2048,384]{1,0:T(8,128)(2,1)} %w_gate_ref.3, bf16[2048,384]{1,0:T(8,128)(2,1)} %w_up_ref.1, bf16[384,2048]{1,0:T(8,128)(2,1)} %w_down_ref.1, s32[1,512]{1,0:T(1,128)} %bitcast.45), custom_call_target="tpu_custom_call" | custom-call | tf_op jit(solution)/shard_map/pallas_call | solution.py:374
  94.8 1.5 %copy.50 = bf16[16,2048]{1,0:T(8,128)(2,1)} copy(bf16[16,2048]{1,0:T(8,128)(2,1)} %shard_map.174) | data formatting | bytes 131072
  (12 shorter events, 0.4 us)
Async XLA Ops:
  0.0 30.6 %copy-start = (bf16[64,128,1,128]{3,1,2,0:T(8,128)(2,1)S(1)}, bf16[64,128,1,128]{3,1,2,0:T(8,128)(2,1)}, u32[]{:S(2)}) copy-start(bf16[64,128,1,128]{3,1,2,0:T(8,128)(2,1)} %param.22) | copy-start | bytes 6291460

commit v10 on v9

--- a/solution.py
+++ b/solution.py
@@ -160,8 +160,9 @@
 
 
 def query_kernel(
-    count, hidden_ref, attn_gain_ref, w_query_ref, query_gain_ref, w_gate_ref, w_value_ref, w_key_ref,
-    key_gain_ref, cos_ref, sin_ref, out_ref, query_ref, gate_ref, value_ref, key_ref, send_sems, recv_sems,
+    count, pool_pages, page_size, hidden_ref, attn_gain_ref, w_query_ref, query_gain_ref, w_gate_ref, w_value_ref,
+    w_key_ref, key_gain_ref, cos_ref, sin_ref, table_ref, lengths_ref, order_ref, out_ref, query_ref, gate_ref,
+    value_ref, key_ref, owned_ref, filled_ref, page_query_ref, slot_scratch, send_sems, recv_sems,
 ):
     me, peers = peers_of("req", count)
     barrier = pltpu.get_barrier_semaphore()
@@ -205,28 +206,68 @@
         key = keys[:, lanes]
         key = key * rms_inv(key) * key_gain_ref[...]
         key_ref[:, lanes] = rope(key, cos_ref, sin_ref, swap).astype(key_ref.dtype)
+    slots, requests = table_ref.shape
+    slot_ids = lax.broadcasted_iota(jnp.int32, (slots, requests), 0)
+    lengths = lengths_ref[...]
+    local_ids = table_ref[...] - me * pool_pages
+    usable = (slot_ids < (lengths + page_size - 1) // page_size) & (local_ids >= 0) & (local_ids < pool_pages)
+    keyed = jnp.where(usable, local_ids, pool_pages)
+    slot_f = slot_ids.astype(jnp.float32)
+
+    def one_page(page, carry):
+        hit = keyed == page
+        owned_ref[pl.ds(page, 1), :] = jnp.max(jnp.where(hit, 1.0, 0.0), axis=0, keepdims=True)
+        slot_scratch[pl.ds(page, 1), :] = jnp.sum(jnp.where(hit, slot_f, 0.0), axis=0, keepdims=True)
+        return carry
+
+    lax.fori_loop(0, pool_pages, one_page, 0)
+    owned_requests = owned_ref[...]
+    owner_slot = jnp.sum(slot_scratch[...], axis=1, keepdims=True)
+    owner_length = jnp.sum(owned_requests * lengths.astype(jnp.float32), axis=1, keepdims=True)
+    filled = jnp.clip(owner_length - owner_slot * page_size, 0.0, float(page_size))
+    filled_ref[...] = jnp.where(jnp.max(owned_requests, axis=1, keepdims=True) > 0.5, filled, 0.0).astype(
+        jnp.int32
+    )
+    dealing = (lax.broadcasted_iota(jnp.int32, (requests, requests), 0) == order_ref[...]).astype(jnp.bfloat16)
+    owned_rows = jnp.dot(owned_requests.astype(jnp.bfloat16), dealing, preferred_element_type=jnp.float32)
+    owned_ref[...] = jnp.where(owned_rows > 0.5, 1.0, 0.0)
     for copy in copies:
         copy.wait()
+    rows = query_ref.shape[0]
+    page_query_ref[...] = jnp.dot(
+        owned_ref[...].astype(jnp.bfloat16),
+        out_ref[...].reshape(count * rows, query_ref.shape[1]),
+        preferred_element_type=jnp.float32,
+    ).astype(page_query_ref.dtype)
 
 
 def query_exchange(
-    hidden, attn_gain, w_query, query_gain, w_gate, w_value, w_key, key_gain, cosine, sine, count, ident
+    hidden, attn_gain, w_query, query_gain, w_gate, w_value, w_key, key_gain, cosine, sine, table, lengths, order,
+    pool_pages, page_size, count, ident,
 ):
     rows = hidden.shape[0]
+    requests = table.shape[1]
     return pl.pallas_call(
-        functools.partial(query_kernel, count),
+        functools.partial(query_kernel, count, pool_pages, page_size),
         out_shape=(
             jax.ShapeDtypeStruct((count, rows, w_query.shape[1]), jnp.bfloat16),
             jax.ShapeDtypeStruct((rows, w_query.shape[1]), jnp.bfloat16),
             jax.ShapeDtypeStruct((rows, w_gate.shape[1]), jnp.float32),
             jax.ShapeDtypeStruct((rows, w_value.shape[1]), jnp.bfloat16),
             jax.ShapeDtypeStruct((rows, w_key.shape[1]), jnp.bfloat16),
+            jax.ShapeDtypeStruct((pool_pages, requests), jnp.float32),
+            jax.ShapeDtypeStruct((pool_pages, 1), jnp.int32),
+            jax.ShapeDtypeStruct((pool_pages, w_query.shape[1]), jnp.bfloat16),
         ),
-        in_specs=[pl.BlockSpec(memory_space=pltpu.VMEM)] * 10,
-        out_specs=tuple(pl.BlockSpec(memory_space=pltpu.VMEM) for _ in range(5)),
-        scratch_shapes=[pltpu.SemaphoreType.DMA((count,)), pltpu.SemaphoreType.DMA((count,))],
+        in_specs=[pl.BlockSpec(memory_space=pltpu.VMEM)] * 13,
+        out_specs=tuple(pl.BlockSpec(memory_space=pltpu.VMEM) for _ in range(8)),
+        scratch_shapes=[
+            pltpu.VMEM((pool_pages, requests), jnp.float32),
+            pltpu.SemaphoreType.DMA((count,)),
+            pltpu.SemaphoreType.DMA((count,)),
+        ],
         compiler_params=pltpu.CompilerParams(collective_id=ident, has_side_effects=True),
-    )(hidden, attn_gain, w_query, query_gain, w_gate, w_value, w_key, key_gain, cosine, sine)
+    )(hidden, attn_gain, w_query, query_gain, w_gate, w_value, w_key, key_gain, cosine, sine, table, lengths, order)
 
 
 def attend_kernel(
@@ -433,7 +474,7 @@
         cosine = jnp.concatenate([jnp.cos(angles)] * 2, axis=1)
         sine = jnp.concatenate([jnp.sin(angles)] * 2, axis=1)
 
-    all_queries, own_queries, gate_logits, new_values, new_keys = query_exchange(
+    outs = query_exchange(
         hidden,
         attn_gain.reshape(1, model_width),
         w_query,
@@ -444,38 +485,20 @@
         key_gain.reshape(1, head_width),
         cosine,
         sine,
+        page_table.T,
+        lengths.reshape(1, all_rows),
+        deal_order.reshape(1, all_rows),
+        pool_pages,
+        page_size,
         req_count,
         0,
     )
-    all_queries = all_queries.reshape(all_rows, head_cols)
+    _, own_queries, gate_logits, new_values, new_keys, owned_f, filled, page_queries = outs
+    filled = filled.reshape(pool_pages)
+    owned = owned_f > 0.5
+    page_queries = page_queries.reshape(pool_pages, local_kv, group_size, head_width)
     new_values = new_values.reshape(local_rows, local_kv, head_width)
     new_keys = new_keys.reshape(local_rows, local_kv, head_width)
-
-    with jax.named_scope("page_owners"):
-        page_counts = (lengths + page_size - 1) // page_size
-        slot_ids = jnp.arange(page_table.shape[1], dtype=jnp.int32)
-        local_ids = page_table - req_index * pool_pages
-        usable = (
-            (slot_ids[None, :] < page_counts[:, None]) & (local_ids >= 0) & (local_ids < pool_pages)
-        )
-        keyed = jnp.where(usable, local_ids, pool_pages)
-        page_ids = jnp.arange(pool_pages, dtype=jnp.int32)
-        match = keyed[None, :, :] == page_ids[:, None, None]
-        owned_requests = jnp.any(match, axis=2)
-        owner_slot = jnp.sum(jnp.where(match, slot_ids[None, None, :], 0), axis=(1, 2))
-        owner_length = jnp.sum(jnp.where(owned_requests, lengths[None, :], 0), axis=1)
-        filled = jnp.clip(owner_length - owner_slot * page_size, 0, page_size)
-        filled = jnp.where(jnp.any(owned_requests, axis=1), filled, 0)
-        dealing = (request_ids[:, None] == deal_order[None, :]).astype(jnp.bfloat16)
-        owned = (
-            jnp.dot(owned_requests.astype(jnp.bfloat16), dealing, preferred_element_type=jnp.float32)
-            > 0.5
-        )
-        page_queries = (
-            jnp.dot(owned.astype(jnp.bfloat16), all_queries, preferred_element_type=jnp.float32)
-            .astype(jnp.bfloat16)
-            .reshape(pool_pages, local_kv, group_size, head_width)
-        )
 
     with jax.named_scope("page_attention"):
         scores = (
@@ -499,7 +522,6 @@
             value_cache,
             preferred_element_type=jnp.float32,
         )
-        owned_f = owned.astype(jnp.float32)
         row_totals = jnp.dot(
             owned_f.T, page_totals.reshape(pool_pages, pairs), precision=lax.Precision.HIGHEST
         )

time: 96.6 us -> 91.6 us (0.948)
  other arithmetic: 8.8 us -> 3.81 us
  matrix products: 7.86 us -> 6.85 us
    reduce_or x1 -> x0, other arithmetic: 2.19 us -> none  [body(): filled = jnp.where(jnp.any(owned_requests, axis=1), filled, 0)]
    dot_general x2 -> x0, matrix products: 2.11 us -> none  [the longest x1 1.12 us: body(): jnp.dot(owned.astype(jnp.bfloat16), all_queries, preferred_element_type=j...]
    reduce_sum x2 -> x0, other arithmetic: 2.07 us -> none  [the longest x1 1.27 us: body(): jnp.sum(jnp.where(match, slot_ids[None, None, :], 0), axis=(1, 2))]
    select_n x3 -> x0, other arithmetic: 1.64 us -> none  [the longest x1 0.94 us: body(): keyed = jnp.where(usable, local_ids, pool_pages)]
where the time goes in v10:
time: 91.6 us; the launch traced here: 91.3 us
  Pallas kernels  77 us (84%)
  matrix products  6.85 us (7%)
  other arithmetic  3.81 us (4%)
  local copies, waits for them, and re-layouts  3.58 us (4%)
    pallas_call x1, Pallas kernels, attend_exchange(): pl.pallas_call(functools.partial(attend_kernel, req_count, head_count, gr...  31 us
    pallas_call x1, Pallas kernels, tail_exchange(): pl.pallas_call(functools.partial(tail_kernel, head_count, req_count), out...  26.1 us
    pallas_call x1, Pallas kernels, query_exchange(): pl.pallas_call(functools.partial(query_kernel, count, pool_pages, page_si...  19.9 us
    dot_general x1, matrix products, body(): jnp.einsum('pkgt,ptkd->pkgd', weights.astype(jnp.bfloat16), value_cache,...  2.3 us
    dot_general x1, matrix products, body(): jnp.dot(owned_f.T, page_totals.reshape(pool_pages, pairs), precision=lax....  1.95 us

profile of v10, /device:TPU:1, one launch (start us, length us, event | category | flops | bytes accessed | tf_op | source)
XLA Modules:
  0.0 91.3 jit_solution(16687519493943739411)
XLA Ops:
  0.0 0.9 dynamic_slice.3
  0.9 0.9 select_reduce_fusion.2
  1.8 0.1 multiply_sine_fusion
  1.9 0.7 pad_maximum_fusion
  2.6 19.9 %shard_map.172 = (bf16[32,16,256]{2,1,0:T(8,128)(2,1)}, bf16[16,256]{1,0:T(8,128)(2,1)}, f32[16,256]{1,0:T(8,128)}, bf16[16,128]{1,0:T(8,128)(2,1)}, bf16[16,128...) custom-call(bf16[16,2048]{1,0:T(8,128)(2,1)} %hidden_ref.3, f32[1,2048]{1,0:T(1,128)} %bitcast.41, ...), custom_call_target="tpu_custom_call" | custom-call | tf_op jit(solution)/shard_map/pallas_call | solution.py:250
  22.5 0.9 reduce.6
  23.4 0.1 iota_compare_fusion
  23.5 0.8 reshape.132
  24.2 1.3 %fusion.16 = (f32[64,2]{1,0:T(8,128)S(1)}, f32[64,2,128]{2,1,0:T(2,128)S(1)}) fusion(bf16[64,2,128]{2,1,0:T(2,128)(2,1)S(1)} %reshape.132, bf16[64,128,1,128]{3,1,2,0:T(8,128)(2,1)S(1)} %copy-done, pred[64,128]{1,0:T(8,128)(4,1)S(1)} %iota_compare_fusion), kind=kOutput, calls=%fused_computation.27 | convolution fusion | flops 4243328 | bytes 2204160 | tf_op jit(solution)/shard_map/page_attention/pkgd,ptkd->pkgt/dot_general | solution.py:505
  25.5 0.1 copy.34
  25.6 0.0 copy-done.1
  25.6 0.1 select_reduce_fusion.1
  25.8 0.1 select_reduce_fusion
  25.9 0.1 copy.35
  26.0 0.2 fusion.15
  26.2 0.1 copy.36
  26.3 1.9 %fusion.12 = f32[32,16,2]{1,2,0:T(2,128)S(1)} fusion(f32[32,16,64]{2,1,0:T(8,128)S(1)} %bitcast.37, f32[64,2]{1,0:T(8,128)S(1)} %fusion.15), kind=kOutput, calls=%fused_computation.14 | convolution fusion | flops 786432 | bytes 135680 | tf_op jit(solution)/shard_map/page_attention/dot_general | solution.py:525
  28.3 0.1 mul.55
  28.4 0.7 maximum_bitcast_fusion.stats_ref
  29.1 2.3 %fusion = f32[64,2,128]{2,1,0:T(2,128)S(1)} fusion(bf16[64,128,1,128]{3,1,2,0:T(8,128)(2,1)} %param.23, f32[64,2,128]{2,1,0:T(2,128)S(1)} %get-tuple-element.22, pred[64,128]{1,0:T(8,128)(4,1)S(1)} %iota_compare_fusion, f32[64,2]{1,0:T(8,128)S(1)} %copy.35), kind=kOutput, calls=%fused_computation | convolution fusion | flops 4243456 | bytes 2236928 | tf_op jit(solution)/shard_map/page_attention/pkgt,ptkd->pkgd/dot_general | solution.py:519
  31.4 1.3 %convolution_convert_fusion = bf16[512,256]{1,0:T(8,128)(2,1)} fusion(f32[64,512]{1,0:T(8,128)S(1)} %copy-done.1, f32[8,8,2,128]{3,2,1,0:T(2,128)S(1)} %bitcast.40), kind=kOutput, calls=%fused_computation.4 | convolution fusion | flops 100794368 | bytes 458752 | tf_op jit(solution)/shard_map/page_attention/dot_general | solution.py:528
  32.7 31.0 %shard_map.173.mixed_ref = bf16[16,2048]{1,0:T(8,128)(2,1)} custom-call(bf16[32,16,256]{2,1,0:T(8,128)(2,1)} %bitcast.38, f32[32,4,16]{2,1,0:T(4,128)} %maximum_bitcast_fusion.stats_ref, bf16[16,256]{1,0:T(8,128)(2,1)} %get-tuple-element.15.query_ref, bf16[16,128]{1,0:T(8,128)(2,1)} %get-tuple-element.16.key_ref, ...), custom_call_target="tpu_custom_call" | custom-call | tf_op jit(solution)/shard_map/pallas_call | solution.py:353
  63.7 26.1 %shard_map.174 = bf16[16,2048]{1,0:T(8,128)(2,1)} custom-call(bf16[16,2048]{1,0:T(8,128)(2,1)} %shard_map.173.mixed_ref, f32[1,2048]{1,0:T(1,128)} %bitcast.42, bf16[2048,384]{1,0:T(8,128)(2,1)} %w_gate_ref.3, bf16[2048,384]{1,0:T(8,128)(2,1)} %w_up_ref.1, bf16[384,2048]{1,0:T(8,128)(2,1)} %w_down_ref.1, s32[1,512]{1,0:T(1,128)} %bitcast.44), custom_call_target="tpu_custom_call" | custom-call | tf_op jit(solution)/shard_map/pallas_call | solution.py:415
  89.8 1.5 %copy.47 = bf16[16,2048]{1,0:T(8,128)(2,1)} copy(bf16[16,2048]{1,0:T(8,128)(2,1)} %shard_map.174) | data formatting | bytes 131072
  (8 shorter events, 0.1 us)
Async XLA Ops:
  0.0 24.2 %copy-start = (bf16[64,128,1,128]{3,1,2,0:T(8,128)(2,1)S(1)}, bf16[64,128,1,128]{3,1,2,0:T(8,128)(2,1)}, u32[]{:S(2)}) copy-start(bf16[64,128,1,128]{3,1,2,0:T(8,128)(2,1)} %param.22) | copy-start | bytes 6291460
  22.5 3.1 %copy-start.1 = (f32[64,512]{1,0:T(8,128)S(1)}, f32[64,512]{1,0:T(8,128)}, u32[]{:S(2)}) copy-start(f32[64,512]{1,0:T(8,128)} %get-tuple-element.12) | copy-start | bytes 393220

commit v11 on v10

--- a/solution.py
+++ b/solution.py
@@ -225,9 +225,9 @@
     owner_slot = jnp.sum(slot_scratch[...], axis=1, keepdims=True)
     owner_length = jnp.sum(owned_requests * lengths.astype(jnp.float32), axis=1, keepdims=True)
     filled = jnp.clip(owner_length - owner_slot * page_size, 0.0, float(page_size))
-    filled_ref[...] = jnp.where(jnp.max(owned_requests, axis=1, keepdims=True) > 0.5, filled, 0.0).astype(
-        jnp.int32
-    )
+    filled = jnp.where(jnp.max(owned_requests, axis=1, keepdims=True) > 0.5, filled, 0.0)
+    tokens = lax.broadcasted_iota(jnp.int32, filled_ref.shape, 1).astype(jnp.float32)
+    filled_ref[...] = jnp.where(tokens < filled, 1.0, 0.0)
     dealing = (lax.broadcasted_iota(jnp.int32, (requests, requests), 0) == order_ref[...]).astype(jnp.bfloat16)
     owned_rows = jnp.dot(owned_requests.astype(jnp.bfloat16), dealing, preferred_element_type=jnp.float32)
     owned_ref[...] = jnp.where(owned_rows > 0.5, 1.0, 0.0)
@@ -256,7 +256,7 @@
             jax.ShapeDtypeStruct((rows, w_value.shape[1]), jnp.bfloat16),
             jax.ShapeDtypeStruct((rows, w_key.shape[1]), jnp.bfloat16),
             jax.ShapeDtypeStruct((pool_pages, requests), jnp.float32),
-            jax.ShapeDtypeStruct((pool_pages, 1), jnp.int32),
+            jax.ShapeDtypeStruct((pool_pages, page_size), jnp.float32),
             jax.ShapeDtypeStruct((pool_pages, w_query.shape[1]), jnp.bfloat16),
         ),
         in_specs=[pl.BlockSpec(memory_space=pltpu.VMEM)] * 13,
@@ -493,8 +493,7 @@
         req_count,
         0,
     )
-    _, own_queries, gate_logits, new_values, new_keys, owned_f, filled, page_queries = outs
-    filled = filled.reshape(pool_pages)
+    _, own_queries, gate_logits, new_values, new_keys, owned_f, live_tokens, page_queries = outs
     owned = owned_f > 0.5
     page_queries = page_queries.reshape(pool_pages, local_kv, group_size, head_width)
     new_values = new_values.reshape(local_rows, local_kv, head_width)
@@ -505,9 +504,7 @@
             jnp.einsum("pkgd,ptkd->pkgt", page_queries, key_cache, preferred_element_type=jnp.float32)
             * scale_factor
         )
-        live_mask = (
-            jnp.arange(page_size, dtype=jnp.int32)[None, None, None, :] < filled[:, None, None, None]
-        )
+        live_mask = live_tokens[:, None, None, :] > 0.5
         scores = jnp.where(live_mask, scores, LOW_SCORE)
         page_peaks = jnp.max(scores, axis=-1)
         owned_b = owned[:, :, None, None]
@@ -522,13 +519,11 @@
             value_cache,
             preferred_element_type=jnp.float32,
         )
-        row_totals = jnp.dot(
-            owned_f.T, page_totals.reshape(pool_pages, pairs), precision=lax.Precision.HIGHEST
-        )
+        row_totals = jnp.sum(jnp.where(owned_b, page_totals[:, None], 0.0), axis=0).reshape(all_rows, pairs)
         row_numerators = jnp.dot(
-            owned_f.T,
-            page_numerators.reshape(pool_pages, head_cols),
-            precision=lax.Precision.HIGHEST,
+            owned_f.T.astype(jnp.bfloat16),
+            page_numerators.reshape(pool_pages, head_cols).astype(jnp.bfloat16),
+            preferred_element_type=jnp.float32,
         )
         numerator_message = row_numerators.astype(jnp.bfloat16).reshape(req_count, local_rows, head_cols)
         stats_message = jnp.concatenate(

time: 91.6 us -> 90.2 us (0.985)
  matrix products: 6.85 us -> 4.52 us
    dot_general x2 -> x1, matrix products: 3.28 us -> 0.95 us  [body(): jnp.dot(owned_f.T.astype(jnp.bfloat16), page_numerators.reshape(pool_page...]
where the time goes in v11:
time: 90.2 us; the launch traced here: 89.8 us
  Pallas kernels  76.9 us (85%)
  other arithmetic  4.61 us (5%)
  matrix products  4.52 us (5%)
  local copies, waits for them, and re-layouts  3.62 us (4%)
    pallas_call x1, Pallas kernels, attend_exchange(): pl.pallas_call(functools.partial(attend_kernel, req_count, head_count, gr...  31 us
    pallas_call x1, Pallas kernels, tail_exchange(): pl.pallas_call(functools.partial(tail_kernel, head_count, req_count), out...  26.1 us
    pallas_call x1, Pallas kernels, query_exchange(): pl.pallas_call(functools.partial(query_kernel, count, pool_pages, page_si...  19.9 us
    dot_general x1, matrix products, body(): jnp.einsum('pkgt,ptkd->pkgd', weights.astype(jnp.bfloat16), value_cache,...  2.31 us

profile of v11, /device:TPU:1, one launch (start us, length us, event | category | flops | bytes accessed | tf_op | source)
XLA Modules:
  0.0 89.8 jit_solution(1359208529058362389)
XLA Ops:
  0.0 0.9 %dynamic_slice.3 = s32[16]{0:T(128)S(1)} dynamic-slice(s32[512]{0:T(512)} %param.19, s32[]{:T(128)S(6)} %select_n.51), dynamic_slice_sizes={16} | dynamic-slice | bytes 132 | tf_op jit(solution)/shard_map/rotary_tables/dynamic_slice | solution.py:467
  0.9 0.9 select_reduce_fusion.3
  1.8 0.1 multiply_sine_fusion
  1.9 0.7 pad_maximum_fusion
  2.6 19.9 %shard_map.172 = (bf16[32,16,256]{2,1,0:T(8,128)(2,1)}, bf16[16,256]{1,0:T(8,128)(2,1)}, f32[16,256]{1,0:T(8,128)}, bf16[16,128]{1,0:T(8,128)(2,1)}, bf16[16,128...) custom-call(bf16[16,2048]{1,0:T(8,128)(2,1)} %hidden_ref.3, ...), custom_call_target="tpu_custom_call" | custom-call | tf_op jit(solution)/shard_map/pallas_call | solution.py:250
  22.5 0.8 broadcast_compare_fusion.1
  23.2 0.9 %broadcast_compare_fusion = pred[64,512]{1,0:T(8,128)(4,1)S(1)} fusion(f32[64,512]{1,0:T(8,128)} %get-tuple-element.12), kind=kLoop, calls=%fused_computation.13 | loop fusion | flops 32768 | bytes 163840 | tf_op jit(solution)/shard_map/gt | solution.py:497
  24.2 0.8 reshape.119
  24.9 1.3 %fusion.18 = (f32[64,2]{1,0:T(8,128)S(1)}, f32[64,2,128]{2,1,0:T(2,128)S(1)}) fusion(bf16[64,2,128]{2,1,0:T(2,128)(2,1)S(1)} %reshape.119, bf16[64,128,1,128]{3,1,2,0:T(8,128)(2,1)S(1)} %copy-done, pred[64,128]{1,0:T(8,128)(4,1)S(1)} %broadcast_compare_fusion.1), kind=kOutput, calls=%fused_computation.28 | convolution fusion | flops 4243328 | bytes 2204160 | tf_op jit(solution)/shard_map/page_attention/pkgd,ptkd->pkgt/dot_general | solution.py:504
  26.2 0.1 copy.25
  26.3 0.1 select_reduce_fusion.2
  26.4 0.1 select_reduce_fusion.1
  26.5 0.1 mul.55
  26.6 0.1 copy.26
  26.7 0.2 fusion.17
  27.0 2.3 %fusion.10 = bf16[64,2,128]{2,1,0:T(2,128)(2,1)S(1)} fusion(bf16[64,128,1,128]{3,1,2,0:T(8,128)(2,1)} %param.23, f32[64,2,128]{2,1,0:T(2,128)S(1)} %get-tuple-element.22, pred[64,128]{1,0:T(8,128)(4,1)S(1)} %broadcast_compare_fusion.1, f32[64,2]{1,0:T(8,128)S(1)} %copy.26), kind=kOutput, calls=%fused_computation.7 | convolution fusion | flops 4259840 | bytes 2204160 | tf_op jit(solution)/shard_map/page_attention/pkgt,ptkd->pkgd/dot_general | solution.py:516
  29.3 0.1 copy.27
  29.4 0.1 select_reduce_fusion
  29.5 0.1 reshape.123
  29.6 0.7 maximum_bitcast_fusion.stats_ref
  30.3 0.9 %convolution_convert_fusion = bf16[512,256]{1,0:T(8,128)(2,1)} fusion(f32[64,512]{1,0:T(8,128)S(1)} %copy-done.1, bf16[8,8,2,128]{3,2,1,0:T(2,128)(2,1)S(1)} %bitcast.35), kind=kOutput, calls=%fused_computation.4 | convolution fusion | flops 16941056 | bytes 425984 | tf_op jit(solution)/shard_map/page_attention/dot_general | solution.py:523
  31.2 31.0 %shard_map.173.mixed_ref = bf16[16,2048]{1,0:T(8,128)(2,1)} custom-call(bf16[32,16,256]{2,1,0:T(8,128)(2,1)} %bitcast.33, f32[32,4,16]{2,1,0:T(4,128)} %maximum_bitcast_fusion.stats_ref, bf16[16,256]{1,0:T(8,128)(2,1)} %get-tuple-element.15.query_ref, bf16[16,128]{1,0:T(8,128)(2,1)} %get-tuple-element.16.key_ref, ...), custom_call_target="tpu_custom_call" | custom-call | tf_op jit(solution)/shard_map/pallas_call | solution.py:353
  62.2 26.1 %shard_map.174 = bf16[16,2048]{1,0:T(8,128)(2,1)} custom-call(bf16[16,2048]{1,0:T(8,128)(2,1)} %shard_map.173.mixed_ref, f32[1,2048]{1,0:T(1,128)} %bitcast.37, bf16[2048,384]{1,0:T(8,128)(2,1)} %w_gate_ref.3, bf16[2048,384]{1,0:T(8,128)(2,1)} %w_up_ref.1, bf16[384,2048]{1,0:T(8,128)(2,1)} %w_down_ref.1, s32[1,512]{1,0:T(1,128)} %bitcast.39), custom_call_target="tpu_custom_call" | custom-call | tf_op jit(solution)/shard_map/pallas_call | solution.py:415
  88.3 1.5 %copy.36 = bf16[16,2048]{1,0:T(8,128)(2,1)} copy(bf16[16,2048]{1,0:T(8,128)(2,1)} %shard_map.174) | data formatting | bytes 131072
  (9 shorter events, 0.1 us)
Async XLA Ops:
  0.0 24.9 %copy-start = (bf16[64,128,1,128]{3,1,2,0:T(8,128)(2,1)S(1)}, bf16[64,128,1,128]{3,1,2,0:T(8,128)(2,1)}, u32[]{:S(2)}) copy-start(bf16[64,128,1,128]{3,1,2,0:T(8,128)(2,1)} %param.22) | copy-start | bytes 6291460
  26.2 4.1 %copy-start.1 = (f32[64,512]{1,0:T(8,128)S(1)}, f32[64,512]{1,0:T(8,128)}, u32[]{:S(2)}) copy-start(f32[64,512]{1,0:T(8,128)} %get-tuple-element.12) | copy-start | bytes 393220

commit v12 on v11

--- a/solution.py
+++ b/solution.py
@@ -464,15 +464,17 @@
     first_own = req_index * local_rows
 
     with jax.named_scope("rotary_tables"):
-        own_requests = lax.dynamic_slice_in_dim(deal_order, first_own, local_rows)
         request_ids = jnp.arange(all_rows, dtype=jnp.int32)
+        own_rows = first_own + jnp.arange(local_rows, dtype=jnp.int32)
+        own_requests = jnp.sum(jnp.where(own_rows[:, None] == request_ids[None, :], deal_order[None, :], 0), axis=1)
         own_pick = own_requests[:, None] == request_ids[None, :]
         position = jnp.sum(jnp.where(own_pick, lengths[None, :], 0), axis=1).astype(jnp.float32)
         half = head_width // 2
-        frequency = ROPE_BASE ** (-(jnp.arange(half, dtype=jnp.float32) * (2.0 / head_width)))
+        lane_ids = jnp.arange(head_width, dtype=jnp.int32) % half
+        frequency = ROPE_BASE ** (-(lane_ids.astype(jnp.float32) * (2.0 / head_width)))
         angles = position[:, None] * frequency[None, :]
-        cosine = jnp.concatenate([jnp.cos(angles)] * 2, axis=1)
-        sine = jnp.concatenate([jnp.sin(angles)] * 2, axis=1)
+        cosine = jnp.cos(angles)
+        sine = jnp.sin(angles)
 
     outs = query_exchange(
         hidden,

time: 90.2 us -> 90.2 us (level)
  other arithmetic: 4.61 us -> 5.56 us
    reduce_sum x0 -> x1, other arithmetic: none -> 1.01 us  [body(): jnp.sum(jnp.where(own_rows[:, None] == request_ids[None, :], deal_order[N...]
    dynamic_slice x1 -> x0, local copies, waits for them, and re-layouts: 0.9 us -> none  [body(): own_requests = lax.dynamic_slice_in_dim(deal_order, first_own, local_rows)]
where the time goes in v12:
time: 90.2 us; the launch traced here: 89.9 us
  Pallas kernels  77 us (85%)
  other arithmetic  5.56 us (6%)
  matrix products  4.51 us (5%)
  local copies, waits for them, and re-layouts  2.72 us (3%)
    pallas_call x1, Pallas kernels, attend_exchange(): pl.pallas_call(functools.partial(attend_kernel, req_count, head_count, gr...  31 us
    pallas_call x1, Pallas kernels, tail_exchange(): pl.pallas_call(functools.partial(tail_kernel, head_count, req_count), out...  26.1 us
    pallas_call x1, Pallas kernels, query_exchange(): pl.pallas_call(functools.partial(query_kernel, count, pool_pages, page_si...  19.9 us
    dot_general x1, matrix products, body(): jnp.einsum('pkgt,ptkd->pkgd', weights.astype(jnp.bfloat16), value_cache,...  2.31 us

profile of v12, /device:TPU:1, one launch (start us, length us, event | category | flops | bytes accessed | tf_op | source)
XLA Modules:
  0.0 89.9 jit_solution(1961001443677352786)
XLA Ops:
  0.0 1.0 %select_reduce_fusion.4 = s32[16]{0:T(128)S(1)} fusion(s32[512]{0:T(512)} %param.19, s32[16]{0:T(128)S(1)} %iota_add_fusion), kind=kLoop, calls=%fused_computation.20 | loop fusion | flops 24560 | bytes 2176 | tf_op jit(solution)/shard_map/rotary_tables/reduce_sum | solution.py:469
  1.0 0.9 select_reduce_fusion.3
  1.9 0.7 multiply_sine_fusion
  2.6 19.9 %shard_map.172 = (bf16[32,16,256]{2,1,0:T(8,128)(2,1)}, bf16[16,256]{1,0:T(8,128)(2,1)}, f32[16,256]{1,0:T(8,128)}, bf16[16,128]{1,0:T(8,128)(2,1)}, bf16[16,128...) custom-call(bf16[16,2048]{1,0:T(8,128)(2,1)} %hidden_ref.3, ...), custom_call_target="tpu_custom_call" | custom-call | tf_op jit(solution)/shard_map/pallas_call | solution.py:250
  22.5 0.8 broadcast_compare_fusion.1
  23.3 0.9 %broadcast_compare_fusion = pred[64,512]{1,0:T(8,128)(4,1)S(1)} fusion(f32[64,512]{1,0:T(8,128)} %get-tuple-element.12), kind=kLoop, calls=%fused_computation.13 | loop fusion | flops 32768 | bytes 163840 | tf_op jit(solution)/shard_map/gt | solution.py:499
  24.2 0.8 reshape.128
  25.0 0.0 copy-done
  25.0 1.3 %fusion.22 = (f32[64,2]{1,0:T(8,128)S(1)}, f32[64,2,128]{2,1,0:T(2,128)S(1)}) fusion(bf16[64,2,128]{2,1,0:T(2,128)(2,1)S(1)} %reshape.128, bf16[64,128,1,128]{3,1,2,0:T(8,128)(2,1)S(1)} %copy-done, pred[64,128]{1,0:T(8,128)(4,1)S(1)} %broadcast_compare_fusion.1), kind=kOutput, calls=%fused_computation.33 | convolution fusion | flops 4243328 | bytes 2204160 | tf_op jit(solution)/shard_map/page_attention/pkgd,ptkd->pkgt/dot_general | solution.py:506
  26.2 0.1 copy.25
  26.3 0.1 select_reduce_fusion.2
  26.5 0.1 select_reduce_fusion.1
  26.6 0.1 mul.55
  26.7 0.1 copy.26
  26.8 0.2 fusion.21
  27.0 2.3 %fusion.10 = bf16[64,2,128]{2,1,0:T(2,128)(2,1)S(1)} fusion(bf16[64,128,1,128]{3,1,2,0:T(8,128)(2,1)} %param.23, f32[64,2,128]{2,1,0:T(2,128)S(1)} %get-tuple-element.22, pred[64,128]{1,0:T(8,128)(4,1)S(1)} %broadcast_compare_fusion.1, f32[64,2]{1,0:T(8,128)S(1)} %copy.26), kind=kOutput, calls=%fused_computation.7 | convolution fusion | flops 4259840 | bytes 2204160 | tf_op jit(solution)/shard_map/page_attention/pkgt,ptkd->pkgd/dot_general | solution.py:518
  29.3 0.1 copy.27
  29.4 0.1 select_reduce_fusion
  29.5 0.1 reshape.132
  29.6 0.7 maximum_bitcast_fusion.stats_ref
  30.3 0.9 %convolution_convert_fusion = bf16[512,256]{1,0:T(8,128)(2,1)} fusion(f32[64,512]{1,0:T(8,128)S(1)} %copy-done.1, bf16[8,8,2,128]{3,2,1,0:T(2,128)(2,1)S(1)} %bitcast.35), kind=kOutput, calls=%fused_computation.4 | convolution fusion | flops 16941056 | bytes 425984 | tf_op jit(solution)/shard_map/page_attention/dot_general | solution.py:525
  31.2 31.0 %shard_map.173.mixed_ref = bf16[16,2048]{1,0:T(8,128)(2,1)} custom-call(bf16[32,16,256]{2,1,0:T(8,128)(2,1)} %bitcast.33, f32[32,4,16]{2,1,0:T(4,128)} %maximum_bitcast_fusion.stats_ref, bf16[16,256]{1,0:T(8,128)(2,1)} %get-tuple-element.15.query_ref, bf16[16,128]{1,0:T(8,128)(2,1)} %get-tuple-element.16.key_ref, ...), custom_call_target="tpu_custom_call" | custom-call | tf_op jit(solution)/shard_map/pallas_call | solution.py:353
  62.3 26.1 %shard_map.174 = bf16[16,2048]{1,0:T(8,128)(2,1)} custom-call(bf16[16,2048]{1,0:T(8,128)(2,1)} %shard_map.173.mixed_ref, f32[1,2048]{1,0:T(1,128)} %bitcast.39, bf16[2048,384]{1,0:T(8,128)(2,1)} %w_gate_ref.3, bf16[2048,384]{1,0:T(8,128)(2,1)} %w_up_ref.1, bf16[384,2048]{1,0:T(8,128)(2,1)} %w_down_ref.1, s32[1,512]{1,0:T(1,128)} %bitcast.37), custom_call_target="tpu_custom_call" | custom-call | tf_op jit(solution)/shard_map/pallas_call | solution.py:415
  88.4 1.5 %copy.36 = bf16[16,2048]{1,0:T(8,128)(2,1)} copy(bf16[16,2048]{1,0:T(8,128)(2,1)} %shard_map.174) | data formatting | bytes 131072
  (9 shorter events, 0.1 us)
Async XLA Ops:
  0.0 25.0 %copy-start = (bf16[64,128,1,128]{3,1,2,0:T(8,128)(2,1)S(1)}, bf16[64,128,1,128]{3,1,2,0:T(8,128)(2,1)}, u32[]{:S(2)}) copy-start(bf16[64,128,1,128]{3,1,2,0:T(8,128)(2,1)} %param.22) | copy-start | bytes 6291460
  26.2 4.1 %copy-start.1 = (f32[64,512]{1,0:T(8,128)S(1)}, f32[64,512]{1,0:T(8,128)}, u32[]{:S(2)}) copy-start(f32[64,512]{1,0:T(8,128)} %get-tuple-element.12) | copy-start | bytes 393220

commit v13 on v12

--- a/solution.py
+++ b/solution.py
@@ -154,21 +154,30 @@
     )(parts, hidden)
 
 
-def rope(values, cos_ref, sin_ref, swap):
+def rope(values, cosine, sine, swap):
     swapped = jnp.dot(values, swap, precision=lax.Precision.HIGHEST, preferred_element_type=jnp.float32)
-    return values * cos_ref[...] + swapped * sin_ref[...]
+    return values * cosine + swapped * sine
 
 
 def query_kernel(
     count, pool_pages, page_size, hidden_ref, attn_gain_ref, w_query_ref, query_gain_ref, w_gate_ref, w_value_ref,
-    w_key_ref, key_gain_ref, cos_ref, sin_ref, table_ref, lengths_ref, order_ref, out_ref, query_ref, gate_ref,
+    w_key_ref, key_gain_ref, frequency_ref, table_ref, lengths_ref, order_ref, out_ref, query_ref, gate_ref,
     value_ref, key_ref, owned_ref, filled_ref, page_query_ref, slot_scratch, send_sems, recv_sems,
 ):
     me, peers = peers_of("req", count)
     barrier = pltpu.get_barrier_semaphore()
     for _, peer in peers:
         pl.semaphore_signal(barrier, inc=1, device_id={"req": peer}, device_id_type=MESH_IDS)
-    head_width = cos_ref.shape[1]
+    head_width = frequency_ref.shape[1]
+    rows = query_ref.shape[0]
+    requests = order_ref.shape[1]
+    request_ids = lax.broadcasted_iota(jnp.int32, (rows, requests), 1)
+    own_rows = me * rows + lax.broadcasted_iota(jnp.int32, (rows, requests), 0)
+    own_requests = jnp.sum(jnp.where(request_ids == own_rows, order_ref[...], 0), axis=1, keepdims=True)
+    position = jnp.sum(jnp.where(request_ids == own_requests, lengths_ref[...], 0), axis=1, keepdims=True)
+    angles = position.astype(jnp.float32) * frequency_ref[...]
+    cos_ref = jnp.cos(angles)
+    sin_ref = jnp.sin(angles)
     lanes_in = lax.broadcasted_iota(jnp.int32, (head_width, head_width), 0)
     lanes_out = lax.broadcasted_iota(jnp.int32, (head_width, head_width), 1)
     swap = jnp.where(
@@ -242,7 +251,7 @@
 
 
 def query_exchange(
-    hidden, attn_gain, w_query, query_gain, w_gate, w_value, w_key, key_gain, cosine, sine, table, lengths, order,
+    hidden, attn_gain, w_query, query_gain, w_gate, w_value, w_key, key_gain, frequency, table, lengths, order,
     pool_pages, page_size, count, ident,
 ):
     rows = hidden.shape[0]
@@ -259,7 +268,7 @@
             jax.ShapeDtypeStruct((pool_pages, page_size), jnp.float32),
             jax.ShapeDtypeStruct((pool_pages, w_query.shape[1]), jnp.bfloat16),
         ),
-        in_specs=[pl.BlockSpec(memory_space=pltpu.VMEM)] * 13,
+        in_specs=[pl.BlockSpec(memory_space=pltpu.VMEM)] * 12,
         out_specs=tuple(pl.BlockSpec(memory_space=pltpu.VMEM) for _ in range(8)),
         scratch_shapes=[
             pltpu.VMEM((pool_pages, requests), jnp.float32),
@@ -267,7 +276,7 @@
             pltpu.SemaphoreType.DMA((count,)),
         ],
         compiler_params=pltpu.CompilerParams(collective_id=ident, has_side_effects=True),
-    )(hidden, attn_gain, w_query, query_gain, w_gate, w_value, w_key, key_gain, cosine, sine, table, lengths, order)
+    )(hidden, attn_gain, w_query, query_gain, w_gate, w_value, w_key, key_gain, frequency, table, lengths, order)
 
 
 def attend_kernel(
@@ -464,17 +473,9 @@
     first_own = req_index * local_rows
 
     with jax.named_scope("rotary_tables"):
-        request_ids = jnp.arange(all_rows, dtype=jnp.int32)
-        own_rows = first_own + jnp.arange(local_rows, dtype=jnp.int32)
-        own_requests = jnp.sum(jnp.where(own_rows[:, None] == request_ids[None, :], deal_order[None, :], 0), axis=1)
-        own_pick = own_requests[:, None] == request_ids[None, :]
-        position = jnp.sum(jnp.where(own_pick, lengths[None, :], 0), axis=1).astype(jnp.float32)
         half = head_width // 2
         lane_ids = jnp.arange(head_width, dtype=jnp.int32) % half
         frequency = ROPE_BASE ** (-(lane_ids.astype(jnp.float32) * (2.0 / head_width)))
-        angles = position[:, None] * frequency[None, :]
-        cosine = jnp.cos(angles)
-        sine = jnp.sin(angles)
 
     outs = query_exchange(
         hidden,
@@ -485,8 +486,7 @@
         w_value,
         w_key,
         key_gain.reshape(1, head_width),
-        cosine,
-        sine,
+        frequency.reshape(1, head_width),
         page_table.T,
         lengths.reshape(1, all_rows),
         deal_order.reshape(1, all_rows),

time: 90.2 us -> 88.2 us (0.978)
  other arithmetic: 5.56 us -> 3.46 us
    reduce_sum x2 -> x0, other arithmetic: 1.88 us -> none  [the longest x1 1.01 us: body(): jnp.sum(jnp.where(own_rows[:, None] == request_ids[None, :], deal_order[N...]
where the time goes in v13:
time: 88.2 us; the launch traced here: 87.9 us
  Pallas kernels  77.1 us (87%)
  matrix products  4.51 us (5%)
  other arithmetic  3.46 us (4%)
  local copies, waits for them, and re-layouts  2.72 us (3%)
    pallas_call x1, Pallas kernels, attend_exchange(): pl.pallas_call(functools.partial(attend_kernel, req_count, head_count, gr...  31.1 us
    pallas_call x1, Pallas kernels, tail_exchange(): pl.pallas_call(functools.partial(tail_kernel, head_count, req_count), out...  26.1 us
    pallas_call x1, Pallas kernels, query_exchange(): pl.pallas_call(functools.partial(query_kernel, count, pool_pages, page_si...  20 us
    dot_general x1, matrix products, body(): jnp.einsum('pkgt,ptkd->pkgd', weights.astype(jnp.bfloat16), value_cache,...  2.31 us

profile of v13, /device:TPU:1, one launch (start us, length us, event | category | flops | bytes accessed | tf_op | source)
XLA Modules:
  0.0 87.9 jit_solution(5995527984371431299)
XLA Ops:
  0.0 0.0 copy-start
  0.0 0.5 fusion.20.frequency_ref
  0.5 20.0 %shard_map.172 = (bf16[32,16,256]{2,1,0:T(8,128)(2,1)}, bf16[16,256]{1,0:T(8,128)(2,1)}, f32[16,256]{1,0:T(8,128)}, bf16[16,128]{1,0:T(8,128)(2,1)}, bf16[16,128...) custom-call(bf16[16,2048]{1,0:T(8,128)(2,1)} %hidden_ref.3, ...), custom_call_target="tpu_custom_call" | custom-call | tf_op jit(solution)/shard_map/pallas_call | solution.py:259
  20.5 0.8 broadcast_compare_fusion.1
  21.3 0.9 %broadcast_compare_fusion = pred[64,512]{1,0:T(8,128)(4,1)S(1)} fusion(f32[64,512]{1,0:T(8,128)} %get-tuple-element.12), kind=kLoop, calls=%fused_computation.13 | loop fusion | flops 32768 | bytes 163840 | tf_op jit(solution)/shard_map/gt | solution.py:499
  22.2 0.8 reshape.146
  23.0 0.0 copy-done
  23.0 1.3 %fusion.22 = (f32[64,2]{1,0:T(8,128)S(1)}, f32[64,2,128]{2,1,0:T(2,128)S(1)}) fusion(bf16[64,2,128]{2,1,0:T(2,128)(2,1)S(1)} %reshape.146, bf16[64,128,1,128]{3,1,2,0:T(8,128)(2,1)S(1)} %copy-done, pred[64,128]{1,0:T(8,128)(4,1)S(1)} %broadcast_compare_fusion.1), kind=kOutput, calls=%fused_computation.26 | convolution fusion | flops 4243328 | bytes 2204160 | tf_op jit(solution)/shard_map/page_attention/pkgd,ptkd->pkgt/dot_general | solution.py:506
  24.2 0.1 copy.25
  24.3 0.1 select_reduce_fusion.2
  24.4 0.1 select_reduce_fusion.1
  24.6 0.1 mul.38
  24.7 0.1 copy.26
  24.8 0.2 fusion.21
  25.0 2.3 %fusion.10 = bf16[64,2,128]{2,1,0:T(2,128)(2,1)S(1)} fusion(bf16[64,128,1,128]{3,1,2,0:T(8,128)(2,1)} %param.23, f32[64,2,128]{2,1,0:T(2,128)S(1)} %get-tuple-element.20, pred[64,128]{1,0:T(8,128)(4,1)S(1)} %broadcast_compare_fusion.1, f32[64,2]{1,0:T(8,128)S(1)} %copy.26), kind=kOutput, calls=%fused_computation.7 | convolution fusion | flops 4259840 | bytes 2204160 | tf_op jit(solution)/shard_map/page_attention/pkgt,ptkd->pkgd/dot_general | solution.py:518
  27.3 0.1 copy.27
  27.4 0.1 select_reduce_fusion
  27.5 0.1 reshape.150
  27.6 0.7 maximum_bitcast_fusion.stats_ref
  28.3 0.0 copy-done.1
  28.3 0.9 %convolution_convert_fusion = bf16[512,256]{1,0:T(8,128)(2,1)} fusion(f32[64,512]{1,0:T(8,128)S(1)} %copy-done.1, bf16[8,8,2,128]{3,2,1,0:T(2,128)(2,1)S(1)} %bitcast.35), kind=kOutput, calls=%fused_computation.4 | convolution fusion | flops 16941056 | bytes 425984 | tf_op jit(solution)/shard_map/page_attention/dot_general | solution.py:525
  29.2 31.1 %shard_map.173.mixed_ref = bf16[16,2048]{1,0:T(8,128)(2,1)} custom-call(bf16[32,16,256]{2,1,0:T(8,128)(2,1)} %bitcast.33, f32[32,4,16]{2,1,0:T(4,128)} %maximum_bitcast_fusion.stats_ref, bf16[16,256]{1,0:T(8,128)(2,1)} %get-tuple-element.15.query_ref, bf16[16,128]{1,0:T(8,128)(2,1)} %get-tuple-element.16.key_ref, ...), custom_call_target="tpu_custom_call" | custom-call | tf_op jit(solution)/shard_map/pallas_call | solution.py:362
  60.3 26.1 %shard_map.174 = bf16[16,2048]{1,0:T(8,128)(2,1)} custom-call(bf16[16,2048]{1,0:T(8,128)(2,1)} %shard_map.173.mixed_ref, f32[1,2048]{1,0:T(1,128)} %bitcast.37, bf16[2048,384]{1,0:T(8,128)(2,1)} %w_gate_ref.3, bf16[2048,384]{1,0:T(8,128)(2,1)} %w_up_ref.1, bf16[384,2048]{1,0:T(8,128)(2,1)} %w_down_ref.1, s32[1,512]{1,0:T(1,128)} %bitcast.39), custom_call_target="tpu_custom_call" | custom-call | tf_op jit(solution)/shard_map/pallas_call | solution.py:424
  86.4 1.5 %copy.36 = bf16[16,2048]{1,0:T(8,128)(2,1)} copy(bf16[16,2048]{1,0:T(8,128)(2,1)} %shard_map.174) | data formatting | bytes 131072
  (4 shorter events, 0.1 us)
Async XLA Ops:
  0.0 23.0 %copy-start = (bf16[64,128,1,128]{3,1,2,0:T(8,128)(2,1)S(1)}, bf16[64,128,1,128]{3,1,2,0:T(8,128)(2,1)}, u32[]{:S(2)}) copy-start(bf16[64,128,1,128]{3,1,2,0:T(8,128)(2,1)} %param.22) | copy-start | bytes 6291460
  24.2 4.1 %copy-start.1 = (f32[64,512]{1,0:T(8,128)S(1)}, f32[64,512]{1,0:T(8,128)}, u32[]{:S(2)}) copy-start(f32[64,512]{1,0:T(8,128)} %get-tuple-element.12) | copy-start | bytes 393220

commit v14 on v13

--- a/solution.py
+++ b/solution.py
@@ -496,7 +496,6 @@
         0,
     )
     _, own_queries, gate_logits, new_values, new_keys, owned_f, live_tokens, page_queries = outs
-    owned = owned_f > 0.5
     page_queries = page_queries.reshape(pool_pages, local_kv, group_size, head_width)
     new_values = new_values.reshape(local_rows, local_kv, head_width)
     new_keys = new_keys.reshape(local_rows, local_kv, head_width)
@@ -506,14 +505,12 @@
             jnp.einsum("pkgd,ptkd->pkgt", page_queries, key_cache, preferred_element_type=jnp.float32)
             * scale_factor
         )
-        live_mask = live_tokens[:, None, None, :] > 0.5
-        scores = jnp.where(live_mask, scores, LOW_SCORE)
+        scores = jnp.where(live_tokens[:, None, None, :] > 0.5, scores, LOW_SCORE)
         page_peaks = jnp.max(scores, axis=-1)
-        owned_b = owned[:, :, None, None]
-        row_peaks = jnp.max(jnp.where(owned_b, page_peaks[:, None], LOW_SCORE), axis=0)
+        row_peaks = jnp.max(jnp.where(owned_f[:, :, None, None] > 0.5, page_peaks[:, None], LOW_SCORE), axis=0)
         row_shift = LOG_TWO * jnp.ceil(row_peaks / LOG_TWO)
-        page_shift = jnp.max(jnp.where(owned_b, row_shift[None], LOW_SCORE), axis=1)
-        weights = jnp.where(live_mask, jnp.exp(scores - page_shift[..., None]), 0.0)
+        page_shift = jnp.max(jnp.where(owned_f[:, :, None, None] > 0.5, row_shift[None], LOW_SCORE), axis=1)
+        weights = live_tokens[:, None, None, :] * jnp.exp(scores - page_shift[..., None])
         page_totals = jnp.sum(weights, axis=-1)
         page_numerators = jnp.einsum(
             "pkgt,ptkd->pkgd",
@@ -521,7 +518,7 @@
             value_cache,
             preferred_element_type=jnp.float32,
         )
-        row_totals = jnp.sum(jnp.where(owned_b, page_totals[:, None], 0.0), axis=0).reshape(all_rows, pairs)
+        row_totals = jnp.sum(owned_f[:, :, None, None] * page_totals[:, None], axis=0).reshape(all_rows, pairs)
         row_numerators = jnp.dot(
             owned_f.T.astype(jnp.bfloat16),
             page_numerators.reshape(pool_pages, head_cols).astype(jnp.bfloat16),

time: 88.2 us -> 88.2 us (level)
  no operation moved by 1% of the time
where the time goes in v14:
time: 88.2 us; the launch traced here: 87.9 us
  Pallas kernels  77.1 us (87%)
  matrix products  4.51 us (5%)
  other arithmetic  3.46 us (4%)
  local copies, waits for them, and re-layouts  2.72 us (3%)
    pallas_call x1, Pallas kernels, attend_exchange(): pl.pallas_call(functools.partial(attend_kernel, req_count, head_count, gr...  31.1 us
    pallas_call x1, Pallas kernels, tail_exchange(): pl.pallas_call(functools.partial(tail_kernel, head_count, req_count), out...  26.1 us
    pallas_call x1, Pallas kernels, query_exchange(): pl.pallas_call(functools.partial(query_kernel, count, pool_pages, page_si...  20 us
    dot_general x1, matrix products, body(): jnp.einsum('pkgt,ptkd->pkgd', weights.astype(jnp.bfloat16), value_cache,...  2.3 us

profile of v14, /device:TPU:1, one launch (start us, length us, event | category | flops | bytes accessed | tf_op | source)
XLA Modules:
  0.0 87.9 jit_solution(3249278213034787803)
XLA Ops:
  0.0 0.0 copy-start
  0.0 0.5 fusion.20.frequency_ref
  0.5 20.0 %shard_map.172 = (bf16[32,16,256]{2,1,0:T(8,128)(2,1)}, bf16[16,256]{1,0:T(8,128)(2,1)}, f32[16,256]{1,0:T(8,128)}, bf16[16,128]{1,0:T(8,128)(2,1)}, bf16[16,128...) custom-call(bf16[16,2048]{1,0:T(8,128)(2,1)} %hidden_ref.3, ...), custom_call_target="tpu_custom_call" | custom-call | tf_op jit(solution)/shard_map/pallas_call | solution.py:259
  20.5 0.0 copy-start.2
  20.5 0.8 reshape.153
  21.3 0.8 broadcast_compare_fusion.1
  22.0 0.9 %broadcast_compare_fusion = pred[64,512]{1,0:T(8,128)(4,1)S(1)} fusion(f32[64,512]{1,0:T(8,128)} %get-tuple-element.12), kind=kLoop, calls=%fused_computation.13 | loop fusion | flops 32768 | bytes 163840 | tf_op jit(solution)/shard_map/page_attention/gt | solution.py:512
  23.0 1.3 %fusion.22 = (f32[64,2]{1,0:T(8,128)S(1)}, f32[64,2,128]{2,1,0:T(2,128)S(1)}) fusion(bf16[64,2,128]{2,1,0:T(2,128)(2,1)S(1)} %reshape.153, bf16[64,128,1,128]{3,1,2,0:T(8,128)(2,1)S(1)} %copy-done, pred[64,128]{1,0:T(8,128)(4,1)S(1)} %broadcast_compare_fusion.1), kind=kOutput, calls=%fused_computation.26 | convolution fusion | flops 4243328 | bytes 2204160 | tf_op jit(solution)/shard_map/page_attention/pkgd,ptkd->pkgt/dot_general | solution.py:505
  24.3 0.1 copy.25
  24.3 0.1 select_reduce_fusion.1
  24.5 0.1 select_reduce_fusion
  24.6 0.1 mul.70
  24.7 0.1 copy.26
  24.8 0.0 copy-done.2
  24.8 0.2 fusion.21
  25.0 2.3 %fusion.10 = bf16[64,2,128]{2,1,0:T(2,128)(2,1)S(1)} fusion(bf16[64,128,1,128]{3,1,2,0:T(8,128)(2,1)} %param.23, f32[64,2,128]{2,1,0:T(2,128)S(1)} %get-tuple-element.20, f32[64,2]{1,0:T(8,128)S(1)} %copy.26, f32[64,128]{1,0:T(8,128)S(1)} %copy-done.2), kind=kOutput, calls=%fused_computation.7 | convolution fusion | flops 4259840 | bytes 2228736 | tf_op jit(solution)/shard_map/page_attention/pkgt,ptkd->pkgd/dot_general | solution.py:515
  27.3 0.1 copy.27
  27.4 0.1 multiply_reduce_fusion
  27.5 0.1 reshape.157
  27.6 0.7 maximum_bitcast_fusion.stats_ref
  28.3 0.9 %convolution_convert_fusion = bf16[512,256]{1,0:T(8,128)(2,1)} fusion(f32[64,512]{1,0:T(8,128)S(1)} %copy-done.1, bf16[8,8,2,128]{3,2,1,0:T(2,128)(2,1)S(1)} %bitcast.35), kind=kOutput, calls=%fused_computation.4 | convolution fusion | flops 16941056 | bytes 425984 | tf_op jit(solution)/shard_map/page_attention/dot_general | solution.py:522
  29.3 31.1 %shard_map.173.mixed_ref = bf16[16,2048]{1,0:T(8,128)(2,1)} custom-call(bf16[32,16,256]{2,1,0:T(8,128)(2,1)} %bitcast.33, f32[32,4,16]{2,1,0:T(4,128)} %maximum_bitcast_fusion.stats_ref, bf16[16,256]{1,0:T(8,128)(2,1)} %get-tuple-element.15.query_ref, bf16[16,128]{1,0:T(8,128)(2,1)} %get-tuple-element.16.key_ref, ...), custom_call_target="tpu_custom_call" | custom-call | tf_op jit(solution)/shard_map/pallas_call | solution.py:362
  60.3 26.1 %shard_map.174 = bf16[16,2048]{1,0:T(8,128)(2,1)} custom-call(bf16[16,2048]{1,0:T(8,128)(2,1)} %shard_map.173.mixed_ref, f32[1,2048]{1,0:T(1,128)} %bitcast.37, bf16[2048,384]{1,0:T(8,128)(2,1)} %w_gate_ref.3, bf16[2048,384]{1,0:T(8,128)(2,1)} %w_up_ref.1, bf16[384,2048]{1,0:T(8,128)(2,1)} %w_down_ref.1, s32[1,512]{1,0:T(1,128)} %bitcast.39), custom_call_target="tpu_custom_call" | custom-call | tf_op jit(solution)/shard_map/pallas_call | solution.py:424
  86.4 1.5 %copy.36 = bf16[16,2048]{1,0:T(8,128)(2,1)} copy(bf16[16,2048]{1,0:T(8,128)(2,1)} %shard_map.174) | data formatting | bytes 131072
  (6 shorter events, 0.1 us)
Async XLA Ops:
  0.0 23.0 %copy-start = (bf16[64,128,1,128]{3,1,2,0:T(8,128)(2,1)S(1)}, bf16[64,128,1,128]{3,1,2,0:T(8,128)(2,1)}, u32[]{:S(2)}) copy-start(bf16[64,128,1,128]{3,1,2,0:T(8,128)(2,1)} %param.22) | copy-start | bytes 6291460
  20.5 4.3 %copy-start.2 = (f32[64,128]{1,0:T(8,128)S(1)}, f32[64,128]{1,0:T(8,128)}, u32[]{:S(2)}) copy-start(f32[64,128]{1,0:T(8,128)} %get-tuple-element.13) | copy-start | bytes 98308
  23.0 4.4 %copy-start.1 = (f32[64,512]{1,0:T(8,128)S(1)}, f32[64,512]{1,0:T(8,128)}, u32[]{:S(2)}) copy-start(f32[64,512]{1,0:T(8,128)} %get-tuple-element.12) | copy-start | bytes 393220

commit v15 on v14

--- a/solution.py
+++ b/solution.py
@@ -243,11 +243,13 @@
     for copy in copies:
         copy.wait()
     rows = query_ref.shape[0]
-    page_query_ref[...] = jnp.dot(
+    page_queries = jnp.dot(
         owned_ref[...].astype(jnp.bfloat16),
         out_ref[...].reshape(count * rows, query_ref.shape[1]),
         preferred_element_type=jnp.float32,
     ).astype(page_query_ref.dtype)
+    for pair in range(page_query_ref.shape[1]):
+        page_query_ref[:, pair, :] = page_queries[:, pair * head_width : (pair + 1) * head_width]
 
 
 def query_exchange(
@@ -266,7 +268,7 @@
             jax.ShapeDtypeStruct((rows, w_key.shape[1]), jnp.bfloat16),
             jax.ShapeDtypeStruct((pool_pages, requests), jnp.float32),
             jax.ShapeDtypeStruct((pool_pages, page_size), jnp.float32),
-            jax.ShapeDtypeStruct((pool_pages, w_query.shape[1]), jnp.bfloat16),
+            jax.ShapeDtypeStruct((pool_pages, w_query.shape[1] // key_gain.shape[1], key_gain.shape[1]), jnp.bfloat16),
         ),
         in_specs=[pl.BlockSpec(memory_space=pltpu.VMEM)] * 12,
         out_specs=tuple(pl.BlockSpec(memory_space=pltpu.VMEM) for _ in range(8)),

time: 88.2 us -> 88.3 us (level)
  no operation moved by 1% of the time
where the time goes in v15:
time: 88.3 us; the launch traced here: 88 us
  Pallas kernels  77.1 us (87%)
  matrix products  5.3 us (6%)
  other arithmetic  3.53 us (4%)
  local copies, waits for them, and re-layouts  1.95 us (2%)
    pallas_call x1, Pallas kernels, attend_exchange(): pl.pallas_call(functools.partial(attend_kernel, req_count, head_count, gr...  31.1 us
    pallas_call x1, Pallas kernels, tail_exchange(): pl.pallas_call(functools.partial(tail_kernel, head_count, req_count), out...  26.1 us
    pallas_call x1, Pallas kernels, query_exchange(): pl.pallas_call(functools.partial(query_kernel, count, pool_pages, page_si...  20 us
    dot_general x1, matrix products, body(): jnp.einsum('pkgt,ptkd->pkgd', weights.astype(jnp.bfloat16), value_cache,...  2.3 us
    dot_general x1, matrix products, body(): jnp.einsum('pkgd,ptkd->pkgt', page_queries, key_cache, preferred_element_...  2.05 us

profile of v15, /device:TPU:1, one launch (start us, length us, event | category | flops | bytes accessed | tf_op | source)
XLA Modules:
  0.0 88.0 jit_solution(15608919326233785310)
XLA Ops:
  0.0 0.0 copy-start
  0.0 0.5 fusion.20.frequency_ref
  0.5 20.0 %shard_map.172 = (bf16[32,16,256]{2,1,0:T(8,128)(2,1)}, bf16[16,256]{1,0:T(8,128)(2,1)}, f32[16,256]{1,0:T(8,128)}, bf16[16,128]{1,0:T(8,128)(2,1)}, bf16[16,128...) custom-call(bf16[16,2048]{1,0:T(8,128)(2,1)} %hidden_ref.3, ...), custom_call_target="tpu_custom_call" | custom-call | tf_op jit(solution)/shard_map/pallas_call | solution.py:261
  20.6 0.0 copy-start.2
  20.6 0.8 broadcast_compare_fusion.1
  21.4 0.9 %broadcast_compare_fusion = pred[64,512]{1,0:T(8,128)(4,1)S(1)} fusion(f32[64,512]{1,0:T(8,128)} %get-tuple-element.12), kind=kLoop, calls=%fused_computation.13 | loop fusion | flops 32768 | bytes 163840 | tf_op jit(solution)/shard_map/page_attention/gt | solution.py:514
  22.3 0.0 copy-done
  22.3 2.1 %fusion.22 = (f32[64,2]{1,0:T(8,128)S(1)}, f32[64,2,128]{2,1,0:T(2,128)S(1)}) fusion(bf16[64,2,128]{2,1,0:T(2,128)(2,1)} %get-tuple-element.14, bf16[64,128,1,128]{3,1,2,0:T(8,128)(2,1)S(1)} %copy-done, pred[64,128]{1,0:T(8,128)(4,1)S(1)} %broadcast_compare_fusion.1), kind=kOutput, calls=%fused_computation.26 | convolution fusion | flops 4243328 | bytes 2204160 | tf_op jit(solution)/shard_map/page_attention/pkgd,ptkd->pkgt/dot_general | solution.py:507
  24.4 0.1 copy.25
  24.5 0.1 select_reduce_fusion.1
  24.6 0.1 select_reduce_fusion
  24.7 0.1 mul.70
  24.8 0.1 copy.26
  24.9 0.2 fusion.21
  25.2 2.3 %fusion.10 = bf16[64,2,128]{2,1,0:T(2,128)(2,1)S(1)} fusion(bf16[64,128,1,128]{3,1,2,0:T(8,128)(2,1)} %param.23, f32[64,2,128]{2,1,0:T(2,128)S(1)} %get-tuple-element.20, f32[64,2]{1,0:T(8,128)S(1)} %copy.26, f32[64,128]{1,0:T(8,128)S(1)} %copy-done.2), kind=kOutput, calls=%fused_computation.7 | convolution fusion | flops 4259840 | bytes 2228736 | tf_op jit(solution)/shard_map/page_attention/pkgt,ptkd->pkgd/dot_general | solution.py:517
  27.5 0.1 copy.27
  27.6 0.0 copy-done.1
  27.6 0.1 multiply_reduce_fusion
  27.7 0.1 reshape.154
  27.8 0.7 maximum_bitcast_fusion.stats_ref
  28.5 0.9 %convolution_convert_fusion = bf16[512,256]{1,0:T(8,128)(2,1)} fusion(f32[64,512]{1,0:T(8,128)S(1)} %copy-done.1, bf16[8,8,2,128]{3,2,1,0:T(2,128)(2,1)S(1)} %bitcast.35), kind=kOutput, calls=%fused_computation.4 | convolution fusion | flops 16941056 | bytes 425984 | tf_op jit(solution)/shard_map/page_attention/dot_general | solution.py:524
  29.4 31.1 %shard_map.173.mixed_ref = bf16[16,2048]{1,0:T(8,128)(2,1)} custom-call(bf16[32,16,256]{2,1,0:T(8,128)(2,1)} %bitcast.33, f32[32,4,16]{2,1,0:T(4,128)} %maximum_bitcast_fusion.stats_ref, bf16[16,256]{1,0:T(8,128)(2,1)} %get-tuple-element.15.query_ref, bf16[16,128]{1,0:T(8,128)(2,1)} %get-tuple-element.16.key_ref, ...), custom_call_target="tpu_custom_call" | custom-call | tf_op jit(solution)/shard_map/pallas_call | solution.py:364
  60.5 26.1 %shard_map.174 = bf16[16,2048]{1,0:T(8,128)(2,1)} custom-call(bf16[16,2048]{1,0:T(8,128)(2,1)} %shard_map.173.mixed_ref, f32[1,2048]{1,0:T(1,128)} %bitcast.37, bf16[2048,384]{1,0:T(8,128)(2,1)} %w_gate_ref.3, bf16[2048,384]{1,0:T(8,128)(2,1)} %w_up_ref.1, bf16[384,2048]{1,0:T(8,128)(2,1)} %w_down_ref.1, s32[1,512]{1,0:T(1,128)} %bitcast.39), custom_call_target="tpu_custom_call" | custom-call | tf_op jit(solution)/shard_map/pallas_call | solution.py:426
  86.5 1.5 %copy.36 = bf16[16,2048]{1,0:T(8,128)(2,1)} copy(bf16[16,2048]{1,0:T(8,128)(2,1)} %shard_map.174) | data formatting | bytes 131072
  (5 shorter events, 0.1 us)
Async XLA Ops:
  0.0 22.3 %copy-start = (bf16[64,128,1,128]{3,1,2,0:T(8,128)(2,1)S(1)}, bf16[64,128,1,128]{3,1,2,0:T(8,128)(2,1)}, u32[]{:S(2)}) copy-start(bf16[64,128,1,128]{3,1,2,0:T(8,128)(2,1)} %param.22) | copy-start | bytes 6291460
  20.6 4.4 %copy-start.2 = (f32[64,128]{1,0:T(8,128)S(1)}, f32[64,128]{1,0:T(8,128)}, u32[]{:S(2)}) copy-start(f32[64,128]{1,0:T(8,128)} %get-tuple-element.13) | copy-start | bytes 98308
  22.3 5.2 %copy-start.1 = (f32[64,512]{1,0:T(8,128)S(1)}, f32[64,512]{1,0:T(8,128)}, u32[]{:S(2)}) copy-start(f32[64,512]{1,0:T(8,128)} %get-tuple-element.12) | copy-start | bytes 393220

commit v16 on v14

--- a/solution.py
+++ b/solution.py
@@ -290,7 +290,19 @@
     pairs = stats_ref.shape[1] // 2
     head_width = query_ref.shape[1] // pairs
     mine = pl.ds(pl.multiple_of(head_me * cols, cols), cols)
-    greet([("req", peer) for _, peer in req_peers] + [("head", peer) for _, peer in head_peers])
+    barrier = pltpu.get_barrier_semaphore()
+    everyone = [("req", peer) for _, peer in req_peers] + [("head", peer) for _, peer in head_peers]
+    for axis, peer in everyone:
+        pl.semaphore_signal(barrier, inc=1, device_id={axis: peer}, device_id_type=MESH_IDS)
+    self_scores = []
+    for pair in range(pairs):
+        kv = pair // group_size
+        query = query_ref[:, pair * head_width : (pair + 1) * head_width].astype(jnp.float32)
+        key = key_ref[:, kv * head_width : (kv + 1) * head_width].astype(jnp.float32)
+        self_scores.append(jnp.sum(query * key, axis=1, keepdims=True) * scale_factor)
+    gate = gate_ref[...]
+    gate_scale = 1.0 / (1.0 + jnp.exp(-gate))
+    pl.semaphore_wait(barrier, len(everyone))
     got_num[req_me] = num_ref[req_me]
     got_stats[req_me] = stats_ref[req_me]
     copies = []
@@ -327,8 +339,7 @@
             precision=lax.Precision.HIGHEST,
             preferred_element_type=jnp.float32,
         )
-        query = query_ref[:, lanes].astype(jnp.float32)
-        self_score = jnp.sum(query * key_ref[:, kv_lanes].astype(jnp.float32), axis=1, keepdims=True) * scale_factor
+        self_score = self_scores[pair]
         self_shift = LOG_TWO * jnp.ceil(self_score / LOG_TWO)
         shift = jnp.maximum(jnp.max(shifts, axis=1, keepdims=True), self_shift)
         factor = jnp.exp(shifts - shift)
@@ -339,8 +350,7 @@
             acc = acc + factor[:, source : source + 1] * got_num[source, :, lanes].astype(jnp.float32)
         heads.append(acc / total)
     heads_out = jnp.concatenate(heads, axis=1)
-    gate = gate_ref[...]
-    attended = (heads_out * (1.0 / (1.0 + jnp.exp(-gate)))).astype(jnp.bfloat16)
+    attended = (heads_out * gate_scale).astype(jnp.bfloat16)
     projected[...] = jnp.dot(attended, w_out_ref[...], preferred_element_type=jnp.float32)
     summed[head_me] = projected[:, mine]
     send_all(

time: 88.2 us -> 88.2 us (level)
  no operation moved by 1% of the time
where the time goes in v16:
time: 88.2 us; the launch traced here: 87.9 us
  Pallas kernels  77.1 us (87%)
  matrix products  4.51 us (5%)
  other arithmetic  3.46 us (4%)
  local copies, waits for them, and re-layouts  2.72 us (3%)
    pallas_call x1, Pallas kernels, attend_exchange(): pl.pallas_call(functools.partial(attend_kernel, req_count, head_count, gr...  31.1 us
    pallas_call x1, Pallas kernels, tail_exchange(): pl.pallas_call(functools.partial(tail_kernel, head_count, req_count), out...  26.1 us
    pallas_call x1, Pallas kernels, query_exchange(): pl.pallas_call(functools.partial(query_kernel, count, pool_pages, page_si...  20 us
    dot_general x1, matrix products, body(): jnp.einsum('pkgt,ptkd->pkgd', weights.astype(jnp.bfloat16), value_cache,...  2.3 us

profile of v16, /device:TPU:1, one launch (start us, length us, event | category | flops | bytes accessed | tf_op | source)
XLA Modules:
  0.0 87.9 jit_solution(15193835835601173680)
XLA Ops:
  0.0 0.0 copy-start
  0.0 0.5 fusion.20.frequency_ref
  0.5 20.0 %shard_map.172 = (bf16[32,16,256]{2,1,0:T(8,128)(2,1)}, bf16[16,256]{1,0:T(8,128)(2,1)}, f32[16,256]{1,0:T(8,128)}, bf16[16,128]{1,0:T(8,128)(2,1)}, bf16[16,128...) custom-call(bf16[16,2048]{1,0:T(8,128)(2,1)} %hidden_ref.3, ...), custom_call_target="tpu_custom_call" | custom-call | tf_op jit(solution)/shard_map/pallas_call | solution.py:259
  20.5 0.0 copy-start.2
  20.5 0.8 reshape.153
  21.3 0.8 broadcast_compare_fusion.1
  22.0 0.9 %broadcast_compare_fusion = pred[64,512]{1,0:T(8,128)(4,1)S(1)} fusion(f32[64,512]{1,0:T(8,128)} %get-tuple-element.12), kind=kLoop, calls=%fused_computation.13 | loop fusion | flops 32768 | bytes 163840 | tf_op jit(solution)/shard_map/page_attention/gt | solution.py:522
  23.0 0.0 copy-done
  23.0 1.3 %fusion.22 = (f32[64,2]{1,0:T(8,128)S(1)}, f32[64,2,128]{2,1,0:T(2,128)S(1)}) fusion(bf16[64,2,128]{2,1,0:T(2,128)(2,1)S(1)} %reshape.153, bf16[64,128,1,128]{3,1,2,0:T(8,128)(2,1)S(1)} %copy-done, pred[64,128]{1,0:T(8,128)(4,1)S(1)} %broadcast_compare_fusion.1), kind=kOutput, calls=%fused_computation.26 | convolution fusion | flops 4243328 | bytes 2204160 | tf_op jit(solution)/shard_map/page_attention/pkgd,ptkd->pkgt/dot_general | solution.py:515
  24.3 0.1 copy.25
  24.3 0.1 select_reduce_fusion.1
  24.5 0.1 select_reduce_fusion
  24.6 0.1 mul.70
  24.7 0.1 copy.26
  24.8 0.2 fusion.21
  25.0 2.3 %fusion.10 = bf16[64,2,128]{2,1,0:T(2,128)(2,1)S(1)} fusion(bf16[64,128,1,128]{3,1,2,0:T(8,128)(2,1)} %param.23, f32[64,2,128]{2,1,0:T(2,128)S(1)} %get-tuple-element.20, f32[64,2]{1,0:T(8,128)S(1)} %copy.26, f32[64,128]{1,0:T(8,128)S(1)} %copy-done.2), kind=kOutput, calls=%fused_computation.7 | convolution fusion | flops 4259840 | bytes 2228736 | tf_op jit(solution)/shard_map/page_attention/pkgt,ptkd->pkgd/dot_general | solution.py:525
  27.3 0.1 copy.27
  27.4 0.1 multiply_reduce_fusion
  27.5 0.1 reshape.157
  27.6 0.7 maximum_bitcast_fusion.stats_ref
  28.3 0.9 %convolution_convert_fusion = bf16[512,256]{1,0:T(8,128)(2,1)} fusion(f32[64,512]{1,0:T(8,128)S(1)} %copy-done.1, bf16[8,8,2,128]{3,2,1,0:T(2,128)(2,1)S(1)} %bitcast.35), kind=kOutput, calls=%fused_computation.4 | convolution fusion | flops 16941056 | bytes 425984 | tf_op jit(solution)/shard_map/page_attention/dot_general | solution.py:532
  29.3 31.1 %shard_map.173.mixed_ref = bf16[16,2048]{1,0:T(8,128)(2,1)} custom-call(bf16[32,16,256]{2,1,0:T(8,128)(2,1)} %bitcast.33, f32[32,4,16]{2,1,0:T(4,128)} %maximum_bitcast_fusion.stats_ref, bf16[16,256]{1,0:T(8,128)(2,1)} %get-tuple-element.15.query_ref, bf16[16,128]{1,0:T(8,128)(2,1)} %get-tuple-element.16.key_ref, ...), custom_call_target="tpu_custom_call" | custom-call | tf_op jit(solution)/shard_map/pallas_call | solution.py:372
  60.3 26.1 %shard_map.174 = bf16[16,2048]{1,0:T(8,128)(2,1)} custom-call(bf16[16,2048]{1,0:T(8,128)(2,1)} %shard_map.173.mixed_ref, f32[1,2048]{1,0:T(1,128)} %bitcast.37, bf16[2048,384]{1,0:T(8,128)(2,1)} %w_gate_ref.3, bf16[2048,384]{1,0:T(8,128)(2,1)} %w_up_ref.1, bf16[384,2048]{1,0:T(8,128)(2,1)} %w_down_ref.1, s32[1,512]{1,0:T(1,128)} %bitcast.39), custom_call_target="tpu_custom_call" | custom-call | tf_op jit(solution)/shard_map/pallas_call | solution.py:434
  86.4 1.5 %copy.36 = bf16[16,2048]{1,0:T(8,128)(2,1)} copy(bf16[16,2048]{1,0:T(8,128)(2,1)} %shard_map.174) | data formatting | bytes 131072
  (6 shorter events, 0.1 us)
Async XLA Ops:
  0.0 23.0 %copy-start = (bf16[64,128,1,128]{3,1,2,0:T(8,128)(2,1)S(1)}, bf16[64,128,1,128]{3,1,2,0:T(8,128)(2,1)}, u32[]{:S(2)}) copy-start(bf16[64,128,1,128]{3,1,2,0:T(8,128)(2,1)} %param.22) | copy-start | bytes 6291460
  20.5 4.3 %copy-start.2 = (f32[64,128]{1,0:T(8,128)S(1)}, f32[64,128]{1,0:T(8,128)}, u32[]{:S(2)}) copy-start(f32[64,128]{1,0:T(8,128)} %get-tuple-element.13) | copy-start | bytes 98308
  23.0 4.4 %copy-start.1 = (f32[64,512]{1,0:T(8,128)S(1)}, f32[64,512]{1,0:T(8,128)}, u32[]{:S(2)}) copy-start(f32[64,512]{1,0:T(8,128)} %get-tuple-element.12) | copy-start | bytes 393220

commit v17 on v14

--- a/solution.py
+++ b/solution.py
@@ -395,8 +395,10 @@
     up_part = jnp.dot(normed, w_up_ref[...], preferred_element_type=jnp.float32)
     inner_act = (gate_part / (1.0 + jnp.exp(-gate_part)) * up_part).astype(jnp.bfloat16)
     parts_ref[...] = jnp.dot(inner_act, w_down_ref[...], preferred_element_type=jnp.float32)
+    summed[head_me] = parts_ref[:, mine]
+    wanted = req_me * rows + lax.broadcasted_iota(jnp.int32, (rows, req_count * rows), 0)
+    picker = (order_ref[...] == wanted).astype(jnp.bfloat16)
     pl.semaphore_wait(barrier, len(everyone))
-    summed[head_me] = parts_ref[:, mine]
     send_all(
         "head",
         head_peers,
@@ -410,8 +412,6 @@
         results.dtype
     )
     send_all("req", req_peers, lambda peer: results.at[req_me], results.at[req_me], send_sems, recv_sems, 1)
-    wanted = req_me * rows + lax.broadcasted_iota(jnp.int32, (rows, req_count * rows), 0)
-    picker = (order_ref[...] == wanted).astype(jnp.bfloat16)
     out_ref[:, mine] = jnp.dot(
         picker, results[...].reshape(req_count * rows, cols), preferred_element_type=jnp.float32
     ).astype(out_ref.dtype)

time: 88.2 us -> 88.2 us (level)
  no operation moved by 1% of the time
where the time goes in v17:
time: 88.2 us; the launch traced here: 87.9 us
  Pallas kernels  77.1 us (87%)
  matrix products  4.51 us (5%)
  other arithmetic  3.46 us (4%)
  local copies, waits for them, and re-layouts  2.72 us (3%)
    pallas_call x1, Pallas kernels, attend_exchange(): pl.pallas_call(functools.partial(attend_kernel, req_count, head_count, gr...  31.1 us
    pallas_call x1, Pallas kernels, tail_exchange(): pl.pallas_call(functools.partial(tail_kernel, head_count, req_count), out...  26.1 us
    pallas_call x1, Pallas kernels, query_exchange(): pl.pallas_call(functools.partial(query_kernel, count, pool_pages, page_si...  20 us
    dot_general x1, matrix products, body(): jnp.einsum('pkgt,ptkd->pkgd', weights.astype(jnp.bfloat16), value_cache,...  2.3 us

profile of v17, /device:TPU:1, one launch (start us, length us, event | category | flops | bytes accessed | tf_op | source)
XLA Modules:
  0.0 87.9 jit_solution(6534727026363074667)
XLA Ops:
  0.0 0.0 copy-start
  0.0 0.5 fusion.20.frequency_ref
  0.5 20.0 %shard_map.172 = (bf16[32,16,256]{2,1,0:T(8,128)(2,1)}, bf16[16,256]{1,0:T(8,128)(2,1)}, f32[16,256]{1,0:T(8,128)}, bf16[16,128]{1,0:T(8,128)(2,1)}, bf16[16,128...) custom-call(bf16[16,2048]{1,0:T(8,128)(2,1)} %hidden_ref.3, ...), custom_call_target="tpu_custom_call" | custom-call | tf_op jit(solution)/shard_map/pallas_call | solution.py:259
  20.5 0.0 copy-start.2
  20.5 0.8 reshape.153
  21.3 0.8 broadcast_compare_fusion.1
  22.0 0.9 %broadcast_compare_fusion = pred[64,512]{1,0:T(8,128)(4,1)S(1)} fusion(f32[64,512]{1,0:T(8,128)} %get-tuple-element.12), kind=kLoop, calls=%fused_computation.13 | loop fusion | flops 32768 | bytes 163840 | tf_op jit(solution)/shard_map/page_attention/gt | solution.py:512
  23.0 1.3 %fusion.22 = (f32[64,2]{1,0:T(8,128)S(1)}, f32[64,2,128]{2,1,0:T(2,128)S(1)}) fusion(bf16[64,2,128]{2,1,0:T(2,128)(2,1)S(1)} %reshape.153, bf16[64,128,1,128]{3,1,2,0:T(8,128)(2,1)S(1)} %copy-done, pred[64,128]{1,0:T(8,128)(4,1)S(1)} %broadcast_compare_fusion.1), kind=kOutput, calls=%fused_computation.26 | convolution fusion | flops 4243328 | bytes 2204160 | tf_op jit(solution)/shard_map/page_attention/pkgd,ptkd->pkgt/dot_general | solution.py:505
  24.3 0.1 copy.25
  24.3 0.1 select_reduce_fusion.1
  24.5 0.1 select_reduce_fusion
  24.6 0.1 mul.70
  24.7 0.1 copy.26
  24.8 0.0 copy-done.2
  24.8 0.2 fusion.21
  25.0 2.3 %fusion.10 = bf16[64,2,128]{2,1,0:T(2,128)(2,1)S(1)} fusion(bf16[64,128,1,128]{3,1,2,0:T(8,128)(2,1)} %param.23, f32[64,2,128]{2,1,0:T(2,128)S(1)} %get-tuple-element.20, f32[64,2]{1,0:T(8,128)S(1)} %copy.26, f32[64,128]{1,0:T(8,128)S(1)} %copy-done.2), kind=kOutput, calls=%fused_computation.7 | convolution fusion | flops 4259840 | bytes 2228736 | tf_op jit(solution)/shard_map/page_attention/pkgt,ptkd->pkgd/dot_general | solution.py:515
  27.3 0.1 copy.27
  27.4 0.1 multiply_reduce_fusion
  27.5 0.1 reshape.157
  27.6 0.7 maximum_bitcast_fusion.stats_ref
  28.3 0.9 %convolution_convert_fusion = bf16[512,256]{1,0:T(8,128)(2,1)} fusion(f32[64,512]{1,0:T(8,128)S(1)} %copy-done.1, bf16[8,8,2,128]{3,2,1,0:T(2,128)(2,1)S(1)} %bitcast.35), kind=kOutput, calls=%fused_computation.4 | convolution fusion | flops 16941056 | bytes 425984 | tf_op jit(solution)/shard_map/page_attention/dot_general | solution.py:522
  29.3 31.1 %shard_map.173.mixed_ref = bf16[16,2048]{1,0:T(8,128)(2,1)} custom-call(bf16[32,16,256]{2,1,0:T(8,128)(2,1)} %bitcast.33, f32[32,4,16]{2,1,0:T(4,128)} %maximum_bitcast_fusion.stats_ref, bf16[16,256]{1,0:T(8,128)(2,1)} %get-tuple-element.15.query_ref, bf16[16,128]{1,0:T(8,128)(2,1)} %get-tuple-element.16.key_ref, ...), custom_call_target="tpu_custom_call" | custom-call | tf_op jit(solution)/shard_map/pallas_call | solution.py:362
  60.3 26.1 %shard_map.174 = bf16[16,2048]{1,0:T(8,128)(2,1)} custom-call(bf16[16,2048]{1,0:T(8,128)(2,1)} %shard_map.173.mixed_ref, f32[1,2048]{1,0:T(1,128)} %bitcast.37, bf16[2048,384]{1,0:T(8,128)(2,1)} %w_gate_ref.3, bf16[2048,384]{1,0:T(8,128)(2,1)} %w_up_ref.1, bf16[384,2048]{1,0:T(8,128)(2,1)} %w_down_ref.1, s32[1,512]{1,0:T(1,128)} %bitcast.39), custom_call_target="tpu_custom_call" | custom-call | tf_op jit(solution)/shard_map/pallas_call | solution.py:424
  86.4 1.5 %copy.36 = bf16[16,2048]{1,0:T(8,128)(2,1)} copy(bf16[16,2048]{1,0:T(8,128)(2,1)} %shard_map.174) | data formatting | bytes 131072
  (6 shorter events, 0.1 us)
Async XLA Ops:
  0.0 23.0 %copy-start = (bf16[64,128,1,128]{3,1,2,0:T(8,128)(2,1)S(1)}, bf16[64,128,1,128]{3,1,2,0:T(8,128)(2,1)}, u32[]{:S(2)}) copy-start(bf16[64,128,1,128]{3,1,2,0:T(8,128)(2,1)} %param.22) | copy-start | bytes 6291460
  20.5 4.3 %copy-start.2 = (f32[64,128]{1,0:T(8,128)S(1)}, f32[64,128]{1,0:T(8,128)}, u32[]{:S(2)}) copy-start(f32[64,128]{1,0:T(8,128)} %get-tuple-element.13) | copy-start | bytes 98308
  23.0 4.4 %copy-start.1 = (f32[64,512]{1,0:T(8,128)S(1)}, f32[64,512]{1,0:T(8,128)}, u32[]{:S(2)}) copy-start(f32[64,512]{1,0:T(8,128)} %get-tuple-element.12) | copy-start | bytes 393220
